TPU v7x, 128 devices: a whole 4x4x4 slice. The times are simulated.
128 devices in a mesh: sx: 8 (over x, z_hi), sy: 16 (over z_lo, y, core).
Axes of the slice: x: 4, y: 4, z: 4 (z_hi: 2, z_lo: 2; z = z_hi * 2 + z_lo), core: 2. Of those that a mesh axis runs over, the one named last changes fastest.
Arguments:
- scalar_field: float32 [256, 512, 512], P('sx', 'sy'), may hold values from -4 to 7
- diffusivity: float32 [256, 512, 512], P('sx', 'sy'), may hold values from 0.03 to 0.11
- reaction_rate: float32 [256, 512, 512], P('sx', 'sy'), may hold values from 0.05 to 0.5
- shear_offsets: int32 [4, 512], replicated, may hold values from 0 to 31
- depth_order: int32 [4, 512], replicated, may hold values from 0 to 1
- tf_centres: float32 [8], replicated, may hold values from -2 to 2
- tf_colour: float32 [3, 8], replicated, may hold values from 0.5 to 2
- tf_opacity: float32 [8], replicated, may hold values from 0.0009765625 to 0.009765625
Outputs:
- field_out: float32 [256, 512, 512], P('sx', 'sy')
- image: float32 [4, 3, 256, 512], P(None, None, ('sx', 'sy'))
- transmittance: float32 [4, 256, 512], P(None, ('sx', 'sy'))
All inputs are finite; a program needn't handle non-finite values.
Results may differ from a plain program's by a relative error of at most 0.0002.
Values sent between devices are 32-bit elements; how exact they have to be, the bound alone decides.
No kernel may reach another device: no remote copies, remote signals or barrier semaphores. Data moves between devices by JAX's collectives and lax.ppermute only.
A program may use at most 128 MiB of HBM per device.

v0:
```python
import jax
import jax.numpy as jnp
from jax import lax
from jax.sharding import PartitionSpec as P

STEPS = 4
VIEWS = 4
MAXSHIFT = 8


diff_gain = 0.4
bump_sharpness = 2.0


def with_halo(value, sides, width):
    for axis, dim in sides:
        size, length = (lax.axis_size(axis), value.shape[dim])
        up = [(i, (i + 1) % size) for i in range(size - 1)]
        down = [(j, i) for i, j in up]
        last = lax.slice_in_dim(value, length - width, length, axis=dim)
        leading = lax.slice_in_dim(value, 0, width, axis=dim)
        before = lax.ppermute(last, axis, up)
        after = lax.ppermute(leading, axis, down)
        value = jnp.concatenate([before, value, after], axis=dim)
    return value


def prefix(part, axis, combine, identity, reverse):
    count = lax.axis_size(axis)
    place = lax.axis_index(axis)
    ahead = count - 1 - place if reverse else place
    gathered = lax.all_gather(part, axis)
    state = jnp.zeros_like(part) + jnp.asarray(identity, part.dtype)

    def one(turn, state):
        source = count - 1 - turn if reverse else turn
        return combine(state, lax.dynamic_index_in_dim(gathered, source, 0, False))

    return lax.fori_loop(0, ahead, one, state)


def neighbour_flux(field_pad, diff_pad):
    centre_cut = (slice(1, -1), slice(1, -1), slice(1, -1))
    neighbours = [
        (slice(2, None), slice(1, -1), slice(1, -1)),
        (slice(None, -2), slice(1, -1), slice(1, -1)),
        (slice(1, -1), slice(2, None), slice(1, -1)),
        (slice(1, -1), slice(None, -2), slice(1, -1)),
        (slice(1, -1), slice(1, -1), slice(2, None)),
        (slice(1, -1), slice(1, -1), slice(None, -2)),
    ]
    centre_field = field_pad[centre_cut]
    centre_diff = diff_pad[centre_cut]
    change = jnp.zeros_like(centre_field)
    for cut in neighbours:
        change = change + 0.5 * (centre_diff + diff_pad[cut]) * (field_pad[cut] - centre_field)
    return change


def pad_depth(values):
    return jnp.pad(values, ((0, 0), (0, 0), (1, 1)))


def shear_view(field_block, offsets):
    z_cells = field_block.shape[2]
    whole_cells = offsets // 4
    fraction = (offsets % 4).astype(jnp.float32) * 0.25
    padded = jnp.pad(field_block, ((0, 0), (0, 0), (0, MAXSHIFT + 1)))
    window = jax.vmap(
        lambda plane, start: lax.dynamic_slice_in_dim(plane, start, z_cells + 1, 1),
        in_axes=(1, 0),
        out_axes=1,
    )(padded, whole_cells)
    fraction = fraction[None, :, None]
    return (1.0 - fraction) * window[:, :, :z_cells] + fraction * window[:, :, 1:]


def transfer(sheared, tf_centres, tf_colour, tf_opacity):
    optical = jnp.zeros_like(sheared)
    colours = [jnp.zeros_like(sheared) for channel in range(3)]
    for bump_index in range(tf_centres.shape[0]):
        bump_value = jnp.exp(-jnp.square(bump_sharpness * (sheared - tf_centres[bump_index])))
        optical = optical + tf_opacity[bump_index] * bump_value
        colours = [
            colours[channel] + tf_colour[channel, bump_index] * bump_value for channel in range(3)
        ]
    return (optical, colours)


def render_views(field_block, offsets, depth_order, tf_centres, tf_colour, tf_opacity):
    depth_rows = field_block.shape[1]
    rows_iota = lax.broadcasted_iota(jnp.int32, (depth_rows, depth_rows), 0)
    cols_iota = lax.broadcasted_iota(jnp.int32, (depth_rows, depth_rows), 1)
    lower_tri = (cols_iota < rows_iota).astype(jnp.float32)
    colour_views = []
    tau_views = []
    for viewer in range(VIEWS):
        sheared = shear_view(field_block, offsets[viewer])
        optical, colours = transfer(sheared, tf_centres, tf_colour, tf_opacity)
        front_part = jnp.einsum("ij,xjz->xiz", lower_tri, optical, precision=lax.Precision.HIGHEST)
        slab_total = jnp.sum(optical, axis=1)
        back_part = slab_total[:, None, :] - front_part - optical
        rising = (depth_order[viewer] == 0)[None, None, :]
        before = jnp.where(rising, front_part, back_part)
        weight = (1.0 - jnp.exp(-optical)) * jnp.exp(-before)
        colour_views.append(jnp.stack([jnp.sum(channel * weight, axis=1) for channel in colours]))
        tau_views.append(slab_total)
    return (jnp.stack(colour_views), jnp.stack(tau_views))


def add_terms(earlier, later):
    return earlier + later


def attenuate(colour_sum, slab_tau, front_tau, back_tau, depth_order):
    before = jnp.where((depth_order == 0)[:, None, :], front_tau, back_tau)
    lit = colour_sum * jnp.exp(-before)[:, None]
    return jnp.concatenate([lit, slab_tau[:, None]], axis=1)


def per_device(
    scalar_field,
    diffusivity,
    reaction_rate,
    shear_offsets,
    depth_order,
    tf_centres,
    tf_colour,
    tf_opacity,
):
    field_now = scalar_field
    for iteration in range(STEPS):
        diff_now = diffusivity * (1.0 + diff_gain * jnp.tanh(field_now))
        both_rims = with_halo(jnp.stack([field_now, diff_now]), (("sx", 1), ("sy", 2)), 1)
        field_pad = pad_depth(both_rims[0])
        diff_pad = pad_depth(both_rims[1])
        field_now = (
            field_now + neighbour_flux(field_pad, diff_pad) + reaction_rate * jnp.tanh(field_now)
        )
    brick = lax.all_to_all(
        lax.all_to_all(field_now, "sy", split_axis=0, concat_axis=1, tiled=True),
        "sx",
        split_axis=1,
        concat_axis=0,
        tiled=True,
    )
    depth_rows = brick.shape[1]
    plane_rows = lax.dynamic_slice_in_dim(
        shear_offsets, lax.axis_index("sx") * depth_rows, depth_rows, 1
    )
    colour_sum, slab_tau = render_views(
        brick, plane_rows, depth_order, tf_centres, tf_colour, tf_opacity
    )
    front_tau = prefix(slab_tau, "sx", add_terms, jnp.zeros_like(slab_tau), False)
    back_tau = prefix(slab_tau, "sx", add_terms, jnp.zeros_like(slab_tau), True)
    partial_image = attenuate(colour_sum, slab_tau, front_tau, back_tau, depth_order)
    shares = lax.psum_scatter(partial_image, "sx", scatter_dimension=2, tiled=True)
    image = shares[:, :3]
    transmittance = jnp.exp(-shares[:, 3])
    return (field_now, image, transmittance)


def solution(mesh):
    in_specs = (
        P("sx", "sy", None),
        P("sx", "sy", None),
        P("sx", "sy", None),
        P(),
        P(),
        P(),
        P(),
        P(),
    )
    out_specs = (
        P("sx", "sy", None),
        P(None, None, ("sx", "sy"), None),
        P(None, ("sx", "sy"), None),
    )
    return jax.shard_map(
        per_device, mesh=mesh, in_specs=in_specs, out_specs=out_specs, check_vma=False
    )
```

profile of v0, /device:TPU:0, one launch (start us, length us, event | category | flops | bytes accessed | tf_op | source)
XLA Modules:
  0.0 764.0 jit_solution(12752237303191843035)
XLA Ops:
  143.4 41.7 %all_to_all.36 = f32[32,32,512]{2,1,0:T(8,128)S(1)} all-to-all(f32[32,32,512]{2,1,0:T(8,128)} %fusion.42), channel_id=1, replica_groups=mesh['sx'=8,'sy'=16] {'sy'}, dimensions={0} | all-to-all | bytes 4194304 | tf_op jit(solution)/shard_map/all_to_all | solution.py:141
  197.1 26.7 %all-to-all-done.1 = f32[2,512,512]{2,0,1:T(2,128)S(1)} async-done(((f32[2,512,512]{2,0,1:T(2,128)}), f32[2,512,512]{2,0,1:T(2,128)S(1)}, u32[]{:S(2)}, u32[]{:S(2)}) %all-to-all-start.1) | async-done | bytes 2097184 | tf_op jit(solution)/shard_map/all_to_all | solution.py:140
  249.6 28.2 %gather_fusion.3 = f32[64,16,513]{1,0,2:T(8,128)} fusion(f32[64,16,521]{1,0,2:T(8,128)} %pad_bitcast_fusion, s32[64]{0:T(128)S(1)} %get-tuple-element.201), kind=kCustom, calls=%fused_computation.3 | custom fusion | bytes 4203264 | tf_op jit(solution)/shard_map/vmap()/gather | solution.py:70
  289.4 28.4 %gather_fusion.2 = f32[64,16,513]{1,0,2:T(8,128)} fusion(f32[64,16,521]{1,0,2:T(8,128)} %pad_bitcast_fusion, s32[64]{0:T(128)S(1)} %get-tuple-element.200), kind=kCustom, calls=%fused_computation.2 | custom fusion | bytes 4203264 | tf_op jit(solution)/shard_map/vmap()/gather | solution.py:70
  328.4 16.1 %fusion.156 = (f32[16,512]{1,0:T(8,128)S(1)}, f32[16,64,512]{2,1,0:T(8,128)S(1)}, f32[16,64,512]{2,1,0:T(8,128)S(1)}) fusion(f32[]{:T(128)} %bitcast.44, f32[]{:T(128)} %bitcast.52, f32[]{:T(128)} %bitcast.42, f32[]{:T(128)} %bitcast.51, f32[]{:T(128)} %bitcast.40, f32[]{:T(128)} %bitcast.50, f32[]{:T(128)} %bitcast.38, f32[]{:T(128)} %bitcast.49, ...), kind=kLoop, calls=%fused_computation.364 | loop fusion | flops 26730496 | bytes 8421952 | tf_op jit(solution)/shard_map/reduce_sum | solution.py:101
  344.5 14.9 %fusion.153 = (f32[16,512]{1,0:T(8,128)S(1)}, f32[16,64,512]{2,1,0:T(8,128)S(1)}, f32[16,64,512]{2,1,0:T(8,128)S(1)}) fusion(f32[]{:T(128)} %bitcast.44, f32[]{:T(128)} %bitcast.52, f32[]{:T(128)} %bitcast.42, f32[]{:T(128)} %bitcast.51, f32[]{:T(128)} %bitcast.40, f32[]{:T(128)} %bitcast.50, f32[]{:T(128)} %bitcast.38, f32[]{:T(128)} %bitcast.49, ...), kind=kLoop, calls=%fused_computation.363 | loop fusion | flops 26730496 | bytes 8421952 | tf_op jit(solution)/shard_map/reduce_sum | solution.py:101
  359.4 15.7 %multiply_reduce_fusion = (f32[16,512]{1,0:T(8,128)S(1)}, f32[16,64,512]{2,1,0:T(8,128)S(1)}) fusion(f32[]{:T(128)} %bitcast.70, f32[]{:T(128)} %bitcast.69, f32[]{:T(128)} %bitcast.68, f32[]{:T(128)} %bitcast.67, f32[]{:T(128)} %bitcast.66, f32[]{:T(128)} %bitcast.65, f32[]{:T(128)} %bitcast.64, f32[]{:T(128)} %bitcast.63, ...), kind=kOutput, calls=%fused_computation.195 | convolution fusion | flops 432009216 | bytes 6357568 | tf_op jit(solution)/shard_map/ij,xjz->xiz/dot_general | solution.py:100
  375.1 15.7 %multiply_reduce_fusion.3 = (f32[16,512]{1,0:T(8,128)S(1)}, f32[16,64,512]{2,1,0:T(8,128)S(1)}) fusion(f32[]{:T(128)} %bitcast.70, f32[]{:T(128)} %bitcast.69, f32[]{:T(128)} %bitcast.68, f32[]{:T(128)} %bitcast.67, f32[]{:T(128)} %bitcast.66, f32[]{:T(128)} %bitcast.65, f32[]{:T(128)} %bitcast.64, f32[]{:T(128)} %bitcast.63, ...), kind=kOutput, calls=%fused_computation.207 | convolution fusion | flops 432009216 | bytes 6357568 | tf_op jit(solution)/shard_map/ij,xjz->xiz/dot_general | solution.py:100
  390.9 14.4 %multiply_reduce_fusion.1 = f32[16,512]{1,0:T(8,128)S(1)} fusion(f32[16,64,512]{2,1,0:T(8,128)S(1)} %get-tuple-element.219, f32[]{:T(128)} %bitcast.62, f32[]{:T(128)} %bitcast.61, f32[]{:T(128)} %bitcast.60, f32[]{:T(128)} %bitcast.59, f32[]{:T(128)} %bitcast.58, f32[]{:T(128)} %bitcast.57, f32[]{:T(128)} %bitcast.56, f32[]{:T(128)} %bitcast.55, ...), kind=kLoop, calls=%fused_computation.196 | loop fusion | flops 25681920 | bytes 4227136 | tf_op jit(solution)/shard_map/reduce_sum | solution.py:106
  405.2 14.2 %multiply_reduce_fusion.4 = f32[16,512]{1,0:T(8,128)S(1)} fusion(f32[16,64,512]{2,1,0:T(8,128)S(1)} %get-tuple-element.221, f32[]{:T(128)} %bitcast.62, f32[]{:T(128)} %bitcast.61, f32[]{:T(128)} %bitcast.60, f32[]{:T(128)} %bitcast.59, f32[]{:T(128)} %bitcast.58, f32[]{:T(128)} %bitcast.57, f32[]{:T(128)} %bitcast.56, f32[]{:T(128)} %bitcast.55, ...), kind=kLoop, calls=%fused_computation.208 | loop fusion | flops 25681920 | bytes 4227136 | tf_op jit(solution)/shard_map/reduce_sum | solution.py:106
  419.4 13.9 %multiply_reduce_fusion.2 = f32[16,512]{1,0:T(8,128)S(1)} fusion(f32[16,64,512]{2,1,0:T(8,128)S(1)} %get-tuple-element.219, f32[]{:T(128)} %bitcast.43, f32[]{:T(128)} %bitcast.41, f32[]{:T(128)} %bitcast.39, f32[]{:T(128)} %bitcast.37, f32[]{:T(128)} %bitcast.35, f32[]{:T(128)} %bitcast.33, f32[]{:T(128)} %bitcast.31, f32[]{:T(128)} %bitcast.18, ...), kind=kLoop, calls=%fused_computation.197 | loop fusion | flops 25681920 | bytes 4227136 | tf_op jit(solution)/shard_map/reduce_sum | solution.py:106
  433.3 13.9 %multiply_reduce_fusion.5 = f32[16,512]{1,0:T(8,128)S(1)} fusion(f32[16,64,512]{2,1,0:T(8,128)S(1)} %get-tuple-element.221, f32[]{:T(128)} %bitcast.43, f32[]{:T(128)} %bitcast.41, f32[]{:T(128)} %bitcast.39, f32[]{:T(128)} %bitcast.37, f32[]{:T(128)} %bitcast.35, f32[]{:T(128)} %bitcast.33, f32[]{:T(128)} %bitcast.31, f32[]{:T(128)} %bitcast.18, ...), kind=kLoop, calls=%fused_computation.209 | loop fusion | flops 25681920 | bytes 4227136 | tf_op jit(solution)/shard_map/reduce_sum | solution.py:106
  447.3 28.4 %gather_fusion.1 = f32[64,16,513]{1,0,2:T(8,128)} fusion(f32[64,16,521]{1,0,2:T(8,128)} %pad_bitcast_fusion, s32[64]{0:T(128)S(1)} %get-tuple-element.199), kind=kCustom, calls=%fused_computation.1 | custom fusion | bytes 4203264 | tf_op jit(solution)/shard_map/vmap()/gather | solution.py:70
  486.2 14.9 %fusion.150 = (f32[16,512]{1,0:T(8,128)S(1)}, f32[16,64,512]{2,1,0:T(8,128)S(1)}, f32[16,64,512]{2,1,0:T(8,128)S(1)}) fusion(f32[]{:T(128)} %bitcast.44, f32[]{:T(128)} %bitcast.52, f32[]{:T(128)} %bitcast.42, f32[]{:T(128)} %bitcast.51, f32[]{:T(128)} %bitcast.40, f32[]{:T(128)} %bitcast.50, f32[]{:T(128)} %bitcast.38, f32[]{:T(128)} %bitcast.49, ...), kind=kLoop, calls=%fused_computation.362 | loop fusion | flops 26730496 | bytes 8421952 | tf_op jit(solution)/shard_map/reduce_sum | solution.py:101
  501.1 15.7 %multiply_reduce_fusion.6 = (f32[16,512]{1,0:T(8,128)S(1)}, f32[16,64,512]{2,1,0:T(8,128)S(1)}) fusion(f32[]{:T(128)} %bitcast.70, f32[]{:T(128)} %bitcast.69, f32[]{:T(128)} %bitcast.68, f32[]{:T(128)} %bitcast.67, f32[]{:T(128)} %bitcast.66, f32[]{:T(128)} %bitcast.65, f32[]{:T(128)} %bitcast.64, f32[]{:T(128)} %bitcast.63, ...), kind=kOutput, calls=%fused_computation.219 | convolution fusion | flops 432009216 | bytes 6357568 | tf_op jit(solution)/shard_map/ij,xjz->xiz/dot_general | solution.py:100
  516.8 14.2 %multiply_reduce_fusion.7 = f32[16,512]{1,0:T(8,128)S(1)} fusion(f32[16,64,512]{2,1,0:T(8,128)S(1)} %get-tuple-element.223, f32[]{:T(128)} %bitcast.62, f32[]{:T(128)} %bitcast.61, f32[]{:T(128)} %bitcast.60, f32[]{:T(128)} %bitcast.59, f32[]{:T(128)} %bitcast.58, f32[]{:T(128)} %bitcast.57, f32[]{:T(128)} %bitcast.56, f32[]{:T(128)} %bitcast.55, ...), kind=kLoop, calls=%fused_computation.220 | loop fusion | flops 25681920 | bytes 4227136 | tf_op jit(solution)/shard_map/reduce_sum | solution.py:106
  531.0 13.9 %multiply_reduce_fusion.8 = f32[16,512]{1,0:T(8,128)S(1)} fusion(f32[16,64,512]{2,1,0:T(8,128)S(1)} %get-tuple-element.223, f32[]{:T(128)} %bitcast.43, f32[]{:T(128)} %bitcast.41, f32[]{:T(128)} %bitcast.39, f32[]{:T(128)} %bitcast.37, f32[]{:T(128)} %bitcast.35, f32[]{:T(128)} %bitcast.33, f32[]{:T(128)} %bitcast.31, f32[]{:T(128)} %bitcast.18, ...), kind=kLoop, calls=%fused_computation.221 | loop fusion | flops 25681920 | bytes 4227136 | tf_op jit(solution)/shard_map/reduce_sum | solution.py:106
  545.2 28.4 %gather_fusion = f32[64,16,513]{1,0,2:T(8,128)} fusion(f32[64,16,521]{1,0,2:T(8,128)} %pad_bitcast_fusion, s32[64]{0:T(128)S(1)} %get-tuple-element.198), kind=kCustom, calls=%fused_computation | custom fusion | bytes 4203264 | tf_op jit(solution)/shard_map/vmap()/gather | solution.py:70
  584.2 14.7 %fusion.147 = (f32[16,512]{1,0:T(8,128)S(1)}, f32[16,64,512]{2,1,0:T(8,128)S(1)}, f32[16,64,512]{2,1,0:T(8,128)S(1)}) fusion(f32[]{:T(128)} %bitcast.44, f32[]{:T(128)} %bitcast.52, f32[]{:T(128)} %bitcast.42, f32[]{:T(128)} %bitcast.51, f32[]{:T(128)} %bitcast.40, f32[]{:T(128)} %bitcast.50, f32[]{:T(128)} %bitcast.38, f32[]{:T(128)} %bitcast.49, ...), kind=kLoop, calls=%fused_computation.361 | loop fusion | flops 26730496 | bytes 8421952 | tf_op jit(solution)/shard_map/reduce_sum | solution.py:101
  598.9 15.8 %multiply_reduce_fusion.9 = (f32[16,512]{1,0:T(8,128)S(1)}, f32[16,64,512]{2,1,0:T(8,128)S(1)}) fusion(f32[]{:T(128)} %bitcast.70, f32[]{:T(128)} %bitcast.69, f32[]{:T(128)} %bitcast.68, f32[]{:T(128)} %bitcast.67, f32[]{:T(128)} %bitcast.66, f32[]{:T(128)} %bitcast.65, f32[]{:T(128)} %bitcast.64, f32[]{:T(128)} %bitcast.63, ...), kind=kOutput, calls=%fused_computation.231 | convolution fusion | flops 432009216 | bytes 6357568 | tf_op jit(solution)/shard_map/ij,xjz->xiz/dot_general | solution.py:100
  615.4 15.3 %multiply_reduce_fusion.11 = f32[16,512]{1,0:T(8,128)S(1)} fusion(f32[16,64,512]{2,1,0:T(8,128)S(1)} %get-tuple-element.225, f32[]{:T(128)} %bitcast.43, f32[]{:T(128)} %bitcast.41, f32[]{:T(128)} %bitcast.39, f32[]{:T(128)} %bitcast.37, f32[]{:T(128)} %bitcast.35, f32[]{:T(128)} %bitcast.33, f32[]{:T(128)} %bitcast.31, f32[]{:T(128)} %bitcast.18, ...), kind=kLoop, calls=%fused_computation.233 | loop fusion | flops 25681920 | bytes 4227136 | tf_op jit(solution)/shard_map/reduce_sum | solution.py:106
  630.8 14.2 %multiply_reduce_fusion.10 = f32[16,512]{1,0:T(8,128)S(1)} fusion(f32[16,64,512]{2,1,0:T(8,128)S(1)} %get-tuple-element.225, f32[]{:T(128)} %bitcast.62, f32[]{:T(128)} %bitcast.61, f32[]{:T(128)} %bitcast.60, f32[]{:T(128)} %bitcast.59, f32[]{:T(128)} %bitcast.58, f32[]{:T(128)} %bitcast.57, f32[]{:T(128)} %bitcast.56, f32[]{:T(128)} %bitcast.55, ...), kind=kLoop, calls=%fused_computation.232 | loop fusion | flops 25681920 | bytes 4227136 | tf_op jit(solution)/shard_map/reduce_sum | solution.py:106
  645.5 15.4 %all-gather.3.cloned.1.call-done = f32[32,16,512]{2,1,0:T(8,128)} async-done(((f32[4,16,512]{2,1,0:T(8,128)}), f32[32,16,512]{2,1,0:T(8,128)}) %all-gather.3.cloned.1.call-update) | async-done | bytes 1048592 | tf_op jit(solution)/shard_map/all_gather | solution.py:32
  670.4 83.5 %all-reduce.16.cloned.1.call-done = f32[4,4,16,512]{3,1,0,2:T(4,128)} async-done(((f32[4,4,16,512]{3,1,0,2:T(4,128)}), f32[4,4,16,512]{3,1,0,2:T(4,128)}) %all-reduce.16.cloned.1.call-update) | async-done | bytes 524304
  (145 shorter events, 236.7 us)
Async XLA Ops:
  7.2 187.0 %copy-start = (s32[4,512]{1,0:T(4,128)S(1)}, s32[4,512]{1,0:T(4,128)}, u32[]{:S(2)}) copy-start(s32[4,512]{1,0:T(4,128)} %param.15) | copy-start | bytes 24580
  10.1 8.6 %collective-permute-start = (f32[2,1,32,512]{3,2,1,0:T(8,128)S(1)}, f32[2,1,32,512]{3,2,1,0:T(8,128)S(1)}, u32[]{:S(2)}, u32[]{:S(2)}) collective-permute-start(f32[2,1,32,512]{3,2,1,0:T(8,128)S(1)} %get-tuple-element.164), channel_id=1, source_target_pairs={{0,16},{16,32},{32,48},{48,64},{64,80},{80,96},{96,112},{1,17},{17... | collective-permute-start | bytes 393224 | tf_op jit(solution)/shard_map/ppermute | solution.py:22
  16.0 8.4 %collective-permute-start.1 = (f32[2,1,32,512]{3,2,1,0:T(8,128)S(1)}, f32[2,1,32,512]{3,2,1,0:T(8,128)S(1)}, u32[]{:S(2)}, u32[]{:S(2)}) collective-permute-start(f32[2,1,32,512]{3,2,1,0:T(8,128)S(1)} %get-tuple-element.165), channel_id=1, source_target_pairs={{16,0},{32,16},{48,32},{64,48},{80,64},{96,80},{112,96},{17,1},{33... | collective-permute-start | bytes 393224 | tf_op jit(solution)/shard_map/ppermute | solution.py:23
  24.6 2.6 collective-permute-start.2
  25.9 5.1 collective-permute-start.3
  43.3 6.0 collective-permute-start.4
  46.9 8.4 %collective-permute-start.5 = (f32[2,1,32,512]{3,2,1,0:T(8,128)S(1)}, f32[2,1,32,512]{3,2,1,0:T(8,128)S(1)}, u32[]{:S(2)}, u32[]{:S(2)}) collective-permute-start(f32[2,1,32,512]{3,2,1,0:T(8,128)S(1)} %get-tuple-element.163), channel_id=1, source_target_pairs={{16,0},{32,16},{48,32},{64,48},{80,64},{96,80},{112,96},{17,1},{33... | collective-permute-start | bytes 393224 | tf_op jit(solution)/shard_map/ppermute | solution.py:23
  55.5 5.4 collective-permute-start.6
  59.6 4.9 collective-permute-start.7
  75.6 15.2 %copy-start.6 = (f32[1,32,32,512]{3,2,1,0:T(8,128)S(1)}, f32[1,32,32,512]{3,2,1,0:T(8,128)}, u32[]{:S(2)}) copy-start(f32[1,32,32,512]{3,2,1,0:T(8,128)} %get-tuple-element.138) | copy-start | bytes 6291460
  76.7 8.3 %collective-permute-start.8 = (f32[2,1,32,512]{3,2,1,0:T(8,128)S(1)}, f32[2,1,32,512]{3,2,1,0:T(8,128)S(1)}, u32[]{:S(2)}, u32[]{:S(2)}) collective-permute-start(f32[2,1,32,512]{3,2,1,0:T(8,128)S(1)} %get-tuple-element.160), channel_id=1, source_target_pairs={{0,16},{16,32},{32,48},{48,64},{64,80},{80,96},{96,112},{1,17},{17... | collective-permute-start | bytes 393224 | tf_op jit(solution)/shard_map/ppermute | solution.py:22
  82.5 8.4 %collective-permute-start.9 = (f32[2,1,32,512]{3,2,1,0:T(8,128)S(1)}, f32[2,1,32,512]{3,2,1,0:T(8,128)S(1)}, u32[]{:S(2)}, u32[]{:S(2)}) collective-permute-start(f32[2,1,32,512]{3,2,1,0:T(8,128)S(1)} %get-tuple-element.161), channel_id=1, source_target_pairs={{16,0},{32,16},{48,32},{64,48},{80,64},{96,80},{112,96},{17,1},{33... | collective-permute-start | bytes 393224 | tf_op jit(solution)/shard_map/ppermute | solution.py:23
  91.1 5.9 collective-permute-start.10
  95.2 4.6 collective-permute-start.11
  112.1 6.7 collective-permute-start.12
  116.3 8.4 %collective-permute-start.13 = (f32[2,1,32,512]{3,2,1,0:T(8,128)S(1)}, f32[2,1,32,512]{3,2,1,0:T(8,128)S(1)}, u32[]{:S(2)}, u32[]{:S(2)}) collective-permute-start(f32[2,1,32,512]{3,2,1,0:T(8,128)S(1)} %get-tuple-element.159), channel_id=1, source_target_pairs={{16,0},{32,16},{48,32},{64,48},{80,64},{96,80},{112,96},{17,1},{33... | collective-permute-start | bytes 393224 | tf_op jit(solution)/shard_map/ppermute | solution.py:23
  125.0 5.4 collective-permute-start.14
  129.1 4.0 collective-permute-start.15
  188.3 35.4 %all-to-all-start.1 = ((f32[2,512,512]{2,0,1:T(2,128)}), f32[2,512,512]{2,0,1:T(2,128)S(1)}, u32[]{:S(2)}, u32[]{:S(2)}) async-start(f32[2,512,512]{2,0,1:T(2,128)} %copy.32), calls=%async_computation.1 | async-start | bytes 4194304 | tf_op jit(solution)/shard_map/all_to_all | solution.py:140
  194.0 467.0 %all-gather.3.cloned.1.call-start = ((), (), s32[]{:S(2)}) async-start(), calls=%async_computation.2 | async-start | bytes 1179648 | tf_op jit(solution)/shard_map/all_gather | solution.py:32
  598.9 15.8 %copy-start.9 = (f32[16,64,512]{2,1,0:T(8,128)}, f32[16,64,512]{2,1,0:T(8,128)S(1)}, u32[]{:S(2)}) copy-start(f32[16,64,512]{2,1,0:T(8,128)S(1)} %get-tuple-element.118) | copy-start | bytes 6291460
  615.4 138.5 %all-reduce.16.cloned.1.call-start = ((), (), s32[]{:S(2)}) async-start(), calls=%async_computation.3 | async-start | bytes 1048576
  615.4 15.4 %copy-start.10 = (f32[16,64,512]{2,1,0:T(8,128)S(1)}, f32[16,64,512]{2,1,0:T(8,128)}, u32[]{:S(2)}) copy-start(f32[16,64,512]{2,1,0:T(8,128)} %copy-done.9) | copy-start | bytes 6291460
  667.8 89.1 %copy-start.1 = (s32[4,512]{1,0:T(4,128)S(1)}, s32[4,512]{1,0:T(4,128)}, u32[]{:S(2)}) copy-start(s32[4,512]{1,0:T(4,128)} %param.15) | copy-start | bytes 24580
  (11 other events, 87.7 us)
Sparse Core Ops, SparseCore 0:
  615.5 45.4 all-gather.2
  669.3 84.5 all-reduce.15
where the time goes:
time: 776 us; the launch traced here: 764 us
  other arithmetic  232 us (30%)
  local copies, waits for them, and re-layouts  195 us (25%)
  waiting for transfers between devices  167 us (22%)
  matrix products  62.9 us (8%)
  starting transfers between devices  49.7 us (6%)
  blocking collectives  41.7 us (5%)
  between operations  15.6 us (2%)
    gather x8, local copies, waits for them, and re-layouts, shear_view(): lax.dynamic_slice_in_dim(plane, start, z_cells + 1, 1)  157 us
    reduce_sum x8, other arithmetic, render_views(): jnp.sum(channel * weight, axis=1)  114 us
    unnamed x3, waiting for transfers between devices  83.5 us
    dot_general x4, matrix products, render_views(): jnp.einsum('ij,xjz->xiz', lower_tri, optical, precision=lax.Precision.HIG...  62.9 us
    reduce_sum x4, other arithmetic, render_views(): slab_total = jnp.sum(optical, axis=1)  60.6 us
    all_to_all x1, blocking collectives, per_device(): lax.all_to_all(field_now, 'sy', split_axis=0, concat_axis=1, tiled=True)  41.7 us
    ppermute x8, waiting for transfers between devices, with_halo(): after = lax.ppermute(leading, axis, down)  36.1 us
    ppermute x8, starting transfers between devices, with_halo(): before = lax.ppermute(last, axis, up)  33 us
  transfers between devices with their start and end apart: 19, of which 15 were waited for; matrix products, arithmetic and copies ran while one was open for 4% of the time, Pallas kernels for 0%

commit v1 on v0

v1 whole, which is shorter than its diff:
```python
import functools

import jax
import jax.numpy as jnp
from jax import lax
from jax.experimental import pallas as pl
from jax.experimental.pallas import tpu as pltpu
from jax.sharding import PartitionSpec as P

STEPS = 4
VIEWS = 4
BUMPS = 8
W = STEPS
LOG2E = 1.4426950408889634
GAIN = 2.0 * LOG2E**0.5

F32 = jnp.float32


def shift(value, axis, up):
    size = lax.axis_size(axis)
    pairs = [(i, i + 1) for i in range(size - 1)]
    if not up:
        pairs = [(j, i) for i, j in pairs]
    return lax.ppermute(value, axis, pairs)


def stencil_kernel(
    place, u_hbm, d_hbm, r_hbm, xm_hbm, xp_hbm, yn, yp, cn, cp,
    out_hbm, ft_hbm,
    ua, ub, dd, rr, kbuf, fbuf, ft, sems, osem,
):
    cx, cy, nz = u_hbm.shape
    blocks = nz // 128
    tiles = cy // 8 + 1
    copies = []
    for src, dst in (
        (u_hbm, ua.at[W : W + cx, 0:cy]),
        (d_hbm, dd.at[W : W + cx, 0:cy]),
        (r_hbm, rr.at[W : W + cx, 0:cy]),
        (xm_hbm.at[0:W], ua.at[0:W, 0:cy]),
        (xm_hbm.at[W : 2 * W], dd.at[0:W, 0:cy]),
        (xm_hbm.at[2 * W : 3 * W - 1], rr.at[1:W, 0:cy]),
        (xp_hbm.at[0:W], ua.at[W + cx : 2 * W + cx, 0:cy]),
        (xp_hbm.at[W : 2 * W], dd.at[W + cx : 2 * W + cx, 0:cy]),
        (xp_hbm.at[2 * W : 3 * W - 1], rr.at[W + cx : 2 * W + cx - 1, 0:cy]),
    ):
        copies.append(pltpu.make_async_copy(src, dst, sems.at[len(copies)]))
    for copy in copies:
        copy.start()

    sx, sy = place[0], place[1]
    last_x, last_y = place[2] - 1, place[3] - 1

    def edge_rows(x, carry):
        for which, dst in enumerate((ua, dd, rr)):
            dst[W + x, cy : cy + W, :] = yn[which, x]
            dst[W + x, cy + W : cy + 2 * W, :] = yp[which, x]
        return carry

    lax.fori_loop(0, cx, edge_rows, 0)
    for side, base in ((0, 0), (1, W + cx)):
        for i in range(W):
            at = side * (3 * W - 1)
            for first, dst in ((0, ua), (W, dd)):
                dst[base + i, cy : cy + W, :] = cn[at + first + i]
                dst[base + i, cy + W : cy + 2 * W, :] = cp[at + first + i]
        for i in range(W - 1):
            at = side * (3 * W - 1) + 2 * W + i
            plane = base + i + (1 if side == 0 else 0)
            rr[plane, cy : cy + W, :] = cn[at]
            rr[plane, cy + W : cy + 2 * W, :] = cp[at]
    for i in range(W):
        ub[i] = jnp.zeros((cy + 8, nz), F32)
        ub[W + cx + i] = jnp.zeros((cy + 8, nz), F32)

    sub = lax.broadcasted_iota(jnp.int32, (8, 128), 0)
    lane = lax.broadcasted_iota(jnp.int32, (8, 128), 1)
    sub_last, sub_first = sub == 7, sub == 0
    lane_last, lane_first = lane == 127, lane == 0
    inside = jnp.where(sub < W, (sy < last_y).astype(F32), (sy > 0).astype(F32))

    for copy in copies:
        copy.wait()

    def cut(tile, block):
        return (slice(8 * tile, 8 * tile + 8), slice(128 * block, 128 * block + 128))

    def conductance(src, plane):
        slot = lax.rem(plane, 2)
        for t in range(tiles):
            for b in range(blocks):
                at = cut(t, b)
                kbuf[(slot,) + at] = dd[(plane,) + at] * (
                    0.5 + 0.2 * jnp.tanh(src[(plane,) + at])
                )

    def face(src, plane):
        slot = lax.rem(plane, 2)
        for t in range(tiles):
            for b in range(blocks):
                at = cut(t, b)
                fbuf[at] = (kbuf[(slot,) + at] + kbuf[(1 - slot,) + at]) * (
                    src[(plane,) + at] - src[(plane - 1,) + at]
                )

    def advance(src, dst, last, plane):
        conductance(src, plane + 1)
        slot = lax.rem(plane, 2)
        for b in range(blocks):
            u = [src[(plane,) + cut(t, b)] for t in range(tiles)]
            k = [kbuf[(slot,) + cut(t, b)] for t in range(tiles)]
            u_up = [pltpu.roll(v, 7, 0) for v in u]
            k_up = [pltpu.roll(v, 7, 0) for v in k]
            flux = []
            for t in range(tiles):
                n = (t + 1) % tiles
                un = jnp.where(sub_last, u_up[n], u_up[t])
                kn = jnp.where(sub_last, k_up[n], k_up[t])
                flux.append((k[t] + kn) * (un - u[t]))
            down = [pltpu.roll(v, 1, 0) for v in flux]
            for t in range(tiles - 1 if last else tiles):
                at = cut(t, b)
                change = flux[t] - jnp.where(sub_first, down[t - 1], down[t])
                ux = src[(plane + 1,) + at]
                kx = kbuf[(1 - slot,) + at]
                fx = (k[t] + kx) * (ux - u[t])
                change = change + (fx - fbuf[at])
                fbuf[at] = fx

                def z_face(low):
                    ul = src[(plane,) + cut(t, low)] if low != b else u[t]
                    kl = kbuf[(slot,) + cut(t, low)] if low != b else k[t]
                    un, kn = pltpu.roll(ul, 127, 1), pltpu.roll(kl, 127, 1)
                    if low + 1 < blocks:
                        u2 = pltpu.roll(src[(plane,) + cut(t, low + 1)], 127, 1)
                        k2 = pltpu.roll(kbuf[(slot,) + cut(t, low + 1)], 127, 1)
                    else:
                        u2 = k2 = jnp.zeros((8, 128), F32)
                    un, kn = jnp.where(lane_last, u2, un), jnp.where(lane_last, k2, kn)
                    return (kl + kn) * (un - ul)

                fz = z_face(b)
                rolled = pltpu.roll(fz, 1, 1)
                if b == 0:
                    carry = k[t] * u[t]
                else:
                    ul, kl = src[(plane,) + cut(t, b - 1)], kbuf[(slot,) + cut(t, b - 1)]
                    carry = (k[t] + pltpu.roll(kl, 1, 1)) * (u[t] - pltpu.roll(ul, 1, 1))
                change = change + (fz - jnp.where(lane_first, carry, rolled))
                new = u[t] + (change + rr[(plane,) + at] * jnp.tanh(u[t]))
                if t == tiles - 1:
                    new = new * inside
                if last:
                    dst[(plane - W,) + at] = new
                else:
                    dst[(plane,) + at] = new

    src, dst = ua, ub
    for step in range(STEPS):
        last = step == STEPS - 1
        low = jnp.where(sx == 0, W, step + 1)
        high = jnp.where(sx == last_x, W + cx, 2 * W + cx - 1 - step)
        if last:
            low, high = W, W + cx
        conductance(src, low - 1)
        conductance(src, low)
        face(src, low)

        def body(plane, carry, src=src, dst=ft if last else dst, last=last):
            advance(src, dst, last, plane)
            return carry

        lax.fori_loop(low, high, body, 0)
        if not last:
            src, dst = dst, src
    done = pltpu.make_async_copy(ft, out_hbm, osem.at[0])
    done.start()
    turned = dst

    def turn(xg, carry):
        for yg in range(cy // 8):
            for b in range(blocks):
                piece = ft[pl.ds(8 * xg, 8), 8 * yg : 8 * yg + 8, 128 * b : 128 * b + 128]
                turned[
                    8 * yg : 8 * yg + 8, pl.ds(pl.multiple_of(8 * xg, 8), 8), 128 * b : 128 * b + 128
                ] = jnp.transpose(piece, (1, 0, 2))
        return carry

    lax.fori_loop(0, cx // 8, turn, 0)
    move = pltpu.make_async_copy(turned.at[0:cy, 0:cx], ft_hbm, osem.at[1])
    move.start()
    done.wait()
    move.wait()


def stencil(place, u, d, r, xm, xp, yn, yp, cn, cp):
    cx, cy, nz = u.shape
    anywhere = pl.BlockSpec(memory_space=pl.ANY)
    local = pl.BlockSpec(memory_space=pltpu.VMEM)
    wide = (cx + 2 * W, cy + 8, nz)
    return pl.pallas_call(
        stencil_kernel,
        out_shape=(
            jax.ShapeDtypeStruct((cx, cy, nz), F32),
            jax.ShapeDtypeStruct((cy, cx, nz), F32),
        ),
        in_specs=[pl.BlockSpec(memory_space=pltpu.SMEM)] + [anywhere] * 5 + [local] * 4,
        out_specs=(anywhere, anywhere),
        scratch_shapes=[
            pltpu.VMEM(wide, F32),
            pltpu.VMEM(wide, F32),
            pltpu.VMEM(wide, F32),
            pltpu.VMEM(wide, F32),
            pltpu.VMEM((2, cy + 8, nz), F32),
            pltpu.VMEM((cy + 8, nz), F32),
            pltpu.VMEM((cx, cy, nz), F32),
            pltpu.SemaphoreType.DMA((9,)),
            pltpu.SemaphoreType.DMA((2,)),
        ],
        name="stencil",
    )(place, u, d, r, xm, xp, yn, yp, cn, cp)


def render_kernel(offs, cen, lev, mix, ft, sign_ref, out, sheared):
    view = pl.program_id(1)
    depth, rows, nz = ft.shape
    blocks = nz // 128
    lane = lax.broadcasted_iota(jnp.int32, (rows, 128), 1)
    lane_last = lane == 127
    zero = jnp.zeros((rows, 128), F32)

    def shear(y, carry):
        q = offs[view, y]
        whole = q // 4
        part = (q - 4 * whole).astype(F32) * 0.25
        cells = [ft[y, :, 128 * b : 128 * b + 128] for b in range(blocks)]
        back = [pltpu.roll(c, 127, 1) for c in cells] + [zero]
        mixed = []
        for b in range(blocks):
            after = jnp.where(lane_last, back[b + 1], back[b])
            mixed.append((cells[b] + part * (after - cells[b])) * GAIN)
        amount = lax.rem(128 - whole, 128)
        moved = [pltpu.roll(c, amount, 1) for c in mixed] + [zero]
        keep = lane < 128 - whole
        for b in range(blocks):
            sheared[y, :, 128 * b : 128 * b + 128] = jnp.where(keep, moved[b], moved[b + 1])
        return carry

    lax.fori_loop(0, depth, shear, 0, unroll=2)

    for b in range(blocks):
        at = slice(128 * b, 128 * b + 128)
        sign = jnp.broadcast_to(sign_ref[0, :, at], (rows, 128))
        rising = sign < 0.0
        light = jnp.ones((rows, 128), F32)
        sums = [zero] * BUMPS
        for y in range(depth):
            s = sheared[y, :, at]
            bumps = []
            for i in range(BUMPS):
                t = s - cen[i]
                bumps.append(jnp.exp2(lev[i] - t * t))
            pairs = [bumps[i] + bumps[i + 1] for i in range(0, BUMPS, 2)]
            total = (pairs[0] + pairs[1]) + (pairs[2] + pairs[3])
            after = light * jnp.exp2(total * sign)
            weight = light - after
            light = after
            sums = [sums[i] + bumps[i] * weight for i in range(BUMPS)]
        inverse = 1.0 / light
        through = jnp.where(rising, light, inverse)
        scale = jnp.where(rising, 1.0, -inverse)
        channels = []
        for c in range(3):
            value = mix[c, 0] * sums[0]
            for i in range(1, BUMPS):
                value = value + mix[c, i] * sums[i]
            channels.append(value * scale)
        channels.append(through)
        for d in range(rows // 2):
            out[d, :, at] = jnp.concatenate([c[2 * d : 2 * d + 2] for c in channels], axis=0)


def render(offs, cen, lev, mix, ft, signs):
    cy, cx, nz = ft.shape
    smem = pl.BlockSpec(memory_space=pltpu.SMEM)
    return pl.pallas_call(
        render_kernel,
        out_shape=jax.ShapeDtypeStruct((cx // 2, 8 * VIEWS, nz), F32),
        grid=(cx // 8, VIEWS),
        in_specs=[
            smem,
            smem,
            smem,
            smem,
            pl.BlockSpec((cy, 8, nz), lambda i, v: (0, i, 0)),
            pl.BlockSpec((1, 1, nz), lambda i, v: (v, 0, 0)),
        ],
        out_specs=pl.BlockSpec((4, 8, nz), lambda i, v: (i, v, 0)),
        scratch_shapes=[pltpu.VMEM((cy, 8, nz), F32)],
        name="render",
    )(offs, cen, lev, mix, ft, signs)


def combine_kernel(parts, sign_ref, image, trans):
    count, _, nz = parts.shape
    sub = lax.broadcasted_iota(jnp.int32, (8, nz), 0)
    for view in range(VIEWS):
        rising = jnp.broadcast_to(sign_ref[view], (8, nz)) < 0.0
        total = jnp.zeros((8, nz), F32)
        ahead = jnp.ones((8, nz), F32)
        for source in range(count):
            block = parts[source, 8 * view : 8 * view + 8, :]
            tail = jnp.where(sub >= 6, block, 0.0)
            pair = tail + pltpu.roll(tail, 4, 0)
            light = pair + pltpu.roll(pair, 2, 0)
            total = total * jnp.where(rising, 1.0, light) + block * jnp.where(rising, ahead, 1.0)
            ahead = ahead * light
        for c in range(3):
            image[view, c] = total[2 * c : 2 * c + 2]
        trans[view] = ahead[6:8]


def combine(parts, signs):
    nz = parts.shape[2]
    return pl.pallas_call(
        combine_kernel,
        out_shape=(
            jax.ShapeDtypeStruct((VIEWS, 3, 2, nz), F32),
            jax.ShapeDtypeStruct((VIEWS, 2, nz), F32),
        ),
        name="combine",
    )(parts, signs)


def per_device(u, d, r, offsets, depth_order, centres, colour, opacity):
    cx, cy, nz = u.shape
    place = jnp.stack(
        [
            lax.axis_index("sx"),
            lax.axis_index("sy"),
            jnp.int32(lax.axis_size("sx")),
            jnp.int32(lax.axis_size("sy")),
        ]
    ).astype(jnp.int32)
    up_x = jnp.concatenate([u[cx - W :], d[cx - W :], r[cx - W + 1 :]])
    down_x = jnp.concatenate([u[:W], d[:W], r[: W - 1]])
    xm = shift(up_x, "sx", True)
    xp = shift(down_x, "sx", False)
    up_y = jnp.stack([a[:, cy - W :] for a in (u, d, r)])
    down_y = jnp.stack([a[:, :W] for a in (u, d, r)])
    yp = shift(up_y, "sy", True)
    yn = shift(down_y, "sy", False)
    cp = shift(jnp.concatenate([xm[:, cy - W :], xp[:, cy - W :]]), "sy", True)
    cn = shift(jnp.concatenate([xm[:, :W], xp[:, :W]]), "sy", False)
    field, turned = stencil(place, u, d, r, xm, xp, yn, yp, cn, cp)

    offs = lax.dynamic_slice_in_dim(offsets, lax.axis_index("sy") * cy, cy, 1)
    signs = jnp.where(depth_order == 0, -1.0, 1.0).astype(F32)[:, None, :]
    level = opacity * LOG2E
    parts = render(offs, centres * GAIN, jnp.log2(level), colour / level, turned, signs)
    parts = lax.all_to_all(parts, "sy", split_axis=0, concat_axis=0, tiled=True)
    image, trans = combine(parts, signs)
    return field, image, trans


def solution(mesh):
    grid = P("sx", "sy", None)
    return jax.shard_map(
        per_device,
        mesh=mesh,
        in_specs=(grid, grid, grid, P(), P(), P(), P(), P()),
        out_specs=(
            grid,
            P(None, None, ("sx", "sy"), None),
            P(None, ("sx", "sy"), None),
        ),
        check_vma=False,
    )
```

time: 776 us -> 188 us (0.24); the launches traced: 764 us -> 185 us
  other arithmetic: 232 us -> 5.8 us
  local copies, waits for them, and re-layouts: 195 us -> 8.3 us
  waiting for transfers between devices: 167 us -> 25.8 us
  Pallas kernels: 0 us -> 102 us
  matrix products: 62.9 us -> 0 us
  starting transfers between devices: 49.7 us -> 16.5 us
  blocking collectives: 41.7 us -> 25.9 us
  between operations: 15.6 us -> 0.84 us
    reduce_sum x12 -> x0, other arithmetic: 175 us -> none  [the longest x8 114 us: render_views(): jnp.sum(channel * weight, axis=1)]
    gather x8 -> x0, local copies, waits for them, and re-layouts: 157 us -> none  [shear_view(): lax.dynamic_slice_in_dim(plane, start, z_cells + 1, 1)]
    pallas_call x0 -> x3, Pallas kernels: none -> 102 us  [the longest x1 58.1 us: render(): pl.pallas_call(render_kernel, out_shape=jax.ShapeDtypeStruct((cx // 2, 8...]
    unnamed x3 -> x0, waiting for transfers between devices: 83.5 us -> none
    dot_general x4 -> x0, matrix products: 62.9 us -> none  [render_views(): jnp.einsum('ij,xjz->xiz', lower_tri, optical, precision=lax.Precision.HIG...]
    another operation x7 -> x3, other arithmetic: 31.7 us -> 2.73 us  [the longest x1 1.06 us: per_device(): down_y = jnp.stack([a[:, :W] for a in (u, d, r)])]
    ppermute x16 -> x6, starting transfers between devices: 43.8 us -> 16.5 us  [shift(): return lax.ppermute(value, axis, pairs)]
    all_to_all x1 -> x0, waiting for transfers between devices: 26.7 us -> none  [per_device(): lax.all_to_all(lax.all_to_all(field_now, 'sy', split_axis=0, concat_axis=...]
  transfers between devices with their start and end apart: 19 -> 6, of which waited for: 15 -> 3; matrix products, arithmetic and copies ran while one was open for 4% -> 5% of each run, Pallas kernels for 0% -> 0%
where the time goes in v1:
time: 188 us; the launch traced here: 185 us
  Pallas kernels  102 us (54%)
  blocking collectives  25.9 us (14%)
  waiting for transfers between devices  25.8 us (14%)
  starting transfers between devices  16.5 us (9%)
  local copies, waits for them, and re-layouts  8.3 us (4%)
  other arithmetic  5.8 us (3%)
    pallas_call x1, Pallas kernels, render(): pl.pallas_call(render_kernel, out_shape=jax.ShapeDtypeStruct((cx // 2, 8...  58.1 us
    pallas_call x1, Pallas kernels, stencil(): pl.pallas_call(stencil_kernel, out_shape=(jax.ShapeDtypeStruct((cx, cy, n...  41.5 us
    all_to_all x1, blocking collectives, per_device(): parts = lax.all_to_all(parts, 'sy', split_axis=0, concat_axis=0, tiled=True)  25.9 us
    ppermute x6, waiting for transfers between devices, shift(): return lax.ppermute(value, axis, pairs)  25.8 us
    ppermute x6, starting transfers between devices, shift(): return lax.ppermute(value, axis, pairs)  16.5 us
  transfers between devices with their start and end apart: 6, of which 3 were waited for; matrix products, arithmetic and copies ran while one was open for 5% of the time, Pallas kernels for 0%

profile of v1, /device:TPU:0, one launch (start us, length us, event | category | flops | bytes accessed | tf_op | source)
XLA Modules:
  0.0 185.1 jit_solution(10871307569015276358)
XLA Ops:
  0.6 1.1 fusion.2
  1.7 1.3 fusion
  3.0 0.9 pad_maximum_fusion.3
  3.9 1.3 collective-permute-start.1
  5.2 0.9 pad_maximum_fusion.2
  6.1 6.6 %collective-permute-start = (f32[11,32,512]{2,1,0:T(8,128)}, f32[11,32,512]{2,1,0:T(8,128)S(1)}, u32[]{:S(2)}, u32[]{:S(2)}) collective-permute-start(f32[11,32,512]{2,1,0:T(8,128)} %pad_maximum_fusion.2), channel_id=1, source_target_pairs={{0,16},{16,32},{32,48},{48,64},{64,80},{80,96},{96,112},{1,17},{17... | collective-permute-start | bytes 2162696 | tf_op jit(solution)/shard_map/ppermute | solution.py:25
  12.7 1.8 slice_bitcast_fusion
  14.5 1.3 slice_bitcast_fusion.2
  15.9 1.1 pad_maximum_fusion
  16.9 1.3 collective-permute-start.2
  18.2 1.1 pad_maximum_fusion.1
  19.3 3.1 %collective-permute-start.3 = (f32[3,32,4,512]{3,2,1,0:T(4,128)}, f32[3,32,4,512]{3,2,1,0:T(4,128)S(1)}, u32[]{:S(2)}, u32[]{:S(2)}) collective-permute-start(f32[3,32,4,512]{3,2,1,0:T(4,128)} %pad_maximum_fusion.1), channel_id=1, source_target_pairs={{0,1},{1,2},{2,3},{3,4},{4,5},{5,6},{6,7},{7,8},{8,9},{9,10},{10,1... | collective-permute-start | bytes 2359304 | tf_op jit(solution)/shard_map/ppermute | solution.py:25
  22.4 0.6 broadcast_in_dim.14.sign_ref
  23.0 0.6 pad_add_fusion.place
  23.6 0.6 constant_dynamic-slice_fusion.offs
  24.8 1.3 collective-permute-done.1.xp_hbm
  26.2 24.1 %collective-permute-done.xm_hbm = f32[11,32,512]{2,1,0:T(8,128)S(1)} collective-permute-done((f32[11,32,512]{2,1,0:T(8,128)}, f32[11,32,512]{2,1,0:T(8,128)S(1)}, u32[]{:S(2)}, u32[]{:S(2)}) %collective-permute-start) | collective-permute-done | bytes 720928 | tf_op jit(solution)/shard_map/ppermute | solution.py:25
  50.3 1.3 collective-permute-start.4
  51.7 3.0 %collective-permute-start.5 = (f32[22,4,512]{2,1,0:T(4,128)S(1)}, f32[22,4,512]{2,1,0:T(4,128)S(1)}, u32[]{:S(2)}, u32[]{:S(2)}) collective-permute-start(f32[22,4,512]{2,1,0:T(4,128)S(1)} %pad_maximum_fusion.5), channel_id=1, source_target_pairs={{0,1},{1,2},{2,3},{3,4},{4,5},{5,6},{6,7},{7,8},{8,9},{9,10},{10,1... | collective-permute-start | bytes 540680 | tf_op jit(solution)/shard_map/ppermute | solution.py:25
  56.6 0.7 copy-done.6
  57.2 41.5 %stencil.1 = (f32[32,32,512]{2,1,0:T(8,128)}, f32[32,32,512]{2,1,0:T(8,128)}) custom-call(s32[4]{0:T(128)} %pad_add_fusion.place, f32[32,32,512]{2,1,0:T(8,128)} %u_hbm.1, f32[32,32,512]{2,1,0:T(8,128)} %d_hbm.1, f32[32,32,512]{2,1,0:T(8,128)} %r_hbm.1, f32[11,32,512]{2,1,0:T(8,128)} %copy-done.2, f32[11,32,512]{2,1,0:T(8,128)} %copy-done.1, ...), custom_call_target="tpu_custom_call" | custom-call | tf_op jit(solution)/shard_map/stencil/pallas_call | solution.py:202
  98.8 58.1 %render.1 = f32[16,32,512]{2,1,0:T(8,128)} custom-call(s32[4,32]{1,0:T(4,128)} %constant_dynamic-slice_fusion.offs, f32[8]{0:T(128)} %get-tuple-element.33.cen, f32[8]{0:T(128)} %get-tuple-element.28.lev, f32[3,8]{1,0:T(4,128)} %broadcast_divide_fusion.mix, f32[32,32,512]{2,1,0:T(8,128)} %get-tuple-element.8.ft, f32[4,1,512]{2,1,0:T(1,128)} %broadcast_in_dim.14.sign_ref), custom_call_target="tpu_custom_call" | custom-call | tf_op jit(solution)/shard_map/render/pallas_call | solution.py:287
  156.9 25.9 %all_to_all.5.parts = f32[16,32,512]{2,1,0:T(8,128)} all-to-all(f32[16,32,512]{2,1,0:T(8,128)} %render.1), channel_id=1, replica_groups=mesh['sx'=8,'sy'=16] {'sy'}, dimensions={0} | all-to-all | bytes 2097152 | tf_op jit(solution)/shard_map/all_to_all | solution.py:362
  182.8 2.2 %combine.1 = (f32[4,3,2,512]{3,2,1,0:T(2,128)}, f32[4,2,512]{2,1,0:T(2,128)}) custom-call(f32[16,32,512]{2,1,0:T(8,128)} %all_to_all.5.parts, f32[4,1,512]{2,1,0:T(1,128)} %broadcast_in_dim.14.sign_ref), custom_call_target="tpu_custom_call" | custom-call | tf_op jit(solution)/shard_map/combine/pallas_call | solution.py:326
  (32 shorter events, 2.5 us)
Async XLA Ops:
  0.6 23.0 %copy-start = (s32[4,512]{1,0:T(4,128)S(1)}, s32[4,512]{1,0:T(4,128)}, u32[]{:S(2)}) copy-start(s32[4,512]{1,0:T(4,128)} %param.11) | copy-start | bytes 24580
  3.9 22.2 %collective-permute-start.1 = (f32[11,32,512]{2,1,0:T(8,128)}, f32[11,32,512]{2,1,0:T(8,128)S(1)}, u32[]{:S(2)}, u32[]{:S(2)}) collective-permute-start(f32[11,32,512]{2,1,0:T(8,128)} %pad_maximum_fusion.3), channel_id=1, source_target_pairs={{16,0},{32,16},{48,32},{64,48},{80,64},{96,80},{112,96},{17,1},{33... | collective-permute-start | bytes 2162696 | tf_op jit(solution)/shard_map/ppermute | solution.py:25
  6.1 44.1 %collective-permute-start = (f32[11,32,512]{2,1,0:T(8,128)}, f32[11,32,512]{2,1,0:T(8,128)S(1)}, u32[]{:S(2)}, u32[]{:S(2)}) collective-permute-start(f32[11,32,512]{2,1,0:T(8,128)} %pad_maximum_fusion.2), channel_id=1, source_target_pairs={{0,16},{16,32},{32,48},{48,64},{64,80},{80,96},{96,112},{1,17},{17... | collective-permute-start | bytes 2162696 | tf_op jit(solution)/shard_map/ppermute | solution.py:25
  14.5 7.9 %copy-start.7 = (s32[4,512]{1,0:T(4,128)S(1)}, s32[4,512]{1,0:T(4,128)}, u32[]{:S(2)}) copy-start(s32[4,512]{1,0:T(4,128)} %param.12) | copy-start | bytes 24580
  14.5 9.8 %copy-start.9 = (f32[8]{0:T(128)S(1)}, f32[8]{0:T(128)}, u32[]{:S(2)}) copy-start(f32[8]{0:T(128)} %param.15) | copy-start | bytes 100
  14.5 9.8 %copy-start.10 = (f32[8]{0:T(128)S(1)}, f32[8]{0:T(128)}, u32[]{:S(2)}) copy-start(f32[8]{0:T(128)} %param.13) | copy-start | bytes 100
  15.9 38.9 %copy-start.8 = (f32[3,8]{1,0:T(4,128)S(1)}, f32[3,8]{1,0:T(4,128)}, u32[]{:S(2)}) copy-start(f32[3,8]{1,0:T(4,128)} %param.14) | copy-start | bytes 292
  16.9 38.4 %collective-permute-start.2 = (f32[3,32,4,512]{3,2,1,0:T(4,128)}, f32[3,32,4,512]{3,2,1,0:T(4,128)S(1)}, u32[]{:S(2)}, u32[]{:S(2)}) collective-permute-start(f32[3,32,4,512]{3,2,1,0:T(4,128)} %pad_maximum_fusion), channel_id=1, source_target_pairs={{1,0},{2,1},{3,2},{4,3},{5,4},{6,5},{7,6},{8,7},{9,8},{10,9},{11,1... | collective-permute-start | bytes 2359304 | tf_op jit(solution)/shard_map/ppermute | solution.py:25
  19.3 36.1 %collective-permute-start.3 = (f32[3,32,4,512]{3,2,1,0:T(4,128)}, f32[3,32,4,512]{3,2,1,0:T(4,128)S(1)}, u32[]{:S(2)}, u32[]{:S(2)}) collective-permute-start(f32[3,32,4,512]{3,2,1,0:T(4,128)} %pad_maximum_fusion.1), channel_id=1, source_target_pairs={{0,1},{1,2},{2,3},{3,4},{4,5},{5,6},{6,7},{7,8},{8,9},{9,10},{10,1... | collective-permute-start | bytes 2359304 | tf_op jit(solution)/shard_map/ppermute | solution.py:25
  26.1 29.6 %copy-start.1 = (f32[11,32,512]{2,1,0:T(8,128)}, f32[11,32,512]{2,1,0:T(8,128)S(1)}, u32[]{:S(2)}) copy-start(f32[11,32,512]{2,1,0:T(8,128)S(1)} %collective-permute-done.1.xp_hbm) | copy-start | bytes 2162692
  50.3 5.5 %copy-start.2 = (f32[11,32,512]{2,1,0:T(8,128)}, f32[11,32,512]{2,1,0:T(8,128)S(1)}, u32[]{:S(2)}) copy-start(f32[11,32,512]{2,1,0:T(8,128)S(1)} %collective-permute-done.xm_hbm) | copy-start | bytes 2162692
  50.3 5.0 %collective-permute-start.4 = (f32[22,4,512]{2,1,0:T(4,128)S(1)}, f32[22,4,512]{2,1,0:T(4,128)S(1)}, u32[]{:S(2)}, u32[]{:S(2)}) collective-permute-start(f32[22,4,512]{2,1,0:T(4,128)S(1)} %pad_maximum_fusion.4), channel_id=1, source_target_pairs={{1,0},{2,1},{3,2},{4,3},{5,4},{6,5},{7,6},{8,7},{9,8},{10,9},{11,1... | collective-permute-start | bytes 540680 | tf_op jit(solution)/shard_map/ppermute | solution.py:25
  51.7 4.1 %collective-permute-start.5 = (f32[22,4,512]{2,1,0:T(4,128)S(1)}, f32[22,4,512]{2,1,0:T(4,128)S(1)}, u32[]{:S(2)}, u32[]{:S(2)}) collective-permute-start(f32[22,4,512]{2,1,0:T(4,128)S(1)} %pad_maximum_fusion.5), channel_id=1, source_target_pairs={{0,1},{1,2},{2,3},{3,4},{4,5},{5,6},{6,7},{7,8},{8,9},{9,10},{10,1... | collective-permute-start | bytes 540680 | tf_op jit(solution)/shard_map/ppermute | solution.py:25
  55.3 0.9 copy-start.3
  55.4 1.1 copy-start.4
  55.4 1.2 copy-start.5
  56.6 0.7 copy-start.6

commit v2 on v1

--- a/solution.py
+++ b/solution.py
@@ -10,6 +10,7 @@
 STEPS = 4
 VIEWS = 4
 BUMPS = 8
+MAXSHIFT = 8
 W = STEPS
 LOG2E = 1.4426950408889634
 GAIN = 2.0 * LOG2E**0.5
@@ -28,7 +29,7 @@
 def stencil_kernel(
     place, u_hbm, d_hbm, r_hbm, xm_hbm, xp_hbm, yn, yp, cn, cp,
     out_hbm, ft_hbm,
-    ua, ub, dd, rr, kbuf, fbuf, ft, sems, osem,
+    ua, ub, dd, rr, kk, fbuf, ft, sems, osem,
 ):
     cx, cy, nz = u_hbm.shape
     blocks = nz // 128
@@ -70,9 +71,9 @@
             plane = base + i + (1 if side == 0 else 0)
             rr[plane, cy : cy + W, :] = cn[at]
             rr[plane, cy + W : cy + 2 * W, :] = cp[at]
-    for i in range(W):
-        ub[i] = jnp.zeros((cy + 8, nz), F32)
-        ub[W + cx + i] = jnp.zeros((cy + 8, nz), F32)
+    rr[0] = jnp.zeros((cy + 8, nz), F32)
+    rr[2 * W + cx - 1] = jnp.zeros((cy + 8, nz), F32)
+    zero = jnp.zeros((8, 128), F32)
 
     sub = lax.broadcasted_iota(jnp.int32, (8, 128), 0)
     lane = lax.broadcasted_iota(jnp.int32, (8, 128), 1)
@@ -86,30 +87,29 @@
     def cut(tile, block):
         return (slice(8 * tile, 8 * tile + 8), slice(128 * block, 128 * block + 128))
 
-    def conductance(src, plane):
-        slot = lax.rem(plane, 2)
+    def local_part(src, dst, plane):
         for t in range(tiles):
-            for b in range(blocks):
-                at = cut(t, b)
-                kbuf[(slot,) + at] = dd[(plane,) + at] * (
-                    0.5 + 0.2 * jnp.tanh(src[(plane,) + at])
-                )
-
-    def face(src, plane):
-        slot = lax.rem(plane, 2)
-        for t in range(tiles):
-            for b in range(blocks):
-                at = cut(t, b)
-                fbuf[at] = (kbuf[(slot,) + at] + kbuf[(1 - slot,) + at]) * (
-                    src[(plane,) + at] - src[(plane - 1,) + at]
-                )
-
-    def advance(src, dst, last, plane):
-        conductance(src, plane + 1)
-        slot = lax.rem(plane, 2)
+            u = [src[(plane,) + cut(t, b)] for b in range(blocks)]
+            warm = [jnp.tanh(v) for v in u]
+            k = [dd[(plane,) + cut(t, b)] * (0.5 + 0.2 * warm[b]) for b in range(blocks)]
+            u_up = [pltpu.roll(v, 127, 1) for v in u] + [zero]
+            k_up = [pltpu.roll(v, 127, 1) for v in k] + [zero]
+            flux = []
+            for b in range(blocks):
+                un = jnp.where(lane_last, u_up[b + 1], u_up[b])
+                kn = jnp.where(lane_last, k_up[b + 1], k_up[b])
+                flux.append((k[b] + kn) * (un - u[b]))
+            down = [pltpu.roll(v, 1, 1) for v in flux]
+            for b in range(blocks):
+                at = (plane,) + cut(t, b)
+                low = jnp.where(lane_first, k[b] * u[b] if b == 0 else down[b - 1], down[b])
+                kk[at] = k[b]
+                dst[at] = u[b] + ((flux[b] - low) + rr[at] * warm[b])
+
+    def across(src, base, dst, last, plane):
         for b in range(blocks):
             u = [src[(plane,) + cut(t, b)] for t in range(tiles)]
-            k = [kbuf[(slot,) + cut(t, b)] for t in range(tiles)]
+            k = [kk[(plane,) + cut(t, b)] for t in range(tiles)]
             u_up = [pltpu.roll(v, 7, 0) for v in u]
             k_up = [pltpu.roll(v, 7, 0) for v in k]
             flux = []
@@ -122,57 +122,40 @@
             for t in range(tiles - 1 if last else tiles):
                 at = cut(t, b)
                 change = flux[t] - jnp.where(sub_first, down[t - 1], down[t])
-                ux = src[(plane + 1,) + at]
-                kx = kbuf[(1 - slot,) + at]
-                fx = (k[t] + kx) * (ux - u[t])
-                change = change + (fx - fbuf[at])
+                fx = (k[t] + kk[(plane + 1,) + at]) * (src[(plane + 1,) + at] - u[t])
+                new = base[(plane,) + at] + (change + (fx - fbuf[at]))
                 fbuf[at] = fx
-
-                def z_face(low):
-                    ul = src[(plane,) + cut(t, low)] if low != b else u[t]
-                    kl = kbuf[(slot,) + cut(t, low)] if low != b else k[t]
-                    un, kn = pltpu.roll(ul, 127, 1), pltpu.roll(kl, 127, 1)
-                    if low + 1 < blocks:
-                        u2 = pltpu.roll(src[(plane,) + cut(t, low + 1)], 127, 1)
-                        k2 = pltpu.roll(kbuf[(slot,) + cut(t, low + 1)], 127, 1)
-                    else:
-                        u2 = k2 = jnp.zeros((8, 128), F32)
-                    un, kn = jnp.where(lane_last, u2, un), jnp.where(lane_last, k2, kn)
-                    return (kl + kn) * (un - ul)
-
-                fz = z_face(b)
-                rolled = pltpu.roll(fz, 1, 1)
-                if b == 0:
-                    carry = k[t] * u[t]
-                else:
-                    ul, kl = src[(plane,) + cut(t, b - 1)], kbuf[(slot,) + cut(t, b - 1)]
-                    carry = (k[t] + pltpu.roll(kl, 1, 1)) * (u[t] - pltpu.roll(ul, 1, 1))
-                change = change + (fz - jnp.where(lane_first, carry, rolled))
-                new = u[t] + (change + rr[(plane,) + at] * jnp.tanh(u[t]))
                 if t == tiles - 1:
                     new = new * inside
-                if last:
-                    dst[(plane - W,) + at] = new
-                else:
-                    dst[(plane,) + at] = new
+                dst[(plane - W if last else plane,) + at] = new
+
+    def loop(low, count, fn):
+        lax.fori_loop(0, count // 2, lambda i, c: (fn(low + 2 * i), fn(low + 2 * i + 1), c)[2], 0)
 
     src, dst = ua, ub
     for step in range(STEPS):
         last = step == STEPS - 1
-        low = jnp.where(sx == 0, W, step + 1)
-        high = jnp.where(sx == last_x, W + cx, 2 * W + cx - 1 - step)
-        if last:
-            low, high = W, W + cx
-        conductance(src, low - 1)
-        conductance(src, low)
-        face(src, low)
-
-        def body(plane, carry, src=src, dst=ft if last else dst, last=last):
-            advance(src, dst, last, plane)
-            return carry
-
-        lax.fori_loop(low, high, body, 0)
+        low, count = step + 1, cx + 2 * (W - 1 - step)
+        loop(low - 1, count + 2, functools.partial(local_part, src, dst))
+        for t in range(tiles):
+            for b in range(blocks):
+                at = cut(t, b)
+                fbuf[at] = (kk[(low - 1,) + at] + kk[(low,) + at]) * (
+                    src[(low,) + at] - src[(low - 1,) + at]
+                )
+        loop(low, count, functools.partial(across, src, dst, ft if last else dst, last))
         if not last:
+
+            @pl.when(sx == 0)
+            def _(dst=dst):
+                for i in range(1, W):
+                    dst[i] = jnp.zeros((cy + 8, nz), F32)
+
+            @pl.when(sx == last_x)
+            def _(dst=dst):
+                for i in range(W - 1):
+                    dst[W + cx + i] = jnp.zeros((cy + 8, nz), F32)
+
             src, dst = dst, src
     done = pltpu.make_async_copy(ft, out_hbm, osem.at[0])
     done.start()
@@ -184,7 +167,7 @@
                 piece = ft[pl.ds(8 * xg, 8), 8 * yg : 8 * yg + 8, 128 * b : 128 * b + 128]
                 turned[
                     8 * yg : 8 * yg + 8, pl.ds(pl.multiple_of(8 * xg, 8), 8), 128 * b : 128 * b + 128
-                ] = jnp.transpose(piece, (1, 0, 2))
+                ] = jnp.transpose(piece, (1, 0, 2)) * GAIN
         return carry
 
     lax.fori_loop(0, cx // 8, turn, 0)
@@ -212,7 +195,7 @@
             pltpu.VMEM(wide, F32),
             pltpu.VMEM(wide, F32),
             pltpu.VMEM(wide, F32),
-            pltpu.VMEM((2, cy + 8, nz), F32),
+            pltpu.VMEM(wide, F32),
             pltpu.VMEM((cy + 8, nz), F32),
             pltpu.VMEM((cx, cy, nz), F32),
             pltpu.SemaphoreType.DMA((9,)),
@@ -222,32 +205,28 @@
     )(place, u, d, r, xm, xp, yn, yp, cn, cp)
 
 
-def render_kernel(offs, cen, lev, mix, ft, sign_ref, out, sheared):
+def render_kernel(whole, part, cen, lev, mix, ft, sign_ref, out, moved):
     view = pl.program_id(1)
     depth, rows, nz = ft.shape
     blocks = nz // 128
-    lane = lax.broadcasted_iota(jnp.int32, (rows, 128), 1)
-    lane_last = lane == 127
     zero = jnp.zeros((rows, 128), F32)
 
-    def shear(y, carry):
-        q = offs[view, y]
-        whole = q // 4
-        part = (q - 4 * whole).astype(F32) * 0.25
-        cells = [ft[y, :, 128 * b : 128 * b + 128] for b in range(blocks)]
-        back = [pltpu.roll(c, 127, 1) for c in cells] + [zero]
-        mixed = []
-        for b in range(blocks):
-            after = jnp.where(lane_last, back[b + 1], back[b])
-            mixed.append((cells[b] + part * (after - cells[b])) * GAIN)
-        amount = lax.rem(128 - whole, 128)
-        moved = [pltpu.roll(c, amount, 1) for c in mixed] + [zero]
-        keep = lane < 128 - whole
-        for b in range(blocks):
-            sheared[y, :, 128 * b : 128 * b + 128] = jnp.where(keep, moved[b], moved[b + 1])
-        return carry
-
-    lax.fori_loop(0, depth, shear, 0, unroll=2)
+    @pl.when(view == 0)
+    def _():
+        lane = lax.broadcasted_iota(jnp.int32, (rows, 128), 1)
+
+        def shifts(y, carry):
+            cells = [ft[y, :, 128 * b : 128 * b + 128] for b in range(blocks)]
+            for b in range(blocks):
+                moved[y, 0, :, 128 * b : 128 * b + 128] = cells[b]
+            for n in range(1, MAXSHIFT + 1):
+                back = [pltpu.roll(c, 128 - n, 1) for c in cells] + [zero]
+                keep = lane < 128 - n
+                for b in range(blocks):
+                    moved[y, n, :, 128 * b : 128 * b + 128] = jnp.where(keep, back[b], back[b + 1])
+            return carry
+
+        lax.fori_loop(0, depth, shifts, 0, unroll=2)
 
     for b in range(blocks):
         at = slice(128 * b, 128 * b + 128)
@@ -256,7 +235,9 @@
         light = jnp.ones((rows, 128), F32)
         sums = [zero] * BUMPS
         for y in range(depth):
-            s = sheared[y, :, at]
+            n = whole[view, y]
+            near = moved[y, n, :, at]
+            s = near + part[view, y] * (moved[y, n + 1, :, at] - near)
             bumps = []
             for i in range(BUMPS):
                 t = s - cen[i]
@@ -281,7 +262,7 @@
             out[d, :, at] = jnp.concatenate([c[2 * d : 2 * d + 2] for c in channels], axis=0)
 
 
-def render(offs, cen, lev, mix, ft, signs):
+def render(whole, part, cen, lev, mix, ft, signs):
     cy, cx, nz = ft.shape
     smem = pl.BlockSpec(memory_space=pltpu.SMEM)
     return pl.pallas_call(
@@ -293,13 +274,14 @@
             smem,
             smem,
             smem,
+            smem,
             pl.BlockSpec((cy, 8, nz), lambda i, v: (0, i, 0)),
             pl.BlockSpec((1, 1, nz), lambda i, v: (v, 0, 0)),
         ],
         out_specs=pl.BlockSpec((4, 8, nz), lambda i, v: (i, v, 0)),
-        scratch_shapes=[pltpu.VMEM((cy, 8, nz), F32)],
+        scratch_shapes=[pltpu.VMEM((cy, MAXSHIFT + 1, 8, nz), F32)],
         name="render",
-    )(offs, cen, lev, mix, ft, signs)
+    )(whole, part, cen, lev, mix, ft, signs)
 
 
 def combine_kernel(parts, sign_ref, image, trans):
@@ -358,7 +340,9 @@
     offs = lax.dynamic_slice_in_dim(offsets, lax.axis_index("sy") * cy, cy, 1)
     signs = jnp.where(depth_order == 0, -1.0, 1.0).astype(F32)[:, None, :]
     level = opacity * LOG2E
-    parts = render(offs, centres * GAIN, jnp.log2(level), colour / level, turned, signs)
+    whole = offs // 4
+    part = (offs % 4).astype(F32) * 0.25
+    parts = render(whole, part, centres * GAIN, jnp.log2(level), colour / level, turned, signs)
     parts = lax.all_to_all(parts, "sy", split_axis=0, concat_axis=0, tiled=True)
     image, trans = combine(parts, signs)
     return field, image, trans

time: 188 us -> 149 us (0.79); the launches traced: 185 us -> 148 us
  Pallas kernels: 102 us -> 64.8 us
    pallas_call x1, Pallas kernels: 58.1 us -> 29.6 us  [render(): pl.pallas_call(render_kernel, out_shape=jax.ShapeDtypeStruct((cx // 2, 8...]
    pallas_call x1, Pallas kernels: 41.5 us -> 33 us  [stencil(): pl.pallas_call(stencil_kernel, out_shape=(jax.ShapeDtypeStruct((cx, cy, n...]
  transfers between devices with their start and end apart: 6 -> 6, of which waited for: 3 -> 3; matrix products, arithmetic and copies ran while one was open for 5% -> 7% of each run, Pallas kernels for 0% -> 0%
where the time goes in v2:
time: 149 us; the launch traced here: 148 us
  Pallas kernels  64.8 us (43%)
  blocking collectives  25.9 us (17%)
  waiting for transfers between devices  25.1 us (17%)
  starting transfers between devices  16.5 us (11%)
  local copies, waits for them, and re-layouts  7.63 us (5%)
  other arithmetic  7.18 us (5%)
    pallas_call x1, Pallas kernels, stencil(): pl.pallas_call(stencil_kernel, out_shape=(jax.ShapeDtypeStruct((cx, cy, n...  33 us
    pallas_call x1, Pallas kernels, render(): pl.pallas_call(render_kernel, out_shape=jax.ShapeDtypeStruct((cx // 2, 8...  29.6 us
    all_to_all x1, blocking collectives, per_device(): parts = lax.all_to_all(parts, 'sy', split_axis=0, concat_axis=0, tiled=True)  25.9 us
    ppermute x6, waiting for transfers between devices, shift(): return lax.ppermute(value, axis, pairs)  25.1 us
    ppermute x6, starting transfers between devices, shift(): return lax.ppermute(value, axis, pairs)  16.5 us
    another operation x2, local copies, waits for them, and re-layouts, per_device(): up_y = jnp.stack([a[:, cy - W:] for a in (u, d, r)])  3.1 us
  transfers between devices with their start and end apart: 6, of which 3 were waited for; matrix products, arithmetic and copies ran while one was open for 7% of the time, Pallas kernels for 0%

profile of v2, /device:TPU:0, one launch (start us, length us, event | category | flops | bytes accessed | tf_op | source)
XLA Modules:
  0.0 148.0 jit_solution(2342039304610531864)
XLA Ops:
  0.6 1.1 fusion.5
  1.7 1.3 fusion.3
  3.0 0.9 pad_maximum_fusion.3
  3.9 1.3 collective-permute-start.1
  5.2 0.9 pad_maximum_fusion.2
  6.1 6.6 %collective-permute-start = (f32[11,32,512]{2,1,0:T(8,128)}, f32[11,32,512]{2,1,0:T(8,128)S(1)}, u32[]{:S(2)}, u32[]{:S(2)}) collective-permute-start(f32[11,32,512]{2,1,0:T(8,128)} %pad_maximum_fusion.2), channel_id=1, source_target_pairs={{0,16},{16,32},{32,48},{48,64},{64,80},{80,96},{96,112},{1,17},{17... | collective-permute-start | bytes 2162696 | tf_op jit(solution)/shard_map/ppermute | solution.py:26
  12.7 1.8 %slice_bitcast_fusion = (f32[1,32,4,512]{3,2,1,0:T(4,128)S(1)}, f32[1,32,4,512]{3,2,1,0:T(4,128)S(1)}, f32[1,32,4,512]{3,2,1,0:T(4,128)S(1)}, f32[1,32,4,512]{3,2,1,0:T(4,128)S(1)}) fusion(f32[32,32,512]{2,1,0:T(8,128)} %r_hbm.1, f32[32,32,512]{2,1,0:T(8,128)} %d_hbm.1), kind=kLoop, calls=%fused_computation.4 | loop fusion | bytes 2097152 | tf_op jit(solution)/shard_map/stack | solution.py:332
  14.5 1.3 slice_bitcast_fusion.2
  15.8 1.1 pad_maximum_fusion
  16.9 1.3 collective-permute-start.2
  18.2 1.1 pad_maximum_fusion.1
  19.3 3.1 %collective-permute-start.3 = (f32[3,32,4,512]{3,2,1,0:T(4,128)}, f32[3,32,4,512]{3,2,1,0:T(4,128)S(1)}, u32[]{:S(2)}, u32[]{:S(2)}) collective-permute-start(f32[3,32,4,512]{3,2,1,0:T(4,128)} %pad_maximum_fusion.1), channel_id=1, source_target_pairs={{0,1},{1,2},{2,3},{3,4},{4,5},{5,6},{6,7},{7,8},{8,9},{9,10},{10,1... | collective-permute-start | bytes 2359304 | tf_op jit(solution)/shard_map/ppermute | solution.py:26
  22.4 0.7 pad_add_fusion.place
  23.6 0.7 add_select_fusion.1.whole
  24.3 0.7 fusion.1.part
  25.5 0.6 collective-permute-done.1.xp_hbm
  26.1 24.1 %collective-permute-done.xm_hbm = f32[11,32,512]{2,1,0:T(8,128)S(1)} collective-permute-done((f32[11,32,512]{2,1,0:T(8,128)}, f32[11,32,512]{2,1,0:T(8,128)S(1)}, u32[]{:S(2)}, u32[]{:S(2)}) %collective-permute-start) | collective-permute-done | bytes 720928 | tf_op jit(solution)/shard_map/ppermute | solution.py:26
  50.3 1.3 collective-permute-start.4
  51.7 3.0 %collective-permute-start.5 = (f32[22,4,512]{2,1,0:T(4,128)S(1)}, f32[22,4,512]{2,1,0:T(4,128)S(1)}, u32[]{:S(2)}, u32[]{:S(2)}) collective-permute-start(f32[22,4,512]{2,1,0:T(4,128)S(1)} %pad_maximum_fusion.5), channel_id=1, source_target_pairs={{0,1},{1,2},{2,3},{3,4},{4,5},{5,6},{6,7},{7,8},{8,9},{9,10},{10,1... | collective-permute-start | bytes 540680 | tf_op jit(solution)/shard_map/ppermute | solution.py:26
  56.6 0.7 copy-done.5
  57.2 33.0 %stencil.1 = (f32[32,32,512]{2,1,0:T(8,128)}, f32[32,32,512]{2,1,0:T(8,128)}) custom-call(s32[4]{0:T(128)} %pad_add_fusion.place, f32[32,32,512]{2,1,0:T(8,128)} %u_hbm.1, f32[32,32,512]{2,1,0:T(8,128)} %d_hbm.1, f32[32,32,512]{2,1,0:T(8,128)} %r_hbm.1, f32[11,32,512]{2,1,0:T(8,128)} %copy-done.1, f32[11,32,512]{2,1,0:T(8,128)} %copy-done, ...), custom_call_target="tpu_custom_call" | custom-call | tf_op jit(solution)/shard_map/stencil/pallas_call | solution.py:185
  90.2 29.6 %render.1 = f32[16,32,512]{2,1,0:T(8,128)} custom-call(s32[4,32]{1,0:T(4,128)} %add_select_fusion.1.whole, f32[4,32]{1,0:T(4,128)} %fusion.1.part, f32[8]{0:T(128)} %get-tuple-element.33.cen, f32[8]{0:T(128)} %get-tuple-element.28.lev, f32[3,8]{1,0:T(4,128)} %broadcast_divide_fusion.mix, f32[32,32,512]{2,1,0:T(8,128)} %get-tuple-element.8.ft, ...), custom_call_target="tpu_custom_call" | custom-call | tf_op jit(solution)/shard_map/render/pallas_call | solution.py:268
  119.8 25.9 %all_to_all.5.parts = f32[16,32,512]{2,1,0:T(8,128)} all-to-all(f32[16,32,512]{2,1,0:T(8,128)} %render.1), channel_id=1, replica_groups=mesh['sx'=8,'sy'=16] {'sy'}, dimensions={0} | all-to-all | bytes 2097152 | tf_op jit(solution)/shard_map/all_to_all | solution.py:346
  145.8 2.2 %combine.1 = (f32[4,3,2,512]{3,2,1,0:T(2,128)}, f32[4,2,512]{2,1,0:T(2,128)}) custom-call(f32[16,32,512]{2,1,0:T(8,128)} %all_to_all.5.parts, f32[4,1,512]{2,1,0:T(1,128)} %broadcast_in_dim.14.sign_ref), custom_call_target="tpu_custom_call" | custom-call | tf_op jit(solution)/shard_map/combine/pallas_call | solution.py:308
  (33 shorter events, 3.1 us)
Async XLA Ops:
  3.9 22.2 %collective-permute-start.1 = (f32[11,32,512]{2,1,0:T(8,128)}, f32[11,32,512]{2,1,0:T(8,128)S(1)}, u32[]{:S(2)}, u32[]{:S(2)}) collective-permute-start(f32[11,32,512]{2,1,0:T(8,128)} %pad_maximum_fusion.3), channel_id=1, source_target_pairs={{16,0},{32,16},{48,32},{64,48},{80,64},{96,80},{112,96},{17,1},{33... | collective-permute-start | bytes 2162696 | tf_op jit(solution)/shard_map/ppermute | solution.py:26
  6.1 44.1 %collective-permute-start = (f32[11,32,512]{2,1,0:T(8,128)}, f32[11,32,512]{2,1,0:T(8,128)S(1)}, u32[]{:S(2)}, u32[]{:S(2)}) collective-permute-start(f32[11,32,512]{2,1,0:T(8,128)} %pad_maximum_fusion.2), channel_id=1, source_target_pairs={{0,16},{16,32},{32,48},{48,64},{64,80},{80,96},{96,112},{1,17},{17... | collective-permute-start | bytes 2162696 | tf_op jit(solution)/shard_map/ppermute | solution.py:26
  14.4 7.9 %copy-start.6 = (s32[4,512]{1,0:T(4,128)S(1)}, s32[4,512]{1,0:T(4,128)}, u32[]{:S(2)}) copy-start(s32[4,512]{1,0:T(4,128)} %param.12) | copy-start | bytes 24580
  14.5 9.2 %copy-start.7 = (s32[4,512]{1,0:T(4,128)S(1)}, s32[4,512]{1,0:T(4,128)}, u32[]{:S(2)}) copy-start(s32[4,512]{1,0:T(4,128)} %param.11) | copy-start | bytes 24580
  14.5 10.5 %copy-start.9 = (f32[8]{0:T(128)S(1)}, f32[8]{0:T(128)}, u32[]{:S(2)}) copy-start(f32[8]{0:T(128)} %param.15) | copy-start | bytes 100
  14.5 10.5 %copy-start.10 = (f32[8]{0:T(128)S(1)}, f32[8]{0:T(128)}, u32[]{:S(2)}) copy-start(f32[8]{0:T(128)} %param.13) | copy-start | bytes 100
  15.8 38.9 %copy-start.8 = (f32[3,8]{1,0:T(4,128)S(1)}, f32[3,8]{1,0:T(4,128)}, u32[]{:S(2)}) copy-start(f32[3,8]{1,0:T(4,128)} %param.14) | copy-start | bytes 292
  16.9 38.4 %collective-permute-start.2 = (f32[3,32,4,512]{3,2,1,0:T(4,128)}, f32[3,32,4,512]{3,2,1,0:T(4,128)S(1)}, u32[]{:S(2)}, u32[]{:S(2)}) collective-permute-start(f32[3,32,4,512]{3,2,1,0:T(4,128)} %pad_maximum_fusion), channel_id=1, source_target_pairs={{1,0},{2,1},{3,2},{4,3},{5,4},{6,5},{7,6},{8,7},{9,8},{10,9},{11,1... | collective-permute-start | bytes 2359304 | tf_op jit(solution)/shard_map/ppermute | solution.py:26
  19.3 36.1 %collective-permute-start.3 = (f32[3,32,4,512]{3,2,1,0:T(4,128)}, f32[3,32,4,512]{3,2,1,0:T(4,128)S(1)}, u32[]{:S(2)}, u32[]{:S(2)}) collective-permute-start(f32[3,32,4,512]{3,2,1,0:T(4,128)} %pad_maximum_fusion.1), channel_id=1, source_target_pairs={{0,1},{1,2},{2,3},{3,4},{4,5},{5,6},{6,7},{7,8},{8,9},{9,10},{10,1... | collective-permute-start | bytes 2359304 | tf_op jit(solution)/shard_map/ppermute | solution.py:26
  26.1 29.6 %copy-start = (f32[11,32,512]{2,1,0:T(8,128)}, f32[11,32,512]{2,1,0:T(8,128)S(1)}, u32[]{:S(2)}) copy-start(f32[11,32,512]{2,1,0:T(8,128)S(1)} %collective-permute-done.1.xp_hbm) | copy-start | bytes 2162692
  50.2 5.5 %copy-start.1 = (f32[11,32,512]{2,1,0:T(8,128)}, f32[11,32,512]{2,1,0:T(8,128)S(1)}, u32[]{:S(2)}) copy-start(f32[11,32,512]{2,1,0:T(8,128)S(1)} %collective-permute-done.xm_hbm) | copy-start | bytes 2162692
  50.3 5.0 %collective-permute-start.4 = (f32[22,4,512]{2,1,0:T(4,128)S(1)}, f32[22,4,512]{2,1,0:T(4,128)S(1)}, u32[]{:S(2)}, u32[]{:S(2)}) collective-permute-start(f32[22,4,512]{2,1,0:T(4,128)S(1)} %pad_maximum_fusion.4), channel_id=1, source_target_pairs={{1,0},{2,1},{3,2},{4,3},{5,4},{6,5},{7,6},{8,7},{9,8},{10,9},{11,1... | collective-permute-start | bytes 540680 | tf_op jit(solution)/shard_map/ppermute | solution.py:26
  51.7 4.1 %collective-permute-start.5 = (f32[22,4,512]{2,1,0:T(4,128)S(1)}, f32[22,4,512]{2,1,0:T(4,128)S(1)}, u32[]{:S(2)}, u32[]{:S(2)}) collective-permute-start(f32[22,4,512]{2,1,0:T(4,128)S(1)} %pad_maximum_fusion.5), channel_id=1, source_target_pairs={{0,1},{1,2},{2,3},{3,4},{4,5},{5,6},{6,7},{7,8},{8,9},{9,10},{10,1... | collective-permute-start | bytes 540680 | tf_op jit(solution)/shard_map/ppermute | solution.py:26
  55.3 0.9 copy-start.2
  55.3 1.1 copy-start.3
  55.4 1.2 copy-start.4
  56.6 0.7 copy-start.5

commit v3 on v2

v3 whole, which is shorter than its diff:
```python
import jax
import jax.numpy as jnp
from jax import lax
from jax.experimental import pallas as pl
from jax.experimental.pallas import tpu as pltpu
from jax.sharding import PartitionSpec as P


STEPS = 4
VIEWS = 4
BUMPS = 8
MAXSHIFT = 8
W = STEPS
LOG2E = 1.4426950408889634
GAIN = 2.0 * LOG2E**0.5

F32 = jnp.float32


def shift(value, axis, up):
    size = lax.axis_size(axis)
    pairs = [(i, i + 1) for i in range(size - 1)]
    if not up:
        pairs = [(j, i) for i, j in pairs]
    return lax.ppermute(value, axis, pairs)


def cut(tile, block):
    return (slice(8 * tile, 8 * tile + 8), slice(128 * block, 128 * block + 128))


class Plane:
    def __init__(self, dd, rr, kk, fbuf, place):
        self.dd, self.rr, self.kk, self.fbuf = dd, rr, kk, fbuf
        self.tiles, self.blocks = dd.shape[1] // 8, dd.shape[2] // 128
        sub = lax.broadcasted_iota(jnp.int32, (8, 128), 0)
        lane = lax.broadcasted_iota(jnp.int32, (8, 128), 1)
        self.sub_last, self.sub_first = sub == 7, sub == 0
        self.lane_last, self.lane_first = lane == 127, lane == 0
        self.zero = jnp.zeros((8, 128), F32)
        self.inside = jnp.where(
            sub < W, (place[1] < place[3] - 1).astype(F32), (place[1] > 0).astype(F32)
        )

    def local(self, src, dst, plane):
        blocks = self.blocks
        for t in range(self.tiles):
            u = [src[(plane,) + cut(t, b)] for b in range(blocks)]
            warm = [jnp.tanh(v) for v in u]
            k = [self.dd[(plane,) + cut(t, b)] * (0.5 + 0.2 * warm[b]) for b in range(blocks)]
            u_up = [pltpu.roll(v, 127, 1) for v in u] + [self.zero]
            k_up = [pltpu.roll(v, 127, 1) for v in k] + [self.zero]
            flux = []
            for b in range(blocks):
                un = jnp.where(self.lane_last, u_up[b + 1], u_up[b])
                kn = jnp.where(self.lane_last, k_up[b + 1], k_up[b])
                flux.append((k[b] + kn) * (un - u[b]))
            down = [pltpu.roll(v, 1, 1) for v in flux]
            for b in range(blocks):
                at = (plane,) + cut(t, b)
                low = jnp.where(self.lane_first, k[b] * u[b] if b == 0 else down[b - 1], down[b])
                self.kk[at] = k[b]
                dst[at] = u[b] + ((flux[b] - low) + self.rr[at] * warm[b])

    def face(self, src, plane):
        for t in range(self.tiles):
            for b in range(self.blocks):
                at = cut(t, b)
                self.fbuf[at] = (self.kk[(plane - 1,) + at] + self.kk[(plane,) + at]) * (
                    src[(plane,) + at] - src[(plane - 1,) + at]
                )

    def across(self, src, base, dst, plane, target, keep=None):
        tiles, kk = self.tiles, self.kk
        for b in range(self.blocks):
            u = [src[(plane,) + cut(t, b)] for t in range(tiles)]
            k = [kk[(plane,) + cut(t, b)] for t in range(tiles)]
            u_up = [pltpu.roll(v, 7, 0) for v in u]
            k_up = [pltpu.roll(v, 7, 0) for v in k]
            flux = []
            for t in range(tiles):
                n = (t + 1) % tiles
                un = jnp.where(self.sub_last, u_up[n], u_up[t])
                kn = jnp.where(self.sub_last, k_up[n], k_up[t])
                flux.append((k[t] + kn) * (un - u[t]))
            down = [pltpu.roll(v, 1, 0) for v in flux]
            for t in range(min(tiles, dst.shape[1] // 8)):
                at = cut(t, b)
                change = flux[t] - jnp.where(self.sub_first, down[t - 1], down[t])
                fx = (k[t] + kk[(plane + 1,) + at]) * (src[(plane + 1,) + at] - u[t])
                new = base[(plane,) + at] + (change + (fx - self.fbuf[at]))
                self.fbuf[at] = fx
                if t == tiles - 1:
                    new = new * self.inside
                if keep is not None:
                    new = new * keep
                dst[(target,) + at] = new


def turn_over(field, turned):
    cx, cy, nz = field.shape[0], field.shape[1], field.shape[2]

    def group(xg, carry):
        rows = pl.ds(pl.multiple_of(8 * xg, 8), 8)
        for yg in range(cy // 8):
            for b in range(nz // 128):
                columns = slice(128 * b, 128 * b + 128)
                piece = field[rows, 8 * yg : 8 * yg + 8, columns]
                turned[8 * yg : 8 * yg + 8, rows, columns] = jnp.transpose(piece, (1, 0, 2)) * GAIN
        return carry

    lax.fori_loop(0, cx // 8, group, 0)


def inner_kernel(
    place, u_hbm, d_hbm, r_hbm, yn, yp,
    out_hbm, ft_hbm, rim,
    ua, ub, dd, rr, kk, fbuf, fin, turned, sems, osem,
):
    cx, cy, _ = u_hbm.shape
    copies = [
        pltpu.make_async_copy(src, dst.at[:, 0:cy], sems.at[i])
        for i, (src, dst) in enumerate(((u_hbm, ua), (d_hbm, dd), (r_hbm, rr)))
    ]
    for copy in copies:
        copy.start()

    def edge_rows(x, carry):
        for which, dst in enumerate((ua, dd, rr)):
            dst[x, cy : cy + W, :] = yn[which, x]
            dst[x, cy + W : cy + 2 * W, :] = yp[which, x]
        return carry

    lax.fori_loop(0, cx, edge_rows, 0)
    work = Plane(dd, rr, kk, fbuf, place)
    for copy in copies:
        copy.wait()

    src, dst = ua, ub
    for step in range(STEPS):
        last = step == STEPS - 1
        low, high = step + 1, cx - 1 - step
        for plane in range(3):
            work.local(src, dst, low - 1 + plane)
        work.face(src, low)

        def body(plane, carry, src=src, dst=dst, last=last, high=high):
            work.across(
                src, dst, fin if last else dst, plane, plane - W if last else plane
            )
            work.local(src, dst, jnp.minimum(plane + 2, high))
            return carry

        lax.fori_loop(low, high, body, 0)
        if not last:
            for i, plane in enumerate((low, low + 1, high - 2, high - 1)):
                rim[4 * step + i] = dst[plane]
            src, dst = dst, src
    done = pltpu.make_async_copy(fin, out_hbm.at[W : cx - W], osem.at[0])
    done.start()
    turn_over(fin.at[8 - W : cx - 8 - W], turned)
    move = pltpu.make_async_copy(turned, ft_hbm, osem.at[1])
    move.start()
    done.wait()
    move.wait()


ANYWHERE = pl.BlockSpec(memory_space=pl.ANY)
LOCAL = pl.BlockSpec(memory_space=pltpu.VMEM)
SCALARS = pl.BlockSpec(memory_space=pltpu.SMEM)


def inner(place, u, d, r, yn, yp):
    cx, cy, nz = u.shape
    wide = pltpu.VMEM((cx, cy + 8, nz), F32)
    return pl.pallas_call(
        inner_kernel,
        out_shape=(
            jax.ShapeDtypeStruct((cx, cy, nz), F32),
            jax.ShapeDtypeStruct((cy, cx - 16, nz), F32),
            jax.ShapeDtypeStruct((4 * (STEPS - 1), cy + 8, nz), F32),
        ),
        in_specs=[SCALARS] + [ANYWHERE] * 3 + [LOCAL] * 2,
        out_specs=(ANYWHERE, ANYWHERE, LOCAL),
        scratch_shapes=[wide] * 5
        + [
            pltpu.VMEM((cy + 8, nz), F32),
            pltpu.VMEM((cx - 2 * W, cy, nz), F32),
            pltpu.VMEM((cy, cx - 16, nz), F32),
            pltpu.SemaphoreType.DMA((3,)),
            pltpu.SemaphoreType.DMA((2,)),
        ],
        cost_estimate=pl.CostEstimate(
            flops=40 * STEPS * cx * cy * nz, bytes_accessed=24 * cx * cy * nz, transcendentals=0
        ),
        name="inner",
    )(place, u, d, r, yn, yp)


SPAN = 2 * W + 1


def outer_kernel(
    place, u_hbm, d_hbm, r_hbm, yn, yp, xm_hbm, xp_hbm, cn, cp, rim, field_hbm,
    out_hbm, ft_hbm,
    ua, ub, dd, rr, kk, fbuf, fin, turned, sems, osem,
):
    cx, cy, nz = u_hbm.shape
    own = slice(0, cy)
    copies = []
    for src, dst in (
        (xm_hbm.at[0:W], ua.at[0:W, own]),
        (u_hbm.at[0:2], ua.at[W : W + 2, own]),
        (u_hbm.at[cx - 2 : cx], ua.at[SPAN + W - 1 : SPAN + W + 1, own]),
        (xp_hbm.at[0:W], ua.at[SPAN + W + 1 : 2 * SPAN, own]),
        (xm_hbm.at[W : 2 * W], dd.at[0:W, own]),
        (d_hbm.at[0 : W + 1], dd.at[W:SPAN, own]),
        (d_hbm.at[cx - W - 1 : cx], dd.at[SPAN : SPAN + W + 1, own]),
        (xp_hbm.at[W : 2 * W], dd.at[SPAN + W + 1 : 2 * SPAN, own]),
        (xm_hbm.at[2 * W : 3 * W - 1], rr.at[1:W, own]),
        (r_hbm.at[0 : W + 1], rr.at[W:SPAN, own]),
        (r_hbm.at[cx - W - 1 : cx], rr.at[SPAN : SPAN + W + 1, own]),
        (xp_hbm.at[2 * W : 3 * W - 1], rr.at[SPAN + W + 1 : 2 * SPAN - 1, own]),
        (field_hbm.at[W:8], fin.at[W:8]),
        (field_hbm.at[cx - 8 : cx - W], fin.at[8 : 16 - W]),
    ):
        copies.append(pltpu.make_async_copy(src, dst, sems.at[len(copies)]))
    for copy in copies:
        copy.start()

    rr[0] = jnp.zeros((cy + 8, nz), F32)
    rr[2 * SPAN - 1] = jnp.zeros((cy + 8, nz), F32)

    def rows(dst, plane, after, before):
        dst[plane, cy : cy + W, :] = after
        dst[plane, cy + W : cy + 2 * W, :] = before

    for i in range(W + 1):
        for base, x in ((W + i, i), (SPAN + i, cx - W - 1 + i)):
            for which, dst in enumerate((ua, dd, rr)):
                rows(dst, base, yn[which, x], yp[which, x])
    for side, base in ((0, 0), (1, SPAN + W + 1)):
        at = side * (3 * W - 1)
        for i in range(W):
            rows(ua, base + i, cn[at + i], cp[at + i])
            rows(dd, base + i, cn[at + W + i], cp[at + W + i])
        for i in range(W - 1):
            rows(rr, base + i + 1 - side, cn[at + 2 * W + i], cp[at + 2 * W + i])
    work = Plane(dd, rr, kk, fbuf, place)
    first = (place[0] > 0).astype(F32)
    final = (place[0] < place[2] - 1).astype(F32)
    for copy in copies:
        copy.wait()

    src, dst = ua, ub
    for step in range(STEPS):
        last = step == STEPS - 1

        def end(side, carry, src=src, dst=dst, step=step, last=last):
            base = jnp.where(side == 0, step, SPAN + W - 1 - step)
            for i in range(3):
                work.local(src, dst, base + i)
            work.face(src, base + 1)
            for j in range(W):
                keep = None
                if not last:
                    keep = jnp.where(
                        side == 0, first if j < W - 1 - step else 1.0, final if j > step else 1.0
                    )
                target = side * (16 - W) + j if last else base + 1 + j
                work.across(src, dst, fin if last else dst, base + 1 + j, target, keep)
                if j < W - 1:
                    work.local(src, dst, base + 3 + j)
            return carry

        lax.fori_loop(0, 2, end, 0)
        if not last:
            for i in range(2):
                dst[step + W + 1 + i] = rim[4 * step + i]
                dst[SPAN + W - 2 - step + i] = rim[4 * step + 2 + i]
            src, dst = dst, src
    done = [
        pltpu.make_async_copy(fin.at[0:W], out_hbm.at[0:W], osem.at[0]),
        pltpu.make_async_copy(fin.at[16 - W : 16], out_hbm.at[cx - W : cx], osem.at[1]),
    ]
    for copy in done:
        copy.start()
    turn_over(fin, turned)
    done.append(pltpu.make_async_copy(turned, ft_hbm, osem.at[2]))
    done[2].start()
    for copy in done:
        copy.wait()


def outer(place, u, d, r, yn, yp, xm, xp, cn, cp, rim, field):
    cx, cy, nz = u.shape
    wide = pltpu.VMEM((2 * SPAN, cy + 8, nz), F32)
    return pl.pallas_call(
        outer_kernel,
        out_shape=(
            jax.ShapeDtypeStruct((cx, cy, nz), F32),
            jax.ShapeDtypeStruct((cy, 16, nz), F32),
        ),
        in_specs=[SCALARS] + [ANYWHERE] * 3 + [LOCAL] * 2 + [ANYWHERE] * 2 + [LOCAL] * 3 + [ANYWHERE],
        out_specs=(ANYWHERE, ANYWHERE),
        scratch_shapes=[wide] * 5
        + [
            pltpu.VMEM((cy + 8, nz), F32),
            pltpu.VMEM((16, cy, nz), F32),
            pltpu.VMEM((cy, 16, nz), F32),
            pltpu.SemaphoreType.DMA((14,)),
            pltpu.SemaphoreType.DMA((3,)),
        ],
        input_output_aliases={11: 0},
        name="outer",
    )(place, u, d, r, yn, yp, xm, xp, cn, cp, rim, field)


def render_kernel(whole, part, cen, lev, mix, ft, sign_ref, *rest):
    out, moved = rest[-2:]
    view = pl.program_id(1)
    depth, rows, nz = ft.shape
    blocks = nz // 128
    zero = jnp.zeros((rows, 128), F32)

    @pl.when(view == 0)
    def _():
        lane = lax.broadcasted_iota(jnp.int32, (rows, 128), 1)

        def shifts(y, carry):
            cells = [ft[y, :, 128 * b : 128 * b + 128] for b in range(blocks)]
            for b in range(blocks):
                moved[y, 0, :, 128 * b : 128 * b + 128] = cells[b]
            for n in range(1, MAXSHIFT + 1):
                back = [pltpu.roll(c, 128 - n, 1) for c in cells] + [zero]
                keep = lane < 128 - n
                for b in range(blocks):
                    moved[y, n, :, 128 * b : 128 * b + 128] = jnp.where(keep, back[b], back[b + 1])
            return carry

        lax.fori_loop(0, depth, shifts, 0, unroll=2)

    for b in range(blocks):
        at = slice(128 * b, 128 * b + 128)
        sign = jnp.broadcast_to(sign_ref[0, :, at], (rows, 128))
        rising = sign < 0.0
        light = jnp.ones((rows, 128), F32)
        sums = [zero] * BUMPS
        for y in range(depth):
            n = whole[view, y]
            near = moved[y, n, :, at]
            s = near + part[view, y] * (moved[y, n + 1, :, at] - near)
            bumps = []
            for i in range(BUMPS):
                t = s - cen[i]
                bumps.append(jnp.exp2(lev[i] - t * t))
            pairs = [bumps[i] + bumps[i + 1] for i in range(0, BUMPS, 2)]
            total = (pairs[0] + pairs[1]) + (pairs[2] + pairs[3])
            after = light * jnp.exp2(total * sign)
            weight = light - after
            light = after
            sums = [sums[i] + bumps[i] * weight for i in range(BUMPS)]
        inverse = 1.0 / light
        through = jnp.where(rising, light, inverse)
        scale = jnp.where(rising, 1.0, -inverse)
        channels = []
        for c in range(3):
            value = mix[c, 0] * sums[0]
            for i in range(1, BUMPS):
                value = value + mix[c, i] * sums[i]
            channels.append(value * scale)
        channels.append(through)
        for d in range(rows // 2):
            out[d, :, at] = jnp.concatenate([c[2 * d : 2 * d + 2] for c in channels], axis=0)


def render(whole, part, cen, lev, mix, ft, signs, spread, count, parts=None):
    cy, cx, nz = ft.shape
    operands = [whole, part, cen, lev, mix, ft, signs]
    in_specs = [SCALARS] * 5 + [
        pl.BlockSpec((cy, 8, nz), lambda i, v: (0, i, 0)),
        pl.BlockSpec((1, 1, nz), lambda i, v: (v, 0, 0)),
    ]
    aliases = {}
    if parts is not None:
        operands.append(parts)
        in_specs.append(ANYWHERE)
        aliases = {7: 0}
    cells = VIEWS * cx * cy * nz
    return pl.pallas_call(
        render_kernel,
        out_shape=jax.ShapeDtypeStruct((count, 8 * VIEWS, nz), F32),
        grid=(cx // 8, VIEWS),
        in_specs=in_specs,
        out_specs=pl.BlockSpec((4, 8, nz), lambda i, v: (spread(i), v, 0)),
        scratch_shapes=[pltpu.VMEM((cy, MAXSHIFT + 1, 8, nz), F32)],
        input_output_aliases=aliases,
        cost_estimate=pl.CostEstimate(
            flops=60 * cells, bytes_accessed=4 * (cx * cy + count * 8 * VIEWS) * nz, transcendentals=9 * cells
        ),
        name="render",
    )(*operands)


def combine_kernel(parts, sign_ref, image, trans):
    count, _, nz = parts.shape
    sub = lax.broadcasted_iota(jnp.int32, (8, nz), 0)
    for view in range(VIEWS):
        rising = jnp.broadcast_to(sign_ref[view], (8, nz)) < 0.0
        total = jnp.zeros((8, nz), F32)
        ahead = jnp.ones((8, nz), F32)
        for source in range(count):
            block = parts[source, 8 * view : 8 * view + 8, :]
            tail = jnp.where(sub >= 6, block, 0.0)
            pair = tail + pltpu.roll(tail, 4, 0)
            light = pair + pltpu.roll(pair, 2, 0)
            total = total * jnp.where(rising, 1.0, light) + block * jnp.where(rising, ahead, 1.0)
            ahead = ahead * light
        for c in range(3):
            image[view, c] = total[2 * c : 2 * c + 2]
        trans[view] = ahead[6:8]


def combine(parts, signs):
    nz = parts.shape[2]
    return pl.pallas_call(
        combine_kernel,
        out_shape=(
            jax.ShapeDtypeStruct((VIEWS, 3, 2, nz), F32),
            jax.ShapeDtypeStruct((VIEWS, 2, nz), F32),
        ),
        name="combine",
    )(parts, signs)


def scene_of(u, d, r, offsets, depth_order, centres, colour, opacity):
    cx, cy, _ = u.shape
    place = jnp.stack(
        [
            lax.axis_index("sx"),
            lax.axis_index("sy"),
            jnp.int32(lax.axis_size("sx")),
            jnp.int32(lax.axis_size("sy")),
        ]
    ).astype(jnp.int32)
    up_x = jnp.concatenate([u[cx - W :], d[cx - W :], r[cx - W + 1 :]])
    down_x = jnp.concatenate([u[:W], d[:W], r[: W - 1]])
    xm = shift(up_x, "sx", True)
    xp = shift(down_x, "sx", False)
    up_y = jnp.stack([a[:, cy - W :] for a in (u, d, r)])
    down_y = jnp.stack([a[:, :W] for a in (u, d, r)])
    yp = shift(up_y, "sy", True)
    yn = shift(down_y, "sy", False)
    cp = shift(jnp.concatenate([xm[:, cy - W :], xp[:, cy - W :]]), "sy", True)
    cn = shift(jnp.concatenate([xm[:, :W], xp[:, :W]]), "sy", False)
    offs = lax.dynamic_slice_in_dim(offsets, lax.axis_index("sy") * cy, cy, 1)
    signs = jnp.where(depth_order == 0, -1.0, 1.0).astype(F32)[:, None, :]
    level = opacity * LOG2E
    scene = (offs // 4, (offs % 4).astype(F32) * 0.25, centres * GAIN, jnp.log2(level), colour / level)

    field, turned, rim = inner(place, u, d, r, yn, yp)
    parts = render(*scene, turned, signs, lambda i: i + 1, cx // 2)
    field, turned = outer(place, u, d, r, yn, yp, xm, xp, cn, cp, rim, field)
    parts = render(*scene, turned, signs, lambda i: 3 * i, cx // 2, parts)
    parts = lax.all_to_all(parts, "sy", split_axis=0, concat_axis=0, tiled=True)
    image, trans = combine(parts, signs)
    return field, image, trans


def solution(mesh):
    grid = P("sx", "sy", None)
    return jax.shard_map(
        scene_of,
        mesh=mesh,
        in_specs=(grid, grid, grid, P(), P(), P(), P(), P()),
        out_specs=(
            grid,
            P(None, None, ("sx", "sy"), None),
            P(None, ("sx", "sy"), None),
        ),
        check_vma=False,
    )
```

time: 149 us -> 174 us (1.17)
  the two profiles are of different devices: /device:TPU:0 before, /device:TPU:6 now
where the time goes in v3:
time: 174 us; the launch traced here: 173 us
  Pallas kernels  81.6 us (47%)
  waiting for transfers between devices  30.6 us (18%)
  blocking collectives  26.8 us (15%)
  starting transfers between devices  16.3 us (9%)
  local copies, waits for them, and re-layouts  8.58 us (5%)
  other arithmetic  8.57 us (5%)
    pallas_call x2, Pallas kernels, render(): pl.pallas_call(render_kernel, out_shape=jax.ShapeDtypeStruct((count, 8 *...  31.3 us
    ppermute x6, waiting for transfers between devices, shift(): return lax.ppermute(value, axis, pairs)  30.6 us
    pallas_call x1, Pallas kernels, inner(): pl.pallas_call(inner_kernel, out_shape=(jax.ShapeDtypeStruct((cx, cy, nz)...  29.9 us
    all_to_all x1, blocking collectives, scene_of(): parts = lax.all_to_all(parts, 'sy', split_axis=0, concat_axis=0, tiled=True)  26.8 us
    pallas_call x1, Pallas kernels, outer(): pl.pallas_call(outer_kernel, out_shape=(jax.ShapeDtypeStruct((cx, cy, nz)...  18.2 us
    ppermute x6, starting transfers between devices, shift(): return lax.ppermute(value, axis, pairs)  16.3 us
  transfers between devices with their start and end apart: 6, of which 2 were waited for; matrix products, arithmetic and copies ran while one was open for 6% of the time, Pallas kernels for 26%

profile of v3, /device:TPU:6, one launch (start us, length us, event | category | flops | bytes accessed | tf_op | source)
XLA Modules:
  0.0 173.3 jit_solution(227265389602681269)
XLA Ops:
  0.6 1.3 slice_bitcast_fusion.2
  1.9 1.8 %slice_bitcast_fusion = (f32[1,32,4,512]{3,2,1,0:T(4,128)S(1)}, f32[1,32,4,512]{3,2,1,0:T(4,128)S(1)}, f32[1,32,4,512]{3,2,1,0:T(4,128)S(1)}, f32[1,32,4,512]{3,2,1,0:T(4,128)S(1)}) fusion(f32[32,32,512]{2,1,0:T(8,128)} %r_hbm.3, f32[32,32,512]{2,1,0:T(8,128)} %d_hbm.3), kind=kLoop, calls=%fused_computation.4 | loop fusion | bytes 2097152 | tf_op jit(solution)/shard_map/stack | solution.py:450
  3.7 1.1 pad_maximum_fusion.1
  4.8 1.8 %collective-permute-start.1 = (f32[3,32,4,512]{3,2,1,0:T(4,128)}, f32[3,32,4,512]{3,2,1,0:T(4,128)S(1)}, u32[]{:S(2)}, u32[]{:S(2)}) collective-permute-start(f32[3,32,4,512]{3,2,1,0:T(4,128)} %pad_maximum_fusion.1), channel_id=1, source_target_pairs={{0,1},{1,2},{2,3},{3,4},{4,5},{5,6},{6,7},{7,8},{8,9},{9,10},{10,1... | collective-permute-start | bytes 2359304 | tf_op jit(solution)/shard_map/ppermute | solution.py:25
  6.6 1.1 pad_maximum_fusion
  7.7 1.3 collective-permute-start
  8.9 1.3 fusion.3
  10.3 1.1 fusion.5
  11.3 0.9 pad_maximum_fusion.2
  12.3 5.8 %collective-permute-start.2 = (f32[11,32,512]{2,1,0:T(8,128)}, f32[11,32,512]{2,1,0:T(8,128)S(1)}, u32[]{:S(2)}, u32[]{:S(2)}) collective-permute-start(f32[11,32,512]{2,1,0:T(8,128)} %pad_maximum_fusion.2), channel_id=1, source_target_pairs={{0,16},{16,32},{32,48},{48,64},{64,80},{80,96},{96,112},{1,17},{17... | collective-permute-start | bytes 2162696 | tf_op jit(solution)/shard_map/ppermute | solution.py:25
  18.0 1.0 pad_maximum_fusion.3
  19.0 2.4 %collective-permute-start.3 = (f32[11,32,512]{2,1,0:T(8,128)}, f32[11,32,512]{2,1,0:T(8,128)S(1)}, u32[]{:S(2)}, u32[]{:S(2)}) collective-permute-start(f32[11,32,512]{2,1,0:T(8,128)} %pad_maximum_fusion.3), channel_id=1, source_target_pairs={{16,0},{32,16},{48,32},{64,48},{80,64},{96,80},{112,96},{17,1},{33... | collective-permute-start | bytes 2162696 | tf_op jit(solution)/shard_map/ppermute | solution.py:25
  22.1 1.3 add_select_fusion.1.whole
  24.0 14.2 %collective-permute-done.2.xm_hbm = f32[11,32,512]{2,1,0:T(8,128)S(1)} collective-permute-done((f32[11,32,512]{2,1,0:T(8,128)}, f32[11,32,512]{2,1,0:T(8,128)S(1)}, u32[]{:S(2)}, u32[]{:S(2)}) %collective-permute-start.2) | collective-permute-done | bytes 720928 | tf_op jit(solution)/shard_map/ppermute | solution.py:25
  38.2 16.4 %collective-permute-done.3.xp_hbm = f32[11,32,512]{2,1,0:T(8,128)S(1)} collective-permute-done((f32[11,32,512]{2,1,0:T(8,128)}, f32[11,32,512]{2,1,0:T(8,128)S(1)}, u32[]{:S(2)}, u32[]{:S(2)}) %collective-permute-start.3) | collective-permute-done | bytes 720928 | tf_op jit(solution)/shard_map/ppermute | solution.py:25
  54.8 1.3 collective-permute-start.4
  56.1 3.7 %collective-permute-start.5 = (f32[22,4,512]{2,1,0:T(4,128)S(1)}, f32[22,4,512]{2,1,0:T(4,128)}, u32[]{:S(2)}, u32[]{:S(2)}) collective-permute-start(f32[22,4,512]{2,1,0:T(4,128)S(1)} %pad_maximum_fusion.5), channel_id=1, source_target_pairs={{0,1},{1,2},{2,3},{3,4},{4,5},{5,6},{6,7},{7,8},{8,9},{9,10},{10,1... | collective-permute-start | bytes 540680 | tf_op jit(solution)/shard_map/ppermute | solution.py:25
  61.0 1.3 fusion.1.part
  64.2 29.9 %inner.1 = (f32[32,32,512]{2,1,0:T(8,128)}, f32[32,16,512]{2,1,0:T(8,128)}, f32[12,40,512]{2,1,0:T(8,128)}) custom-call(s32[4]{0:T(128)} %pad_add_fusion.place, f32[32,32,512]{2,1,0:T(8,128)} %u_hbm.3, f32[32,32,512]{2,1,0:T(8,128)} %d_hbm.3, f32[32,32,512]{2,1,0:T(8,128)} %r_hbm.3, f32[3,32,4,512]{3,2,1,0:T(4,128)} %copy-done.1, f32[3,32,4,512]{3,2,1,0:T(4,128)} %copy-done), custom_call_target="tpu_custom_call" | custom-call | flops 83886080 | bytes 12582912 | tf_op jit(solution)/shard_map/inner/pallas_call | solution.py:176
  94.1 15.7 %render.2.rest_0_ = f32[16,32,512]{2,1,0:T(8,128)} custom-call(s32[4,32]{1,0:T(4,128)} %add_select_fusion.1.whole, f32[4,32]{1,0:T(4,128)} %fusion.1.part, f32[8]{0:T(128)} %get-tuple-element.39.cen, f32[8]{0:T(128)} %get-tuple-element.34.lev, f32[3,8]{1,0:T(4,128)} %broadcast_divide_fusion.mix, f32[32,16,512]{2,1,0:T(8,128)} %get-tuple-element.14.ft, ...), custom_call_target="tpu_custom_call" | custom-call | flops 62914560 | bytes 2097152 | tf_op jit(solution)/shard_map/render/pallas_call | solution.py:390
  110.5 18.2 %outer.1 = (f32[32,32,512]{2,1,0:T(8,128)}, f32[32,16,512]{2,1,0:T(8,128)}) custom-call(s32[4]{0:T(128)} %pad_add_fusion.place, f32[32,32,512]{2,1,0:T(8,128)} %u_hbm.3, f32[32,32,512]{2,1,0:T(8,128)} %d_hbm.3, f32[32,32,512]{2,1,0:T(8,128)} %r_hbm.3, f32[3,32,4,512]{3,2,1,0:T(4,128)} %copy-done.1, ...), custom_call_target="tpu_custom_call", output_to_operand_aliasing={{0}: (11, {})} | custom-call | tf_op jit(solution)/shard_map/outer/pallas_call | solution.py:298
  128.6 15.6 %render.3 = f32[16,32,512]{2,1,0:T(8,128)} custom-call(s32[4,32]{1,0:T(4,128)} %add_select_fusion.1.whole, f32[4,32]{1,0:T(4,128)} %fusion.1.part, f32[8]{0:T(128)} %get-tuple-element.39.cen, f32[8]{0:T(128)} %get-tuple-element.34.lev, f32[3,8]{1,0:T(4,128)} %broadcast_divide_fusion.mix, ...), custom_call_target="tpu_custom_call", output_to_operand_aliasing={{}: (7, {})} | custom-call | flops 62914560 | bytes 2097152 | tf_op jit(solution)/shard_map/render/pallas_call | solution.py:390
  144.3 26.8 %all_to_all.5.parts = f32[16,32,512]{2,1,0:T(8,128)} all-to-all(f32[16,32,512]{2,1,0:T(8,128)} %render.3), channel_id=1, replica_groups=mesh['sx'=8,'sy'=16] {'sy'}, dimensions={0} | all-to-all | bytes 2097152 | tf_op jit(solution)/shard_map/all_to_all | solution.py:465
  171.0 2.2 %combine.1 = (f32[4,3,2,512]{3,2,1,0:T(2,128)}, f32[4,2,512]{2,1,0:T(2,128)}) custom-call(f32[16,32,512]{2,1,0:T(8,128)} %all_to_all.5.parts, f32[4,1,512]{2,1,0:T(1,128)} %broadcast_in_dim.14.sign_ref), custom_call_target="tpu_custom_call" | custom-call | tf_op jit(solution)/shard_map/combine/pallas_call | solution.py:426
  (31 shorter events, 5.0 us)
Async XLA Ops:
  4.8 57.6 %collective-permute-start.1 = (f32[3,32,4,512]{3,2,1,0:T(4,128)}, f32[3,32,4,512]{3,2,1,0:T(4,128)S(1)}, u32[]{:S(2)}, u32[]{:S(2)}) collective-permute-start(f32[3,32,4,512]{3,2,1,0:T(4,128)} %pad_maximum_fusion.1), channel_id=1, source_target_pairs={{0,1},{1,2},{2,3},{3,4},{4,5},{5,6},{6,7},{7,8},{8,9},{9,10},{10,1... | collective-permute-start | bytes 2359304 | tf_op jit(solution)/shard_map/ppermute | solution.py:25
  7.7 54.7 %collective-permute-start = (f32[3,32,4,512]{3,2,1,0:T(4,128)}, f32[3,32,4,512]{3,2,1,0:T(4,128)S(1)}, u32[]{:S(2)}, u32[]{:S(2)}) collective-permute-start(f32[3,32,4,512]{3,2,1,0:T(4,128)} %pad_maximum_fusion), channel_id=1, source_target_pairs={{1,0},{2,1},{3,2},{4,3},{5,4},{6,5},{7,6},{8,7},{9,8},{10,9},{11,1... | collective-permute-start | bytes 2359304 | tf_op jit(solution)/shard_map/ppermute | solution.py:25
  10.2 11.3 %copy-start.7 = (f32[8]{0:T(128)S(1)}, f32[8]{0:T(128)}, u32[]{:S(2)}) copy-start(f32[8]{0:T(128)} %param.15) | copy-start | bytes 100
  10.2 11.3 %copy-start.8 = (f32[8]{0:T(128)S(1)}, f32[8]{0:T(128)}, u32[]{:S(2)}) copy-start(f32[8]{0:T(128)} %param.13) | copy-start | bytes 100
  10.2 13.2 %copy-start.6 = (f32[3,8]{1,0:T(4,128)S(1)}, f32[3,8]{1,0:T(4,128)}, u32[]{:S(2)}) copy-start(f32[3,8]{1,0:T(4,128)} %param.14) | copy-start | bytes 292
  10.3 13.7 %copy-start.5 = (s32[4,512]{1,0:T(4,128)S(1)}, s32[4,512]{1,0:T(4,128)}, u32[]{:S(2)}) copy-start(s32[4,512]{1,0:T(4,128)} %param.12) | copy-start | bytes 24580
  12.3 25.9 %collective-permute-start.2 = (f32[11,32,512]{2,1,0:T(8,128)}, f32[11,32,512]{2,1,0:T(8,128)S(1)}, u32[]{:S(2)}, u32[]{:S(2)}) collective-permute-start(f32[11,32,512]{2,1,0:T(8,128)} %pad_maximum_fusion.2), channel_id=1, source_target_pairs={{0,16},{16,32},{32,48},{48,64},{64,80},{80,96},{96,112},{1,17},{17... | collective-permute-start | bytes 2162696 | tf_op jit(solution)/shard_map/ppermute | solution.py:25
  19.0 35.7 %collective-permute-start.3 = (f32[11,32,512]{2,1,0:T(8,128)}, f32[11,32,512]{2,1,0:T(8,128)S(1)}, u32[]{:S(2)}, u32[]{:S(2)}) collective-permute-start(f32[11,32,512]{2,1,0:T(8,128)} %pad_maximum_fusion.3), channel_id=1, source_target_pairs={{16,0},{32,16},{48,32},{64,48},{80,64},{96,80},{112,96},{17,1},{33... | collective-permute-start | bytes 2162696 | tf_op jit(solution)/shard_map/ppermute | solution.py:25
  38.2 55.9 %copy-start.2 = (f32[11,32,512]{2,1,0:T(8,128)}, f32[11,32,512]{2,1,0:T(8,128)S(1)}, u32[]{:S(2)}) copy-start(f32[11,32,512]{2,1,0:T(8,128)S(1)} %collective-permute-done.2.xm_hbm) | copy-start | bytes 2162692
  54.7 39.4 %copy-start.3 = (f32[11,32,512]{2,1,0:T(8,128)}, f32[11,32,512]{2,1,0:T(8,128)S(1)}, u32[]{:S(2)}) copy-start(f32[11,32,512]{2,1,0:T(8,128)S(1)} %collective-permute-done.3.xp_hbm) | copy-start | bytes 2162692
  54.8 55.0 %collective-permute-start.4 = (f32[22,4,512]{2,1,0:T(4,128)S(1)}, f32[22,4,512]{2,1,0:T(4,128)S(1)}, u32[]{:S(2)}, u32[]{:S(2)}) collective-permute-start(f32[22,4,512]{2,1,0:T(4,128)S(1)} %pad_maximum_fusion.4), channel_id=1, source_target_pairs={{1,0},{2,1},{3,2},{4,3},{5,4},{6,5},{7,6},{8,7},{9,8},{10,9},{11,1... | collective-permute-start | bytes 540680 | tf_op jit(solution)/shard_map/ppermute | solution.py:25
  56.1 53.7 %collective-permute-start.5 = (f32[22,4,512]{2,1,0:T(4,128)S(1)}, f32[22,4,512]{2,1,0:T(4,128)}, u32[]{:S(2)}, u32[]{:S(2)}) collective-permute-start(f32[22,4,512]{2,1,0:T(4,128)S(1)} %pad_maximum_fusion.5), channel_id=1, source_target_pairs={{0,1},{1,2},{2,3},{3,4},{4,5},{5,6},{6,7},{7,8},{8,9},{9,10},{10,1... | collective-permute-start | bytes 540680 | tf_op jit(solution)/shard_map/ppermute | solution.py:25
  62.4 0.9 copy-start
  63.3 0.9 copy-start.1
  109.8 0.7 copy-start.4

commit v4 on v3

--- a/solution.py
+++ b/solution.py
@@ -9,7 +9,6 @@
 STEPS = 4
 VIEWS = 4
 BUMPS = 8
-MAXSHIFT = 8
 W = STEPS
 LOG2E = 1.4426950408889634
 GAIN = 2.0 * LOG2E**0.5
@@ -326,19 +325,22 @@
     @pl.when(view == 0)
     def _():
         lane = lax.broadcasted_iota(jnp.int32, (rows, 128), 1)
-
-        def shifts(y, carry):
+        lane_last = lane == 127
+
+        def shear(y, carry):
             cells = [ft[y, :, 128 * b : 128 * b + 128] for b in range(blocks)]
-            for b in range(blocks):
-                moved[y, 0, :, 128 * b : 128 * b + 128] = cells[b]
-            for n in range(1, MAXSHIFT + 1):
-                back = [pltpu.roll(c, 128 - n, 1) for c in cells] + [zero]
+            back = [pltpu.roll(c, 127, 1) for c in cells] + [zero]
+            slope = [jnp.where(lane_last, back[b + 1], back[b]) - cells[b] for b in range(blocks)]
+            for v in range(VIEWS):
+                n, f = whole[v, y], part[v, y]
+                turn = lax.rem(128 - n, 128)
                 keep = lane < 128 - n
+                back = [pltpu.roll(cells[b] + f * slope[b], turn, 1) for b in range(blocks)] + [zero]
                 for b in range(blocks):
-                    moved[y, n, :, 128 * b : 128 * b + 128] = jnp.where(keep, back[b], back[b + 1])
+                    moved[v, y, :, 128 * b : 128 * b + 128] = jnp.where(keep, back[b], back[b + 1])
             return carry
 
-        lax.fori_loop(0, depth, shifts, 0, unroll=2)
+        lax.fori_loop(0, depth, shear, 0, unroll=8)
 
     for b in range(blocks):
         at = slice(128 * b, 128 * b + 128)
@@ -347,9 +349,7 @@
         light = jnp.ones((rows, 128), F32)
         sums = [zero] * BUMPS
         for y in range(depth):
-            n = whole[view, y]
-            near = moved[y, n, :, at]
-            s = near + part[view, y] * (moved[y, n + 1, :, at] - near)
+            s = moved[view, y, :, at]
             bumps = []
             for i in range(BUMPS):
                 t = s - cen[i]
@@ -393,7 +393,7 @@
         grid=(cx // 8, VIEWS),
         in_specs=in_specs,
         out_specs=pl.BlockSpec((4, 8, nz), lambda i, v: (spread(i), v, 0)),
-        scratch_shapes=[pltpu.VMEM((cy, MAXSHIFT + 1, 8, nz), F32)],
+        scratch_shapes=[pltpu.VMEM((VIEWS, cy, 8, nz), F32)],
         input_output_aliases=aliases,
         cost_estimate=pl.CostEstimate(
             flops=60 * cells, bytes_accessed=4 * (cx * cy + count * 8 * VIEWS) * nz, transcendentals=9 * cells

time: 174 us -> 171 us (0.983)
  Pallas kernels: 81.6 us -> 78.4 us
    pallas_call x2, Pallas kernels: 31.3 us -> 28 us  [render(): pl.pallas_call(render_kernel, out_shape=jax.ShapeDtypeStruct((count, 8 *...]
where the time goes in v4:
time: 171 us; the launch traced here: 170 us
  Pallas kernels  78.4 us (46%)
  waiting for transfers between devices  30.6 us (18%)
  blocking collectives  26.8 us (16%)
  starting transfers between devices  16.3 us (10%)
  local copies, waits for them, and re-layouts  8.58 us (5%)
  other arithmetic  8.57 us (5%)
    ppermute x6, waiting for transfers between devices, shift(): return lax.ppermute(value, axis, pairs)  30.6 us
    pallas_call x1, Pallas kernels, inner(): pl.pallas_call(inner_kernel, out_shape=(jax.ShapeDtypeStruct((cx, cy, nz)...  29.9 us
    pallas_call x2, Pallas kernels, render(): pl.pallas_call(render_kernel, out_shape=jax.ShapeDtypeStruct((count, 8 *...  28 us
    all_to_all x1, blocking collectives, scene_of(): parts = lax.all_to_all(parts, 'sy', split_axis=0, concat_axis=0, tiled=True)  26.8 us
    pallas_call x1, Pallas kernels, outer(): pl.pallas_call(outer_kernel, out_shape=(jax.ShapeDtypeStruct((cx, cy, nz)...  18.2 us
    ppermute x6, starting transfers between devices, shift(): return lax.ppermute(value, axis, pairs)  16.3 us
  transfers between devices with their start and end apart: 6, of which 2 were waited for; matrix products, arithmetic and copies ran while one was open for 6% of the time, Pallas kernels for 26%

profile of v4, /device:TPU:6, one launch (start us, length us, event | category | flops | bytes accessed | tf_op | source)
XLA Modules:
  0.0 170.0 jit_solution(16464645590805188569)
XLA Ops:
  0.6 1.3 slice_bitcast_fusion.2
  1.9 1.8 %slice_bitcast_fusion = (f32[1,32,4,512]{3,2,1,0:T(4,128)S(1)}, f32[1,32,4,512]{3,2,1,0:T(4,128)S(1)}, f32[1,32,4,512]{3,2,1,0:T(4,128)S(1)}, f32[1,32,4,512]{3,2,1,0:T(4,128)S(1)}) fusion(f32[32,32,512]{2,1,0:T(8,128)} %r_hbm.3, f32[32,32,512]{2,1,0:T(8,128)} %d_hbm.3), kind=kLoop, calls=%fused_computation.4 | loop fusion | bytes 2097152 | tf_op jit(solution)/shard_map/stack | solution.py:450
  3.7 1.1 pad_maximum_fusion.1
  4.8 1.8 %collective-permute-start.1 = (f32[3,32,4,512]{3,2,1,0:T(4,128)}, f32[3,32,4,512]{3,2,1,0:T(4,128)S(1)}, u32[]{:S(2)}, u32[]{:S(2)}) collective-permute-start(f32[3,32,4,512]{3,2,1,0:T(4,128)} %pad_maximum_fusion.1), channel_id=1, source_target_pairs={{0,1},{1,2},{2,3},{3,4},{4,5},{5,6},{6,7},{7,8},{8,9},{9,10},{10,1... | collective-permute-start | bytes 2359304 | tf_op jit(solution)/shard_map/ppermute | solution.py:24
  6.6 1.1 pad_maximum_fusion
  7.7 1.3 collective-permute-start
  8.9 1.3 fusion.3
  10.3 1.1 fusion.5
  11.3 0.9 pad_maximum_fusion.2
  12.3 5.8 %collective-permute-start.2 = (f32[11,32,512]{2,1,0:T(8,128)}, f32[11,32,512]{2,1,0:T(8,128)S(1)}, u32[]{:S(2)}, u32[]{:S(2)}) collective-permute-start(f32[11,32,512]{2,1,0:T(8,128)} %pad_maximum_fusion.2), channel_id=1, source_target_pairs={{0,16},{16,32},{32,48},{48,64},{64,80},{80,96},{96,112},{1,17},{17... | collective-permute-start | bytes 2162696 | tf_op jit(solution)/shard_map/ppermute | solution.py:24
  18.0 1.0 pad_maximum_fusion.3
  19.0 2.4 %collective-permute-start.3 = (f32[11,32,512]{2,1,0:T(8,128)}, f32[11,32,512]{2,1,0:T(8,128)S(1)}, u32[]{:S(2)}, u32[]{:S(2)}) collective-permute-start(f32[11,32,512]{2,1,0:T(8,128)} %pad_maximum_fusion.3), channel_id=1, source_target_pairs={{16,0},{32,16},{48,32},{64,48},{80,64},{96,80},{112,96},{17,1},{33... | collective-permute-start | bytes 2162696 | tf_op jit(solution)/shard_map/ppermute | solution.py:24
  22.1 1.3 add_select_fusion.1.whole
  24.0 14.2 %collective-permute-done.2.xm_hbm = f32[11,32,512]{2,1,0:T(8,128)S(1)} collective-permute-done((f32[11,32,512]{2,1,0:T(8,128)}, f32[11,32,512]{2,1,0:T(8,128)S(1)}, u32[]{:S(2)}, u32[]{:S(2)}) %collective-permute-start.2) | collective-permute-done | bytes 720928 | tf_op jit(solution)/shard_map/ppermute | solution.py:24
  38.2 16.4 %collective-permute-done.3.xp_hbm = f32[11,32,512]{2,1,0:T(8,128)S(1)} collective-permute-done((f32[11,32,512]{2,1,0:T(8,128)}, f32[11,32,512]{2,1,0:T(8,128)S(1)}, u32[]{:S(2)}, u32[]{:S(2)}) %collective-permute-start.3) | collective-permute-done | bytes 720928 | tf_op jit(solution)/shard_map/ppermute | solution.py:24
  54.8 1.3 collective-permute-start.4
  56.1 3.7 %collective-permute-start.5 = (f32[22,4,512]{2,1,0:T(4,128)S(1)}, f32[22,4,512]{2,1,0:T(4,128)}, u32[]{:S(2)}, u32[]{:S(2)}) collective-permute-start(f32[22,4,512]{2,1,0:T(4,128)S(1)} %pad_maximum_fusion.5), channel_id=1, source_target_pairs={{0,1},{1,2},{2,3},{3,4},{4,5},{5,6},{6,7},{7,8},{8,9},{9,10},{10,1... | collective-permute-start | bytes 540680 | tf_op jit(solution)/shard_map/ppermute | solution.py:24
  61.0 1.3 fusion.1.part
  64.2 29.9 %inner.1 = (f32[32,32,512]{2,1,0:T(8,128)}, f32[32,16,512]{2,1,0:T(8,128)}, f32[12,40,512]{2,1,0:T(8,128)}) custom-call(s32[4]{0:T(128)} %pad_add_fusion.place, f32[32,32,512]{2,1,0:T(8,128)} %u_hbm.3, f32[32,32,512]{2,1,0:T(8,128)} %d_hbm.3, f32[32,32,512]{2,1,0:T(8,128)} %r_hbm.3, f32[3,32,4,512]{3,2,1,0:T(4,128)} %copy-done.1, f32[3,32,4,512]{3,2,1,0:T(4,128)} %copy-done), custom_call_target="tpu_custom_call" | custom-call | flops 83886080 | bytes 12582912 | tf_op jit(solution)/shard_map/inner/pallas_call | solution.py:175
  94.1 14.0 %render.2.rest_0_ = f32[16,32,512]{2,1,0:T(8,128)} custom-call(s32[4,32]{1,0:T(4,128)} %add_select_fusion.1.whole, f32[4,32]{1,0:T(4,128)} %fusion.1.part, f32[8]{0:T(128)} %get-tuple-element.39.cen, f32[8]{0:T(128)} %get-tuple-element.34.lev, f32[3,8]{1,0:T(4,128)} %broadcast_divide_fusion.mix, f32[32,16,512]{2,1,0:T(8,128)} %get-tuple-element.14.ft, ...), custom_call_target="tpu_custom_call" | custom-call | flops 62914560 | bytes 2097152 | tf_op jit(solution)/shard_map/render/pallas_call | solution.py:390
  108.8 18.2 %outer.1 = (f32[32,32,512]{2,1,0:T(8,128)}, f32[32,16,512]{2,1,0:T(8,128)}) custom-call(s32[4]{0:T(128)} %pad_add_fusion.place, f32[32,32,512]{2,1,0:T(8,128)} %u_hbm.3, f32[32,32,512]{2,1,0:T(8,128)} %d_hbm.3, f32[32,32,512]{2,1,0:T(8,128)} %r_hbm.3, f32[3,32,4,512]{3,2,1,0:T(4,128)} %copy-done.1, ...), custom_call_target="tpu_custom_call", output_to_operand_aliasing={{0}: (11, {})} | custom-call | tf_op jit(solution)/shard_map/outer/pallas_call | solution.py:297
  127.0 14.0 %render.3 = f32[16,32,512]{2,1,0:T(8,128)} custom-call(s32[4,32]{1,0:T(4,128)} %add_select_fusion.1.whole, f32[4,32]{1,0:T(4,128)} %fusion.1.part, f32[8]{0:T(128)} %get-tuple-element.39.cen, f32[8]{0:T(128)} %get-tuple-element.34.lev, f32[3,8]{1,0:T(4,128)} %broadcast_divide_fusion.mix, ...), custom_call_target="tpu_custom_call", output_to_operand_aliasing={{}: (7, {})} | custom-call | flops 62914560 | bytes 2097152 | tf_op jit(solution)/shard_map/render/pallas_call | solution.py:390
  141.0 26.8 %all_to_all.5.parts = f32[16,32,512]{2,1,0:T(8,128)} all-to-all(f32[16,32,512]{2,1,0:T(8,128)} %render.3), channel_id=1, replica_groups=mesh['sx'=8,'sy'=16] {'sy'}, dimensions={0} | all-to-all | bytes 2097152 | tf_op jit(solution)/shard_map/all_to_all | solution.py:465
  167.8 2.2 %combine.1 = (f32[4,3,2,512]{3,2,1,0:T(2,128)}, f32[4,2,512]{2,1,0:T(2,128)}) custom-call(f32[16,32,512]{2,1,0:T(8,128)} %all_to_all.5.parts, f32[4,1,512]{2,1,0:T(1,128)} %broadcast_in_dim.14.sign_ref), custom_call_target="tpu_custom_call" | custom-call | tf_op jit(solution)/shard_map/combine/pallas_call | solution.py:426
  (31 shorter events, 5.0 us)
Async XLA Ops:
  4.8 57.6 %collective-permute-start.1 = (f32[3,32,4,512]{3,2,1,0:T(4,128)}, f32[3,32,4,512]{3,2,1,0:T(4,128)S(1)}, u32[]{:S(2)}, u32[]{:S(2)}) collective-permute-start(f32[3,32,4,512]{3,2,1,0:T(4,128)} %pad_maximum_fusion.1), channel_id=1, source_target_pairs={{0,1},{1,2},{2,3},{3,4},{4,5},{5,6},{6,7},{7,8},{8,9},{9,10},{10,1... | collective-permute-start | bytes 2359304 | tf_op jit(solution)/shard_map/ppermute | solution.py:24
  7.7 54.7 %collective-permute-start = (f32[3,32,4,512]{3,2,1,0:T(4,128)}, f32[3,32,4,512]{3,2,1,0:T(4,128)S(1)}, u32[]{:S(2)}, u32[]{:S(2)}) collective-permute-start(f32[3,32,4,512]{3,2,1,0:T(4,128)} %pad_maximum_fusion), channel_id=1, source_target_pairs={{1,0},{2,1},{3,2},{4,3},{5,4},{6,5},{7,6},{8,7},{9,8},{10,9},{11,1... | collective-permute-start | bytes 2359304 | tf_op jit(solution)/shard_map/ppermute | solution.py:24
  10.2 11.3 %copy-start.7 = (f32[8]{0:T(128)S(1)}, f32[8]{0:T(128)}, u32[]{:S(2)}) copy-start(f32[8]{0:T(128)} %param.15) | copy-start | bytes 100
  10.2 11.3 %copy-start.8 = (f32[8]{0:T(128)S(1)}, f32[8]{0:T(128)}, u32[]{:S(2)}) copy-start(f32[8]{0:T(128)} %param.13) | copy-start | bytes 100
  10.2 13.2 %copy-start.6 = (f32[3,8]{1,0:T(4,128)S(1)}, f32[3,8]{1,0:T(4,128)}, u32[]{:S(2)}) copy-start(f32[3,8]{1,0:T(4,128)} %param.14) | copy-start | bytes 292
  10.3 13.7 %copy-start.5 = (s32[4,512]{1,0:T(4,128)S(1)}, s32[4,512]{1,0:T(4,128)}, u32[]{:S(2)}) copy-start(s32[4,512]{1,0:T(4,128)} %param.12) | copy-start | bytes 24580
  12.3 25.9 %collective-permute-start.2 = (f32[11,32,512]{2,1,0:T(8,128)}, f32[11,32,512]{2,1,0:T(8,128)S(1)}, u32[]{:S(2)}, u32[]{:S(2)}) collective-permute-start(f32[11,32,512]{2,1,0:T(8,128)} %pad_maximum_fusion.2), channel_id=1, source_target_pairs={{0,16},{16,32},{32,48},{48,64},{64,80},{80,96},{96,112},{1,17},{17... | collective-permute-start | bytes 2162696 | tf_op jit(solution)/shard_map/ppermute | solution.py:24
  19.0 35.7 %collective-permute-start.3 = (f32[11,32,512]{2,1,0:T(8,128)}, f32[11,32,512]{2,1,0:T(8,128)S(1)}, u32[]{:S(2)}, u32[]{:S(2)}) collective-permute-start(f32[11,32,512]{2,1,0:T(8,128)} %pad_maximum_fusion.3), channel_id=1, source_target_pairs={{16,0},{32,16},{48,32},{64,48},{80,64},{96,80},{112,96},{17,1},{33... | collective-permute-start | bytes 2162696 | tf_op jit(solution)/shard_map/ppermute | solution.py:24
  38.2 55.9 %copy-start.2 = (f32[11,32,512]{2,1,0:T(8,128)}, f32[11,32,512]{2,1,0:T(8,128)S(1)}, u32[]{:S(2)}) copy-start(f32[11,32,512]{2,1,0:T(8,128)S(1)} %collective-permute-done.2.xm_hbm) | copy-start | bytes 2162692
  54.7 39.4 %copy-start.3 = (f32[11,32,512]{2,1,0:T(8,128)}, f32[11,32,512]{2,1,0:T(8,128)S(1)}, u32[]{:S(2)}) copy-start(f32[11,32,512]{2,1,0:T(8,128)S(1)} %collective-permute-done.3.xp_hbm) | copy-start | bytes 2162692
  54.8 53.4 %collective-permute-start.4 = (f32[22,4,512]{2,1,0:T(4,128)S(1)}, f32[22,4,512]{2,1,0:T(4,128)S(1)}, u32[]{:S(2)}, u32[]{:S(2)}) collective-permute-start(f32[22,4,512]{2,1,0:T(4,128)S(1)} %pad_maximum_fusion.4), channel_id=1, source_target_pairs={{1,0},{2,1},{3,2},{4,3},{5,4},{6,5},{7,6},{8,7},{9,8},{10,9},{11,1... | collective-permute-start | bytes 540680 | tf_op jit(solution)/shard_map/ppermute | solution.py:24
  56.1 52.0 %collective-permute-start.5 = (f32[22,4,512]{2,1,0:T(4,128)S(1)}, f32[22,4,512]{2,1,0:T(4,128)}, u32[]{:S(2)}, u32[]{:S(2)}) collective-permute-start(f32[22,4,512]{2,1,0:T(4,128)S(1)} %pad_maximum_fusion.5), channel_id=1, source_target_pairs={{0,1},{1,2},{2,3},{3,4},{4,5},{5,6},{6,7},{7,8},{8,9},{9,10},{10,1... | collective-permute-start | bytes 540680 | tf_op jit(solution)/shard_map/ppermute | solution.py:24
  62.4 0.9 copy-start
  63.3 0.9 copy-start.1
  108.2 0.7 copy-start.4

commit v5 on v4

--- a/solution.py
+++ b/solution.py
@@ -29,8 +29,8 @@
 
 
 class Plane:
-    def __init__(self, dd, rr, kk, fbuf, place):
-        self.dd, self.rr, self.kk, self.fbuf = dd, rr, kk, fbuf
+    def __init__(self, dd, dn, rr, kk, fbuf, place):
+        self.dd, self.dn, self.rr, self.kk, self.fbuf = dd, dn, rr, kk, fbuf
         self.tiles, self.blocks = dd.shape[1] // 8, dd.shape[2] // 128
         sub = lax.broadcasted_iota(jnp.int32, (8, 128), 0)
         lane = lax.broadcasted_iota(jnp.int32, (8, 128), 1)
@@ -41,6 +41,13 @@
             sub < W, (place[1] < place[3] - 1).astype(F32), (place[1] > 0).astype(F32)
         )
 
+    def prepare(self, plane):
+        for t in range(self.tiles):
+            up = [pltpu.roll(self.dd[(plane,) + cut(t, b)], 127, 1) for b in range(self.blocks)]
+            up.append(self.zero)
+            for b in range(self.blocks):
+                self.dn[(plane,) + cut(t, b)] = jnp.where(self.lane_last, up[b + 1], up[b])
+
     def local(self, src, dst, plane):
         blocks = self.blocks
         for t in range(self.tiles):
@@ -48,11 +55,10 @@
             warm = [jnp.tanh(v) for v in u]
             k = [self.dd[(plane,) + cut(t, b)] * (0.5 + 0.2 * warm[b]) for b in range(blocks)]
             u_up = [pltpu.roll(v, 127, 1) for v in u] + [self.zero]
-            k_up = [pltpu.roll(v, 127, 1) for v in k] + [self.zero]
             flux = []
             for b in range(blocks):
                 un = jnp.where(self.lane_last, u_up[b + 1], u_up[b])
-                kn = jnp.where(self.lane_last, k_up[b + 1], k_up[b])
+                kn = self.dn[(plane,) + cut(t, b)] * (0.5 + 0.2 * jnp.tanh(un))
                 flux.append((k[b] + kn) * (un - u[b]))
             down = [pltpu.roll(v, 1, 1) for v in flux]
             for b in range(blocks):
@@ -114,7 +120,7 @@
 def inner_kernel(
     place, u_hbm, d_hbm, r_hbm, yn, yp,
     out_hbm, ft_hbm, rim,
-    ua, ub, dd, rr, kk, fbuf, fin, turned, sems, osem,
+    ua, ub, dd, dn, rr, kk, fbuf, fin, turned, sems, osem,
 ):
     cx, cy, _ = u_hbm.shape
     copies = [
@@ -131,9 +137,10 @@
         return carry
 
     lax.fori_loop(0, cx, edge_rows, 0)
-    work = Plane(dd, rr, kk, fbuf, place)
+    work = Plane(dd, dn, rr, kk, fbuf, place)
     for copy in copies:
         copy.wait()
+    lax.fori_loop(0, dd.shape[0], lambda i, c: (work.prepare(i), c)[1], 0, unroll=2)
 
     src, dst = ua, ub
     for step in range(STEPS):
@@ -181,7 +188,7 @@
         ),
         in_specs=[SCALARS] + [ANYWHERE] * 3 + [LOCAL] * 2,
         out_specs=(ANYWHERE, ANYWHERE, LOCAL),
-        scratch_shapes=[wide] * 5
+        scratch_shapes=[wide] * 6
         + [
             pltpu.VMEM((cy + 8, nz), F32),
             pltpu.VMEM((cx - 2 * W, cy, nz), F32),
@@ -202,7 +209,7 @@
 def outer_kernel(
     place, u_hbm, d_hbm, r_hbm, yn, yp, xm_hbm, xp_hbm, cn, cp, rim, field_hbm,
     out_hbm, ft_hbm,
-    ua, ub, dd, rr, kk, fbuf, fin, turned, sems, osem,
+    ua, ub, dd, dn, rr, kk, fbuf, fin, turned, sems, osem,
 ):
     cx, cy, nz = u_hbm.shape
     own = slice(0, cy)
@@ -245,11 +252,12 @@
             rows(dd, base + i, cn[at + W + i], cp[at + W + i])
         for i in range(W - 1):
             rows(rr, base + i + 1 - side, cn[at + 2 * W + i], cp[at + 2 * W + i])
-    work = Plane(dd, rr, kk, fbuf, place)
+    work = Plane(dd, dn, rr, kk, fbuf, place)
     first = (place[0] > 0).astype(F32)
     final = (place[0] < place[2] - 1).astype(F32)
     for copy in copies:
         copy.wait()
+    lax.fori_loop(0, dd.shape[0], lambda i, c: (work.prepare(i), c)[1], 0, unroll=2)
 
     src, dst = ua, ub
     for step in range(STEPS):
@@ -302,7 +310,7 @@
         ),
         in_specs=[SCALARS] + [ANYWHERE] * 3 + [LOCAL] * 2 + [ANYWHERE] * 2 + [LOCAL] * 3 + [ANYWHERE],
         out_specs=(ANYWHERE, ANYWHERE),
-        scratch_shapes=[wide] * 5
+        scratch_shapes=[wide] * 6
         + [
             pltpu.VMEM((cy + 8, nz), F32),
             pltpu.VMEM((16, cy, nz), F32),

time: 171 us -> 166 us (0.971)
  Pallas kernels: 78.4 us -> 74 us
    pallas_call x1, Pallas kernels: 18.2 us -> 15 us  [outer(): pl.pallas_call(outer_kernel, out_shape=(jax.ShapeDtypeStruct((cx, cy, nz)...]
where the time goes in v5:
time: 166 us
  Pallas kernels  74 us (45%)
  waiting for transfers between devices  30.6 us (18%)
  blocking collectives  26.8 us (16%)
  starting transfers between devices  16.3 us (10%)
  local copies, waits for them, and re-layouts  8.58 us (5%)
  other arithmetic  8.57 us (5%)
    ppermute x6, waiting for transfers between devices, shift(): return lax.ppermute(value, axis, pairs)  30.6 us
    pallas_call x1, Pallas kernels, inner(): pl.pallas_call(inner_kernel, out_shape=(jax.ShapeDtypeStruct((cx, cy, nz)...  28.7 us
    pallas_call x2, Pallas kernels, render(): pl.pallas_call(render_kernel, out_shape=jax.ShapeDtypeStruct((count, 8 *...  28 us
    all_to_all x1, blocking collectives, scene_of(): parts = lax.all_to_all(parts, 'sy', split_axis=0, concat_axis=0, tiled=True)  26.8 us
    ppermute x6, starting transfers between devices, shift(): return lax.ppermute(value, axis, pairs)  16.3 us
    pallas_call x1, Pallas kernels, outer(): pl.pallas_call(outer_kernel, out_shape=(jax.ShapeDtypeStruct((cx, cy, nz)...  15 us
  transfers between devices with their start and end apart: 6, of which 2 were waited for; matrix products, arithmetic and copies ran while one was open for 6% of the time, Pallas kernels for 26%

profile of v5, /device:TPU:6, one launch (start us, length us, event | category | flops | bytes accessed | tf_op | source)
XLA Modules:
  0.0 165.7 jit_solution(6101999690367436071)
XLA Ops:
  0.6 1.3 slice_bitcast_fusion.2
  1.9 1.8 %slice_bitcast_fusion = (f32[1,32,4,512]{3,2,1,0:T(4,128)S(1)}, f32[1,32,4,512]{3,2,1,0:T(4,128)S(1)}, f32[1,32,4,512]{3,2,1,0:T(4,128)S(1)}, f32[1,32,4,512]{3,2,1,0:T(4,128)S(1)}) fusion(f32[32,32,512]{2,1,0:T(8,128)} %r_hbm.3, f32[32,32,512]{2,1,0:T(8,128)} %d_hbm.3), kind=kLoop, calls=%fused_computation.4 | loop fusion | bytes 2097152 | tf_op jit(solution)/shard_map/stack | solution.py:458
  3.7 1.1 pad_maximum_fusion.1
  4.8 1.8 %collective-permute-start.1 = (f32[3,32,4,512]{3,2,1,0:T(4,128)}, f32[3,32,4,512]{3,2,1,0:T(4,128)S(1)}, u32[]{:S(2)}, u32[]{:S(2)}) collective-permute-start(f32[3,32,4,512]{3,2,1,0:T(4,128)} %pad_maximum_fusion.1), channel_id=1, source_target_pairs={{0,1},{1,2},{2,3},{3,4},{4,5},{5,6},{6,7},{7,8},{8,9},{9,10},{10,1... | collective-permute-start | bytes 2359304 | tf_op jit(solution)/shard_map/ppermute | solution.py:24
  6.6 1.1 pad_maximum_fusion
  7.7 1.3 collective-permute-start
  8.9 1.3 fusion.3
  10.3 1.1 fusion.5
  11.3 0.9 pad_maximum_fusion.2
  12.3 5.8 %collective-permute-start.2 = (f32[11,32,512]{2,1,0:T(8,128)}, f32[11,32,512]{2,1,0:T(8,128)S(1)}, u32[]{:S(2)}, u32[]{:S(2)}) collective-permute-start(f32[11,32,512]{2,1,0:T(8,128)} %pad_maximum_fusion.2), channel_id=1, source_target_pairs={{0,16},{16,32},{32,48},{48,64},{64,80},{80,96},{96,112},{1,17},{17... | collective-permute-start | bytes 2162696 | tf_op jit(solution)/shard_map/ppermute | solution.py:24
  18.0 1.0 pad_maximum_fusion.3
  19.0 2.4 %collective-permute-start.3 = (f32[11,32,512]{2,1,0:T(8,128)}, f32[11,32,512]{2,1,0:T(8,128)S(1)}, u32[]{:S(2)}, u32[]{:S(2)}) collective-permute-start(f32[11,32,512]{2,1,0:T(8,128)} %pad_maximum_fusion.3), channel_id=1, source_target_pairs={{16,0},{32,16},{48,32},{64,48},{80,64},{96,80},{112,96},{17,1},{33... | collective-permute-start | bytes 2162696 | tf_op jit(solution)/shard_map/ppermute | solution.py:24
  22.1 1.3 add_select_fusion.1.whole
  24.0 14.2 %collective-permute-done.2.xm_hbm = f32[11,32,512]{2,1,0:T(8,128)S(1)} collective-permute-done((f32[11,32,512]{2,1,0:T(8,128)}, f32[11,32,512]{2,1,0:T(8,128)S(1)}, u32[]{:S(2)}, u32[]{:S(2)}) %collective-permute-start.2) | collective-permute-done | bytes 720928 | tf_op jit(solution)/shard_map/ppermute | solution.py:24
  38.2 16.4 %collective-permute-done.3.xp_hbm = f32[11,32,512]{2,1,0:T(8,128)S(1)} collective-permute-done((f32[11,32,512]{2,1,0:T(8,128)}, f32[11,32,512]{2,1,0:T(8,128)S(1)}, u32[]{:S(2)}, u32[]{:S(2)}) %collective-permute-start.3) | collective-permute-done | bytes 720928 | tf_op jit(solution)/shard_map/ppermute | solution.py:24
  54.8 1.3 collective-permute-start.4
  56.1 3.7 %collective-permute-start.5 = (f32[22,4,512]{2,1,0:T(4,128)S(1)}, f32[22,4,512]{2,1,0:T(4,128)}, u32[]{:S(2)}, u32[]{:S(2)}) collective-permute-start(f32[22,4,512]{2,1,0:T(4,128)S(1)} %pad_maximum_fusion.5), channel_id=1, source_target_pairs={{0,1},{1,2},{2,3},{3,4},{4,5},{5,6},{6,7},{7,8},{8,9},{9,10},{10,1... | collective-permute-start | bytes 540680 | tf_op jit(solution)/shard_map/ppermute | solution.py:24
  61.0 1.3 fusion.1.part
  64.2 28.7 %inner.1 = (f32[32,32,512]{2,1,0:T(8,128)}, f32[32,16,512]{2,1,0:T(8,128)}, f32[12,40,512]{2,1,0:T(8,128)}) custom-call(s32[4]{0:T(128)} %pad_add_fusion.place, f32[32,32,512]{2,1,0:T(8,128)} %u_hbm.3, f32[32,32,512]{2,1,0:T(8,128)} %d_hbm.3, f32[32,32,512]{2,1,0:T(8,128)} %r_hbm.3, f32[3,32,4,512]{3,2,1,0:T(4,128)} %copy-done.1, f32[3,32,4,512]{3,2,1,0:T(4,128)} %copy-done), custom_call_target="tpu_custom_call" | custom-call | flops 83886080 | bytes 12582912 | tf_op jit(solution)/shard_map/inner/pallas_call | solution.py:182
  92.9 14.0 %render.2.rest_0_ = f32[16,32,512]{2,1,0:T(8,128)} custom-call(s32[4,32]{1,0:T(4,128)} %add_select_fusion.1.whole, f32[4,32]{1,0:T(4,128)} %fusion.1.part, f32[8]{0:T(128)} %get-tuple-element.39.cen, f32[8]{0:T(128)} %get-tuple-element.34.lev, f32[3,8]{1,0:T(4,128)} %broadcast_divide_fusion.mix, f32[32,16,512]{2,1,0:T(8,128)} %get-tuple-element.14.ft, ...), custom_call_target="tpu_custom_call" | custom-call | flops 62914560 | bytes 2097152 | tf_op jit(solution)/shard_map/render/pallas_call | solution.py:398
  107.6 15.0 %outer.1 = (f32[32,32,512]{2,1,0:T(8,128)}, f32[32,16,512]{2,1,0:T(8,128)}) custom-call(s32[4]{0:T(128)} %pad_add_fusion.place, f32[32,32,512]{2,1,0:T(8,128)} %u_hbm.3, f32[32,32,512]{2,1,0:T(8,128)} %d_hbm.3, f32[32,32,512]{2,1,0:T(8,128)} %r_hbm.3, f32[3,32,4,512]{3,2,1,0:T(4,128)} %copy-done.1, ...), custom_call_target="tpu_custom_call", output_to_operand_aliasing={{0}: (11, {})} | custom-call | tf_op jit(solution)/shard_map/outer/pallas_call | solution.py:305
  122.6 14.0 %render.3 = f32[16,32,512]{2,1,0:T(8,128)} custom-call(s32[4,32]{1,0:T(4,128)} %add_select_fusion.1.whole, f32[4,32]{1,0:T(4,128)} %fusion.1.part, f32[8]{0:T(128)} %get-tuple-element.39.cen, f32[8]{0:T(128)} %get-tuple-element.34.lev, f32[3,8]{1,0:T(4,128)} %broadcast_divide_fusion.mix, ...), custom_call_target="tpu_custom_call", output_to_operand_aliasing={{}: (7, {})} | custom-call | flops 62914560 | bytes 2097152 | tf_op jit(solution)/shard_map/render/pallas_call | solution.py:398
  136.6 26.8 %all_to_all.5.parts = f32[16,32,512]{2,1,0:T(8,128)} all-to-all(f32[16,32,512]{2,1,0:T(8,128)} %render.3), channel_id=1, replica_groups=mesh['sx'=8,'sy'=16] {'sy'}, dimensions={0} | all-to-all | bytes 2097152 | tf_op jit(solution)/shard_map/all_to_all | solution.py:473
  163.4 2.2 %combine.1 = (f32[4,3,2,512]{3,2,1,0:T(2,128)}, f32[4,2,512]{2,1,0:T(2,128)}) custom-call(f32[16,32,512]{2,1,0:T(8,128)} %all_to_all.5.parts, f32[4,1,512]{2,1,0:T(1,128)} %broadcast_in_dim.14.sign_ref), custom_call_target="tpu_custom_call" | custom-call | tf_op jit(solution)/shard_map/combine/pallas_call | solution.py:434
  (31 shorter events, 5.0 us)
Async XLA Ops:
  4.8 57.6 %collective-permute-start.1 = (f32[3,32,4,512]{3,2,1,0:T(4,128)}, f32[3,32,4,512]{3,2,1,0:T(4,128)S(1)}, u32[]{:S(2)}, u32[]{:S(2)}) collective-permute-start(f32[3,32,4,512]{3,2,1,0:T(4,128)} %pad_maximum_fusion.1), channel_id=1, source_target_pairs={{0,1},{1,2},{2,3},{3,4},{4,5},{5,6},{6,7},{7,8},{8,9},{9,10},{10,1... | collective-permute-start | bytes 2359304 | tf_op jit(solution)/shard_map/ppermute | solution.py:24
  7.7 54.7 %collective-permute-start = (f32[3,32,4,512]{3,2,1,0:T(4,128)}, f32[3,32,4,512]{3,2,1,0:T(4,128)S(1)}, u32[]{:S(2)}, u32[]{:S(2)}) collective-permute-start(f32[3,32,4,512]{3,2,1,0:T(4,128)} %pad_maximum_fusion), channel_id=1, source_target_pairs={{1,0},{2,1},{3,2},{4,3},{5,4},{6,5},{7,6},{8,7},{9,8},{10,9},{11,1... | collective-permute-start | bytes 2359304 | tf_op jit(solution)/shard_map/ppermute | solution.py:24
  10.2 11.3 %copy-start.7 = (f32[8]{0:T(128)S(1)}, f32[8]{0:T(128)}, u32[]{:S(2)}) copy-start(f32[8]{0:T(128)} %param.15) | copy-start | bytes 100
  10.2 11.3 %copy-start.8 = (f32[8]{0:T(128)S(1)}, f32[8]{0:T(128)}, u32[]{:S(2)}) copy-start(f32[8]{0:T(128)} %param.13) | copy-start | bytes 100
  10.2 13.2 %copy-start.6 = (f32[3,8]{1,0:T(4,128)S(1)}, f32[3,8]{1,0:T(4,128)}, u32[]{:S(2)}) copy-start(f32[3,8]{1,0:T(4,128)} %param.14) | copy-start | bytes 292
  10.3 13.7 %copy-start.5 = (s32[4,512]{1,0:T(4,128)S(1)}, s32[4,512]{1,0:T(4,128)}, u32[]{:S(2)}) copy-start(s32[4,512]{1,0:T(4,128)} %param.12) | copy-start | bytes 24580
  12.3 25.9 %collective-permute-start.2 = (f32[11,32,512]{2,1,0:T(8,128)}, f32[11,32,512]{2,1,0:T(8,128)S(1)}, u32[]{:S(2)}, u32[]{:S(2)}) collective-permute-start(f32[11,32,512]{2,1,0:T(8,128)} %pad_maximum_fusion.2), channel_id=1, source_target_pairs={{0,16},{16,32},{32,48},{48,64},{64,80},{80,96},{96,112},{1,17},{17... | collective-permute-start | bytes 2162696 | tf_op jit(solution)/shard_map/ppermute | solution.py:24
  19.0 35.7 %collective-permute-start.3 = (f32[11,32,512]{2,1,0:T(8,128)}, f32[11,32,512]{2,1,0:T(8,128)S(1)}, u32[]{:S(2)}, u32[]{:S(2)}) collective-permute-start(f32[11,32,512]{2,1,0:T(8,128)} %pad_maximum_fusion.3), channel_id=1, source_target_pairs={{16,0},{32,16},{48,32},{64,48},{80,64},{96,80},{112,96},{17,1},{33... | collective-permute-start | bytes 2162696 | tf_op jit(solution)/shard_map/ppermute | solution.py:24
  38.2 54.7 %copy-start.2 = (f32[11,32,512]{2,1,0:T(8,128)}, f32[11,32,512]{2,1,0:T(8,128)S(1)}, u32[]{:S(2)}) copy-start(f32[11,32,512]{2,1,0:T(8,128)S(1)} %collective-permute-done.2.xm_hbm) | copy-start | bytes 2162692
  54.7 38.2 %copy-start.3 = (f32[11,32,512]{2,1,0:T(8,128)}, f32[11,32,512]{2,1,0:T(8,128)S(1)}, u32[]{:S(2)}) copy-start(f32[11,32,512]{2,1,0:T(8,128)S(1)} %collective-permute-done.3.xp_hbm) | copy-start | bytes 2162692
  54.8 52.2 %collective-permute-start.4 = (f32[22,4,512]{2,1,0:T(4,128)S(1)}, f32[22,4,512]{2,1,0:T(4,128)S(1)}, u32[]{:S(2)}, u32[]{:S(2)}) collective-permute-start(f32[22,4,512]{2,1,0:T(4,128)S(1)} %pad_maximum_fusion.4), channel_id=1, source_target_pairs={{1,0},{2,1},{3,2},{4,3},{5,4},{6,5},{7,6},{8,7},{9,8},{10,9},{11,1... | collective-permute-start | bytes 540680 | tf_op jit(solution)/shard_map/ppermute | solution.py:24
  56.1 50.8 %collective-permute-start.5 = (f32[22,4,512]{2,1,0:T(4,128)S(1)}, f32[22,4,512]{2,1,0:T(4,128)}, u32[]{:S(2)}, u32[]{:S(2)}) collective-permute-start(f32[22,4,512]{2,1,0:T(4,128)S(1)} %pad_maximum_fusion.5), channel_id=1, source_target_pairs={{0,1},{1,2},{2,3},{3,4},{4,5},{5,6},{6,7},{7,8},{8,9},{9,10},{10,1... | collective-permute-start | bytes 540680 | tf_op jit(solution)/shard_map/ppermute | solution.py:24
  62.4 0.9 copy-start
  63.3 0.9 copy-start.1
  106.9 0.7 copy-start.4

commit v6 on v5

--- a/solution.py
+++ b/solution.py
@@ -24,12 +24,89 @@
     return lax.ppermute(value, axis, pairs)
 
 
+ANYWHERE = pl.BlockSpec(memory_space=pl.ANY)
+LOCAL = pl.BlockSpec(memory_space=pltpu.VMEM)
+SCALARS = pl.BlockSpec(memory_space=pltpu.SMEM)
+
+
+def rows_kernel(u_hbm, d_hbm, r_hbm, up, down, low, high, sems):
+    cx, cy = u_hbm.shape[0], u_hbm.shape[1]
+    copies = []
+    for which, src in enumerate((u_hbm, d_hbm, r_hbm)):
+        for dst, first in ((low, 0), (high, cy - 8)):
+            copies.append(
+                pltpu.make_async_copy(
+                    src.at[:, first : first + 8], dst.at[which], sems.at[len(copies)]
+                )
+            )
+    for copy in copies:
+        copy.start()
+    for which in range(3):
+        copies[2 * which].wait()
+        copies[2 * which + 1].wait()
+
+        def body(x, carry, which=which):
+            down[which, x] = low[which, x, 0:W, :]
+            up[which, x] = high[which, x, 8 - W : 8, :]
+            return carry
+
+        lax.fori_loop(0, cx, body, 0, unroll=4)
+
+
+def rows_of(u, d, r):
+    cx, _, nz = u.shape
+    message = jax.ShapeDtypeStruct((3, cx, W, nz), F32)
+    return pl.pallas_call(
+        rows_kernel,
+        out_shape=(message, message),
+        in_specs=[ANYWHERE] * 3,
+        out_specs=(LOCAL, LOCAL),
+        scratch_shapes=[
+            pltpu.VMEM((3, cx, 8, nz), F32),
+            pltpu.VMEM((3, cx, 8, nz), F32),
+            pltpu.SemaphoreType.DMA((6,)),
+        ],
+        name="rows",
+    )(u, d, r)
+
+
+def planes_kernel(u_hbm, d_hbm, r_hbm, up, down, sems):
+    cx = u_hbm.shape[0]
+    copies = []
+    for src, first, count in ((u_hbm, 0, W), (d_hbm, W, W), (r_hbm, 2 * W, W - 1)):
+        for dst, start in ((up, cx - count), (down, 0)):
+            copies.append(
+                pltpu.make_async_copy(
+                    src.at[start : start + count],
+                    dst.at[first : first + count],
+                    sems.at[len(copies)],
+                )
+            )
+    for copy in copies:
+        copy.start()
+    for copy in copies:
+        copy.wait()
+
+
+def planes_of(u, d, r):
+    _, cy, nz = u.shape
+    message = jax.ShapeDtypeStruct((3 * W - 1, cy, nz), F32)
+    return pl.pallas_call(
+        planes_kernel,
+        out_shape=(message, message),
+        in_specs=[ANYWHERE] * 3,
+        out_specs=(LOCAL, LOCAL),
+        scratch_shapes=[pltpu.SemaphoreType.DMA((6,))],
+        name="planes",
+    )(u, d, r)
+
+
 def cut(tile, block):
     return (slice(8 * tile, 8 * tile + 8), slice(128 * block, 128 * block + 128))
 
 
 class Plane:
-    def __init__(self, dd, dn, rr, kk, fbuf, place):
+    def __init__(self, dd, dn, rr, kk, fbuf):
         self.dd, self.dn, self.rr, self.kk, self.fbuf = dd, dn, rr, kk, fbuf
         self.tiles, self.blocks = dd.shape[1] // 8, dd.shape[2] // 128
         sub = lax.broadcasted_iota(jnp.int32, (8, 128), 0)
@@ -37,8 +114,9 @@
         self.sub_last, self.sub_first = sub == 7, sub == 0
         self.lane_last, self.lane_first = lane == 127, lane == 0
         self.zero = jnp.zeros((8, 128), F32)
+        sy = lax.axis_index("sy")
         self.inside = jnp.where(
-            sub < W, (place[1] < place[3] - 1).astype(F32), (place[1] > 0).astype(F32)
+            sub < W, (sy < lax.axis_size("sy") - 1).astype(F32), (sy > 0).astype(F32)
         )
 
     def prepare(self, plane):
@@ -118,7 +196,7 @@
 
 
 def inner_kernel(
-    place, u_hbm, d_hbm, r_hbm, yn, yp,
+    u_hbm, d_hbm, r_hbm, yn, yp,
     out_hbm, ft_hbm, rim,
     ua, ub, dd, dn, rr, kk, fbuf, fin, turned, sems, osem,
 ):
@@ -137,7 +215,7 @@
         return carry
 
     lax.fori_loop(0, cx, edge_rows, 0)
-    work = Plane(dd, dn, rr, kk, fbuf, place)
+    work = Plane(dd, dn, rr, kk, fbuf)
     for copy in copies:
         copy.wait()
     lax.fori_loop(0, dd.shape[0], lambda i, c: (work.prepare(i), c)[1], 0, unroll=2)
@@ -171,12 +249,7 @@
     move.wait()
 
 
-ANYWHERE = pl.BlockSpec(memory_space=pl.ANY)
-LOCAL = pl.BlockSpec(memory_space=pltpu.VMEM)
-SCALARS = pl.BlockSpec(memory_space=pltpu.SMEM)
-
-
-def inner(place, u, d, r, yn, yp):
+def inner(u, d, r, yn, yp):
     cx, cy, nz = u.shape
     wide = pltpu.VMEM((cx, cy + 8, nz), F32)
     return pl.pallas_call(
@@ -186,7 +259,7 @@
             jax.ShapeDtypeStruct((cy, cx - 16, nz), F32),
             jax.ShapeDtypeStruct((4 * (STEPS - 1), cy + 8, nz), F32),
         ),
-        in_specs=[SCALARS] + [ANYWHERE] * 3 + [LOCAL] * 2,
+        in_specs=[ANYWHERE] * 3 + [LOCAL] * 2,
         out_specs=(ANYWHERE, ANYWHERE, LOCAL),
         scratch_shapes=[wide] * 6
         + [
@@ -200,14 +273,14 @@
             flops=40 * STEPS * cx * cy * nz, bytes_accessed=24 * cx * cy * nz, transcendentals=0
         ),
         name="inner",
-    )(place, u, d, r, yn, yp)
+    )(u, d, r, yn, yp)
 
 
 SPAN = 2 * W + 1
 
 
 def outer_kernel(
-    place, u_hbm, d_hbm, r_hbm, yn, yp, xm_hbm, xp_hbm, cn, cp, rim, field_hbm,
+    u_hbm, d_hbm, r_hbm, yn, yp, xm_hbm, xp_hbm, cn, cp, rim, field_hbm,
     out_hbm, ft_hbm,
     ua, ub, dd, dn, rr, kk, fbuf, fin, turned, sems, osem,
 ):
@@ -252,9 +325,10 @@
             rows(dd, base + i, cn[at + W + i], cp[at + W + i])
         for i in range(W - 1):
             rows(rr, base + i + 1 - side, cn[at + 2 * W + i], cp[at + 2 * W + i])
-    work = Plane(dd, dn, rr, kk, fbuf, place)
-    first = (place[0] > 0).astype(F32)
-    final = (place[0] < place[2] - 1).astype(F32)
+    work = Plane(dd, dn, rr, kk, fbuf)
+    sx = lax.axis_index("sx")
+    first = (sx > 0).astype(F32)
+    final = (sx < lax.axis_size("sx") - 1).astype(F32)
     for copy in copies:
         copy.wait()
     lax.fori_loop(0, dd.shape[0], lambda i, c: (work.prepare(i), c)[1], 0, unroll=2)
@@ -299,7 +373,7 @@
         copy.wait()
 
 
-def outer(place, u, d, r, yn, yp, xm, xp, cn, cp, rim, field):
+def outer(u, d, r, yn, yp, xm, xp, cn, cp, rim, field):
     cx, cy, nz = u.shape
     wide = pltpu.VMEM((2 * SPAN, cy + 8, nz), F32)
     return pl.pallas_call(
@@ -308,7 +382,7 @@
             jax.ShapeDtypeStruct((cx, cy, nz), F32),
             jax.ShapeDtypeStruct((cy, 16, nz), F32),
         ),
-        in_specs=[SCALARS] + [ANYWHERE] * 3 + [LOCAL] * 2 + [ANYWHERE] * 2 + [LOCAL] * 3 + [ANYWHERE],
+        in_specs=[ANYWHERE] * 3 + [LOCAL] * 2 + [ANYWHERE] * 2 + [LOCAL] * 3 + [ANYWHERE],
         out_specs=(ANYWHERE, ANYWHERE),
         scratch_shapes=[wide] * 6
         + [
@@ -318,12 +392,12 @@
             pltpu.SemaphoreType.DMA((14,)),
             pltpu.SemaphoreType.DMA((3,)),
         ],
-        input_output_aliases={11: 0},
+        input_output_aliases={10: 0},
         name="outer",
-    )(place, u, d, r, yn, yp, xm, xp, cn, cp, rim, field)
-
-
-def render_kernel(whole, part, cen, lev, mix, ft, sign_ref, *rest):
+    )(u, d, r, yn, yp, xm, xp, cn, cp, rim, field)
+
+
+def render_kernel(offs, scene, order, ft, *rest):
     out, moved = rest[-2:]
     view = pl.program_id(1)
     depth, rows, nz = ft.shape
@@ -340,7 +414,9 @@
             back = [pltpu.roll(c, 127, 1) for c in cells] + [zero]
             slope = [jnp.where(lane_last, back[b + 1], back[b]) - cells[b] for b in range(blocks)]
             for v in range(VIEWS):
-                n, f = whole[v, y], part[v, y]
+                q = offs[v, lax.axis_index("sy") * depth + y]
+                n = lax.div(q, 4)
+                f = (q - 4 * n).astype(F32) * 0.25
                 turn = lax.rem(128 - n, 128)
                 keep = lane < 128 - n
                 back = [pltpu.roll(cells[b] + f * slope[b], turn, 1) for b in range(blocks)] + [zero]
@@ -352,7 +428,10 @@
 
     for b in range(blocks):
         at = slice(128 * b, 128 * b + 128)
-        sign = jnp.broadcast_to(sign_ref[0, :, at], (rows, 128))
+        side = jnp.broadcast_to(order[0:1, at], (rows, 128))
+        for v in range(1, VIEWS):
+            side = jnp.where(view == v, jnp.broadcast_to(order[v : v + 1, at], (rows, 128)), side)
+        sign = jnp.where(side == 0, -1.0, 1.0)
         rising = sign < 0.0
         light = jnp.ones((rows, 128), F32)
         sums = [zero] * BUMPS
@@ -360,8 +439,8 @@
             s = moved[view, y, :, at]
             bumps = []
             for i in range(BUMPS):
-                t = s - cen[i]
-                bumps.append(jnp.exp2(lev[i] - t * t))
+                t = s - scene[0, i]
+                bumps.append(jnp.exp2(scene[1, i] - t * t))
             pairs = [bumps[i] + bumps[i + 1] for i in range(0, BUMPS, 2)]
             total = (pairs[0] + pairs[1]) + (pairs[2] + pairs[3])
             after = light * jnp.exp2(total * sign)
@@ -373,27 +452,27 @@
         scale = jnp.where(rising, 1.0, -inverse)
         channels = []
         for c in range(3):
-            value = mix[c, 0] * sums[0]
+            value = scene[2 + c, 0] * sums[0]
             for i in range(1, BUMPS):
-                value = value + mix[c, i] * sums[i]
+                value = value + scene[2 + c, i] * sums[i]
             channels.append(value * scale)
         channels.append(through)
         for d in range(rows // 2):
             out[d, :, at] = jnp.concatenate([c[2 * d : 2 * d + 2] for c in channels], axis=0)
 
 
-def render(whole, part, cen, lev, mix, ft, signs, spread, count, parts=None):
+def render(offs, scene, order, ft, spread, count, parts=None):
     cy, cx, nz = ft.shape
-    operands = [whole, part, cen, lev, mix, ft, signs]
-    in_specs = [SCALARS] * 5 + [
+    operands = [offs, scene, order, ft]
+    in_specs = [SCALARS] * 2 + [
+        pl.BlockSpec((VIEWS, nz), lambda i, v: (0, 0)),
         pl.BlockSpec((cy, 8, nz), lambda i, v: (0, i, 0)),
-        pl.BlockSpec((1, 1, nz), lambda i, v: (v, 0, 0)),
     ]
     aliases = {}
     if parts is not None:
         operands.append(parts)
         in_specs.append(ANYWHERE)
-        aliases = {7: 0}
+        aliases = {4: 0}
     cells = VIEWS * cx * cy * nz
     return pl.pallas_call(
         render_kernel,
@@ -410,11 +489,11 @@
     )(*operands)
 
 
-def combine_kernel(parts, sign_ref, image, trans):
+def combine_kernel(parts, order, image, trans):
     count, _, nz = parts.shape
     sub = lax.broadcasted_iota(jnp.int32, (8, nz), 0)
     for view in range(VIEWS):
-        rising = jnp.broadcast_to(sign_ref[view], (8, nz)) < 0.0
+        rising = jnp.broadcast_to(order[view : view + 1, :], (8, nz)) == 0
         total = jnp.zeros((8, nz), F32)
         ahead = jnp.ones((8, nz), F32)
         for source in range(count):
@@ -429,7 +508,7 @@
         trans[view] = ahead[6:8]
 
 
-def combine(parts, signs):
+def combine(parts, order):
     nz = parts.shape[2]
     return pl.pallas_call(
         combine_kernel,
@@ -438,40 +517,28 @@
             jax.ShapeDtypeStruct((VIEWS, 2, nz), F32),
         ),
         name="combine",
-    )(parts, signs)
+    )(parts, order)
 
 
 def scene_of(u, d, r, offsets, depth_order, centres, colour, opacity):
     cx, cy, _ = u.shape
-    place = jnp.stack(
-        [
-            lax.axis_index("sx"),
-            lax.axis_index("sy"),
-            jnp.int32(lax.axis_size("sx")),
-            jnp.int32(lax.axis_size("sy")),
-        ]
-    ).astype(jnp.int32)
-    up_x = jnp.concatenate([u[cx - W :], d[cx - W :], r[cx - W + 1 :]])
-    down_x = jnp.concatenate([u[:W], d[:W], r[: W - 1]])
+    up_y, down_y = rows_of(u, d, r)
+    yp = shift(up_y, "sy", True)
+    yn = shift(down_y, "sy", False)
+    up_x, down_x = planes_of(u, d, r)
     xm = shift(up_x, "sx", True)
     xp = shift(down_x, "sx", False)
-    up_y = jnp.stack([a[:, cy - W :] for a in (u, d, r)])
-    down_y = jnp.stack([a[:, :W] for a in (u, d, r)])
-    yp = shift(up_y, "sy", True)
-    yn = shift(down_y, "sy", False)
     cp = shift(jnp.concatenate([xm[:, cy - W :], xp[:, cy - W :]]), "sy", True)
     cn = shift(jnp.concatenate([xm[:, :W], xp[:, :W]]), "sy", False)
-    offs = lax.dynamic_slice_in_dim(offsets, lax.axis_index("sy") * cy, cy, 1)
-    signs = jnp.where(depth_order == 0, -1.0, 1.0).astype(F32)[:, None, :]
     level = opacity * LOG2E
-    scene = (offs // 4, (offs % 4).astype(F32) * 0.25, centres * GAIN, jnp.log2(level), colour / level)
-
-    field, turned, rim = inner(place, u, d, r, yn, yp)
-    parts = render(*scene, turned, signs, lambda i: i + 1, cx // 2)
-    field, turned = outer(place, u, d, r, yn, yp, xm, xp, cn, cp, rim, field)
-    parts = render(*scene, turned, signs, lambda i: 3 * i, cx // 2, parts)
+    scene = jnp.concatenate([(centres * GAIN)[None], jnp.log2(level)[None], colour / level])
+
+    field, turned, rim = inner(u, d, r, yn, yp)
+    parts = render(offsets, scene, depth_order, turned, lambda i: i + 1, cx // 2)
+    field, turned = outer(u, d, r, yn, yp, xm, xp, cn, cp, rim, field)
+    parts = render(offsets, scene, depth_order, turned, lambda i: 3 * i, cx // 2, parts)
     parts = lax.all_to_all(parts, "sy", split_axis=0, concat_axis=0, tiled=True)
-    image, trans = combine(parts, signs)
+    image, trans = combine(parts, depth_order)
     return field, image, trans
 
 

time: 166 us -> 157 us (0.946)
  the two profiles are of different devices: /device:TPU:6 before, /device:TPU:0 now
where the time goes in v6:
time: 157 us; the launch traced here: 155 us
  Pallas kernels  79.4 us (51%)
  waiting for transfers between devices  30.7 us (20%)
  blocking collectives  23.3 us (15%)
  starting transfers between devices  16.6 us (11%)
  local copies, waits for them, and re-layouts  2.54 us (2%)
    ppermute x6, waiting for transfers between devices, shift(): return lax.ppermute(value, axis, pairs)  30.7 us
    pallas_call x1, Pallas kernels, inner(): pl.pallas_call(inner_kernel, out_shape=(jax.ShapeDtypeStruct((cx, cy, nz)...  28.7 us
    pallas_call x2, Pallas kernels, render(): pl.pallas_call(render_kernel, out_shape=jax.ShapeDtypeStruct((count, 8 *...  27.8 us
    all_to_all x1, blocking collectives, scene_of(): parts = lax.all_to_all(parts, 'sy', split_axis=0, concat_axis=0, tiled=True)  23.3 us
    ppermute x6, starting transfers between devices, shift(): return lax.ppermute(value, axis, pairs)  16.6 us
    pallas_call x1, Pallas kernels, outer(): pl.pallas_call(outer_kernel, out_shape=(jax.ShapeDtypeStruct((cx, cy, nz)...  15 us
  transfers between devices with their start and end apart: 6, of which 1 were waited for; matrix products, arithmetic and copies ran while one was open for 1% of the time, Pallas kernels for 30%

profile of v6, /device:TPU:0, one launch (start us, length us, event | category | flops | bytes accessed | tf_op | source)
XLA Modules:
  0.0 154.7 jit_solution(12876401261838714733)
XLA Ops:
  0.6 2.5 %planes.1 = (f32[11,32,512]{2,1,0:T(8,128)}, f32[11,32,512]{2,1,0:T(8,128)}) custom-call(f32[32,32,512]{2,1,0:T(8,128)} %u_hbm.7, f32[32,32,512]{2,1,0:T(8,128)} %d_hbm.7, f32[32,32,512]{2,1,0:T(8,128)} %r_hbm.7), custom_call_target="tpu_custom_call" | custom-call | tf_op jit(solution)/shard_map/planes/pallas_call | solution.py:94
  3.1 5.9 %collective-permute-start.2 = (f32[11,32,512]{2,1,0:T(8,128)}, f32[11,32,512]{2,1,0:T(8,128)S(1)}, u32[]{:S(2)}, u32[]{:S(2)}) collective-permute-start(f32[11,32,512]{2,1,0:T(8,128)} %get-tuple-element.16), channel_id=1, source_target_pairs={{0,16},{16,32},{32,48},{48,64},{64,80},{80,96},{96,112},{1,17},{17... | collective-permute-start | bytes 2162696 | tf_op jit(solution)/shard_map/ppermute | solution.py:24
  9.1 0.0 copy-start.6
  9.1 0.0 copy-start.5
  9.1 1.3 collective-permute-start.3
  10.4 3.1 %rows.1 = (f32[3,32,4,512]{3,2,1,0:T(4,128)}, f32[3,32,4,512]{3,2,1,0:T(4,128)}) custom-call(f32[32,32,512]{2,1,0:T(8,128)} %u_hbm.7, f32[32,32,512]{2,1,0:T(8,128)} %d_hbm.7, f32[32,32,512]{2,1,0:T(8,128)} %r_hbm.7), custom_call_target="tpu_custom_call" | custom-call | tf_op jit(solution)/shard_map/rows/pallas_call | solution.py:59
  13.5 1.3 collective-permute-start
  14.8 3.1 %collective-permute-start.1 = (f32[3,32,4,512]{3,2,1,0:T(4,128)}, f32[3,32,4,512]{3,2,1,0:T(4,128)S(1)}, u32[]{:S(2)}, u32[]{:S(2)}) collective-permute-start(f32[3,32,4,512]{3,2,1,0:T(4,128)} %get-tuple-element.15), channel_id=1, source_target_pairs={{0,1},{1,2},{2,3},{3,4},{4,5},{5,6},{6,7},{7,8},{8,9},{9,10},{10,1... | collective-permute-start | bytes 2359304 | tf_op jit(solution)/shard_map/ppermute | solution.py:24
  18.0 30.6 %collective-permute-done.2.xm_hbm = f32[11,32,512]{2,1,0:T(8,128)S(1)} collective-permute-done((f32[11,32,512]{2,1,0:T(8,128)}, f32[11,32,512]{2,1,0:T(8,128)S(1)}, u32[]{:S(2)}, u32[]{:S(2)}) %collective-permute-start.2) | collective-permute-done | bytes 720928 | tf_op jit(solution)/shard_map/ppermute | solution.py:24
  48.6 0.0 collective-permute-done.3.xp_hbm
  48.8 1.3 collective-permute-start.4
  50.1 3.7 %collective-permute-start.5 = (f32[22,4,512]{2,1,0:T(4,128)S(1)}, f32[22,4,512]{2,1,0:T(4,128)}, u32[]{:S(2)}, u32[]{:S(2)}) collective-permute-start(f32[22,4,512]{2,1,0:T(4,128)S(1)} %pad_maximum_fusion.1), channel_id=1, source_target_pairs={{0,1},{1,2},{2,3},{3,4},{4,5},{5,6},{6,7},{7,8},{8,9},{9,10},{10,1... | collective-permute-start | bytes 540680 | tf_op jit(solution)/shard_map/ppermute | solution.py:24
  53.8 0.7 multiply_bitcast_fusion.1
  54.5 0.6 pad_maximum_fusion.2.scene
  55.1 0.9 copy-done
  56.0 0.9 copy-done.1
  56.9 28.7 %inner.1 = (f32[32,32,512]{2,1,0:T(8,128)}, f32[32,16,512]{2,1,0:T(8,128)}, f32[12,40,512]{2,1,0:T(8,128)}) custom-call(f32[32,32,512]{2,1,0:T(8,128)} %u_hbm.7, f32[32,32,512]{2,1,0:T(8,128)} %d_hbm.7, f32[32,32,512]{2,1,0:T(8,128)} %r_hbm.7, f32[3,32,4,512]{3,2,1,0:T(4,128)} %copy-done, f32[3,32,4,512]{3,2,1,0:T(4,128)} %copy-done.1), custom_call_target="tpu_custom_call" | custom-call | flops 83886080 | bytes 12582912 | tf_op jit(solution)/shard_map/inner/pallas_call | solution.py:255
  85.6 13.9 %render.2.rest_0_ = f32[16,32,512]{2,1,0:T(8,128)} custom-call(s32[4,512]{1,0:T(4,128)} %offs.3, f32[5,8]{1,0:T(8,128)} %pad_maximum_fusion.2.scene, s32[4,512]{1,0:T(4,128)} %order.5, f32[32,16,512]{2,1,0:T(8,128)} %get-tuple-element.22.ft), custom_call_target="tpu_custom_call" | custom-call | flops 62914560 | bytes 2097152 | tf_op jit(solution)/shard_map/render/pallas_call | solution.py:477
  99.5 0.0 collective-permute-done.4.cn
  99.5 0.7 copy-done.4
  100.2 15.0 %outer.1 = (f32[32,32,512]{2,1,0:T(8,128)}, f32[32,16,512]{2,1,0:T(8,128)}) custom-call(f32[32,32,512]{2,1,0:T(8,128)} %u_hbm.7, f32[32,32,512]{2,1,0:T(8,128)} %d_hbm.7, f32[32,32,512]{2,1,0:T(8,128)} %r_hbm.7, f32[3,32,4,512]{3,2,1,0:T(4,128)} %copy-done, f32[3,32,4,512]{3,2,1,0:T(4,128)} %copy-done.1, ...), custom_call_target="tpu_custom_call", output_to_operand_aliasing={{0}: (10, {})} | custom-call | tf_op jit(solution)/shard_map/outer/pallas_call | solution.py:379
  115.2 13.9 %render.3 = f32[16,32,512]{2,1,0:T(8,128)} custom-call(s32[4,512]{1,0:T(4,128)} %offs.3, f32[5,8]{1,0:T(8,128)} %pad_maximum_fusion.2.scene, s32[4,512]{1,0:T(4,128)} %order.5, f32[32,16,512]{2,1,0:T(8,128)} %get-tuple-element.21.ft, f32[16,32,512]{2,1,0:T(8,128)} %render.2.rest_0_), custom_call_target="tpu_custom_call", output_to_operand_aliasing={{}: (4, {})} | custom-call | flops 62914560 | bytes 2097152 | tf_op jit(solution)/shard_map/render/pallas_call | solution.py:477
  129.1 23.3 %all_to_all.5.parts = f32[16,32,512]{2,1,0:T(8,128)} all-to-all(f32[16,32,512]{2,1,0:T(8,128)} %render.3), channel_id=1, replica_groups=mesh['sx'=8,'sy'=16] {'sy'}, dimensions={0} | all-to-all | bytes 2097152 | tf_op jit(solution)/shard_map/all_to_all | solution.py:540
  152.5 2.2 %combine.1 = (f32[4,3,2,512]{3,2,1,0:T(2,128)}, f32[4,2,512]{2,1,0:T(2,128)}) custom-call(f32[16,32,512]{2,1,0:T(8,128)} %all_to_all.5.parts, s32[4,512]{1,0:T(4,128)} %order.5), custom_call_target="tpu_custom_call" | custom-call | tf_op jit(solution)/shard_map/combine/pallas_call | solution.py:513
  (18 shorter events, 0.2 us)
Async XLA Ops:
  3.1 45.5 %collective-permute-start.2 = (f32[11,32,512]{2,1,0:T(8,128)}, f32[11,32,512]{2,1,0:T(8,128)S(1)}, u32[]{:S(2)}, u32[]{:S(2)}) collective-permute-start(f32[11,32,512]{2,1,0:T(8,128)} %get-tuple-element.16), channel_id=1, source_target_pairs={{0,16},{16,32},{32,48},{48,64},{64,80},{80,96},{96,112},{1,17},{17... | collective-permute-start | bytes 2162696 | tf_op jit(solution)/shard_map/ppermute | solution.py:24
  9.1 8.8 %copy-start.6 = (f32[8]{0:T(128)S(1)}, f32[8]{0:T(128)}, u32[]{:S(2)}) copy-start(f32[8]{0:T(128)} %param.15) | copy-start | bytes 100
  9.1 8.8 %copy-start.5 = (f32[3,8]{1,0:T(4,128)S(1)}, f32[3,8]{1,0:T(4,128)}, u32[]{:S(2)}) copy-start(f32[3,8]{1,0:T(4,128)} %param.14) | copy-start | bytes 292
  9.1 39.5 %collective-permute-start.3 = (f32[11,32,512]{2,1,0:T(8,128)}, f32[11,32,512]{2,1,0:T(8,128)S(1)}, u32[]{:S(2)}, u32[]{:S(2)}) collective-permute-start(f32[11,32,512]{2,1,0:T(8,128)} %get-tuple-element.17), channel_id=1, source_target_pairs={{16,0},{32,16},{48,32},{64,48},{80,64},{96,80},{112,96},{17,1},{33... | collective-permute-start | bytes 2162696 | tf_op jit(solution)/shard_map/ppermute | solution.py:24
  13.5 41.6 %collective-permute-start = (f32[3,32,4,512]{3,2,1,0:T(4,128)}, f32[3,32,4,512]{3,2,1,0:T(4,128)S(1)}, u32[]{:S(2)}, u32[]{:S(2)}) collective-permute-start(f32[3,32,4,512]{3,2,1,0:T(4,128)} %get-tuple-element.14), channel_id=1, source_target_pairs={{1,0},{2,1},{3,2},{4,3},{5,4},{6,5},{7,6},{8,7},{9,8},{10,9},{11,1... | collective-permute-start | bytes 2359304 | tf_op jit(solution)/shard_map/ppermute | solution.py:24
  14.8 40.3 %collective-permute-start.1 = (f32[3,32,4,512]{3,2,1,0:T(4,128)}, f32[3,32,4,512]{3,2,1,0:T(4,128)S(1)}, u32[]{:S(2)}, u32[]{:S(2)}) collective-permute-start(f32[3,32,4,512]{3,2,1,0:T(4,128)} %get-tuple-element.15), channel_id=1, source_target_pairs={{0,1},{1,2},{2,3},{3,4},{4,5},{5,6},{6,7},{7,8},{8,9},{9,10},{10,1... | collective-permute-start | bytes 2359304 | tf_op jit(solution)/shard_map/ppermute | solution.py:24
  48.6 37.0 %copy-start.2 = (f32[11,32,512]{2,1,0:T(8,128)}, f32[11,32,512]{2,1,0:T(8,128)S(1)}, u32[]{:S(2)}) copy-start(f32[11,32,512]{2,1,0:T(8,128)S(1)} %collective-permute-done.2.xm_hbm) | copy-start | bytes 2162692
  48.7 36.9 %copy-start.3 = (f32[11,32,512]{2,1,0:T(8,128)}, f32[11,32,512]{2,1,0:T(8,128)S(1)}, u32[]{:S(2)}) copy-start(f32[11,32,512]{2,1,0:T(8,128)S(1)} %collective-permute-done.3.xp_hbm) | copy-start | bytes 2162692
  48.8 50.8 %collective-permute-start.4 = (f32[22,4,512]{2,1,0:T(4,128)S(1)}, f32[22,4,512]{2,1,0:T(4,128)S(1)}, u32[]{:S(2)}, u32[]{:S(2)}) collective-permute-start(f32[22,4,512]{2,1,0:T(4,128)S(1)} %pad_maximum_fusion), channel_id=1, source_target_pairs={{1,0},{2,1},{3,2},{4,3},{5,4},{6,5},{7,6},{8,7},{9,8},{10,9},{11,1... | collective-permute-start | bytes 540680 | tf_op jit(solution)/shard_map/ppermute | solution.py:24
  50.1 49.4 %collective-permute-start.5 = (f32[22,4,512]{2,1,0:T(4,128)S(1)}, f32[22,4,512]{2,1,0:T(4,128)}, u32[]{:S(2)}, u32[]{:S(2)}) collective-permute-start(f32[22,4,512]{2,1,0:T(4,128)S(1)} %pad_maximum_fusion.1), channel_id=1, source_target_pairs={{0,1},{1,2},{2,3},{3,4},{4,5},{5,6},{6,7},{7,8},{8,9},{9,10},{10,1... | collective-permute-start | bytes 540680 | tf_op jit(solution)/shard_map/ppermute | solution.py:24
  55.1 0.9 copy-start
  56.0 0.9 copy-start.1
  99.5 0.7 copy-start.4

commit v7 on v6

--- a/solution.py
+++ b/solution.py
@@ -280,9 +280,9 @@
 
 
 def outer_kernel(
-    u_hbm, d_hbm, r_hbm, yn, yp, xm_hbm, xp_hbm, cn, cp, rim, field_hbm,
-    out_hbm, ft_hbm,
-    ua, ub, dd, dn, rr, kk, fbuf, fin, turned, sems, osem,
+    u_hbm, d_hbm, r_hbm, yn, yp, xm_hbm, xp_hbm, cn, cp, rim, offs, scene, order, field_hbm, parts_hbm,
+    out_hbm, all_hbm,
+    ua, ub, dd, dn, rr, kk, fbuf, fin, turned, moved, parts, sems, osem,
 ):
     cx, cy, nz = u_hbm.shape
     own = slice(0, cy)
@@ -367,66 +367,87 @@
     for copy in done:
         copy.start()
     turn_over(fin, turned)
-    done.append(pltpu.make_async_copy(turned, ft_hbm, osem.at[2]))
-    done[2].start()
+    for group in range(2):
+        shear_rows(offs, turned, moved, group)
+
+        def one(view, carry, group=group):
+            def store(d, at, value):
+                parts[4 * group + d, pl.ds(pl.multiple_of(8 * view, 8), 8), at] = value
+
+            march(scene, order, moved, view, store)
+            return carry
+
+        lax.fori_loop(0, VIEWS, one, 0)
+        first = group * (cx // 2 - 4)
+        done.append(
+            pltpu.make_async_copy(
+                parts.at[4 * group : 4 * group + 4],
+                all_hbm.at[first : first + 4],
+                osem.at[2 + group],
+            )
+        )
+        done[-1].start()
     for copy in done:
         copy.wait()
 
 
-def outer(u, d, r, yn, yp, xm, xp, cn, cp, rim, field):
+def outer(u, d, r, yn, yp, xm, xp, cn, cp, rim, offs, scene, order, field, parts):
     cx, cy, nz = u.shape
     wide = pltpu.VMEM((2 * SPAN, cy + 8, nz), F32)
     return pl.pallas_call(
         outer_kernel,
         out_shape=(
             jax.ShapeDtypeStruct((cx, cy, nz), F32),
-            jax.ShapeDtypeStruct((cy, 16, nz), F32),
+            jax.ShapeDtypeStruct(parts.shape, F32),
         ),
-        in_specs=[ANYWHERE] * 3 + [LOCAL] * 2 + [ANYWHERE] * 2 + [LOCAL] * 3 + [ANYWHERE],
+        in_specs=[ANYWHERE] * 3 + [LOCAL] * 2 + [ANYWHERE] * 2 + [LOCAL] * 3 + [SCALARS] * 2 + [LOCAL] + [ANYWHERE] * 2,
         out_specs=(ANYWHERE, ANYWHERE),
         scratch_shapes=[wide] * 6
         + [
             pltpu.VMEM((cy + 8, nz), F32),
             pltpu.VMEM((16, cy, nz), F32),
             pltpu.VMEM((cy, 16, nz), F32),
+            pltpu.VMEM((VIEWS, cy, 8, nz), F32),
+            pltpu.VMEM((8, 8 * VIEWS, nz), F32),
             pltpu.SemaphoreType.DMA((14,)),
-            pltpu.SemaphoreType.DMA((3,)),
+            pltpu.SemaphoreType.DMA((4,)),
         ],
-        input_output_aliases={10: 0},
+        input_output_aliases={13: 0, 14: 1},
         name="outer",
-    )(u, d, r, yn, yp, xm, xp, cn, cp, rim, field)
-
-
-def render_kernel(offs, scene, order, ft, *rest):
-    out, moved = rest[-2:]
-    view = pl.program_id(1)
-    depth, rows, nz = ft.shape
+    )(u, d, r, yn, yp, xm, xp, cn, cp, rim, offs, scene, order, field, parts)
+
+
+def shear_rows(offs, ft, moved, group):
+    depth, nz = ft.shape[0], ft.shape[2]
     blocks = nz // 128
+    lane = lax.broadcasted_iota(jnp.int32, (8, 128), 1)
+    lane_last = lane == 127
+    zero = jnp.zeros((8, 128), F32)
+    rows = slice(0, 8) if group is None else pl.ds(pl.multiple_of(8 * group, 8), 8)
+    first = lax.axis_index("sy") * depth
+
+    def shear(y, carry):
+        cells = [ft[y, rows, 128 * b : 128 * b + 128] for b in range(blocks)]
+        back = [pltpu.roll(c, 127, 1) for c in cells] + [zero]
+        slope = [jnp.where(lane_last, back[b + 1], back[b]) - cells[b] for b in range(blocks)]
+        for v in range(VIEWS):
+            q = offs[v, first + y]
+            n = lax.div(q, 4)
+            f = (q - 4 * n).astype(F32) * 0.25
+            turn = lax.rem(128 - n, 128)
+            keep = lane < 128 - n
+            back = [pltpu.roll(cells[b] + f * slope[b], turn, 1) for b in range(blocks)] + [zero]
+            for b in range(blocks):
+                moved[v, y, :, 128 * b : 128 * b + 128] = jnp.where(keep, back[b], back[b + 1])
+        return carry
+
+    lax.fori_loop(0, depth, shear, 0, unroll=8)
+
+
+def march(scene, order, moved, view, store):
+    depth, rows, nz = moved.shape[1], moved.shape[2], moved.shape[3]
     zero = jnp.zeros((rows, 128), F32)
-
-    @pl.when(view == 0)
-    def _():
-        lane = lax.broadcasted_iota(jnp.int32, (rows, 128), 1)
-        lane_last = lane == 127
-
-        def shear(y, carry):
-            cells = [ft[y, :, 128 * b : 128 * b + 128] for b in range(blocks)]
-            back = [pltpu.roll(c, 127, 1) for c in cells] + [zero]
-            slope = [jnp.where(lane_last, back[b + 1], back[b]) - cells[b] for b in range(blocks)]
-            for v in range(VIEWS):
-                q = offs[v, lax.axis_index("sy") * depth + y]
-                n = lax.div(q, 4)
-                f = (q - 4 * n).astype(F32) * 0.25
-                turn = lax.rem(128 - n, 128)
-                keep = lane < 128 - n
-                back = [pltpu.roll(cells[b] + f * slope[b], turn, 1) for b in range(blocks)] + [zero]
-                for b in range(blocks):
-                    moved[v, y, :, 128 * b : 128 * b + 128] = jnp.where(keep, back[b], back[b + 1])
-            return carry
-
-        lax.fori_loop(0, depth, shear, 0, unroll=8)
-
-    for b in range(blocks):
+    for b in range(nz // 128):
         at = slice(128 * b, 128 * b + 128)
         side = jnp.broadcast_to(order[0:1, at], (rows, 128))
         for v in range(1, VIEWS):
@@ -458,35 +479,41 @@
             channels.append(value * scale)
         channels.append(through)
         for d in range(rows // 2):
-            out[d, :, at] = jnp.concatenate([c[2 * d : 2 * d + 2] for c in channels], axis=0)
-
-
-def render(offs, scene, order, ft, spread, count, parts=None):
+            store(d, at, jnp.concatenate([c[2 * d : 2 * d + 2] for c in channels], axis=0))
+
+
+def render_kernel(offs, scene, order, ft, out, moved):
+    view = pl.program_id(1)
+
+    @pl.when(view == 0)
+    def _():
+        shear_rows(offs, ft, moved, None)
+
+    def store(d, at, value):
+        out[d, :, at] = value
+
+    march(scene, order, moved, view, store)
+
+
+def render(offs, scene, order, ft, spread, count):
     cy, cx, nz = ft.shape
-    operands = [offs, scene, order, ft]
-    in_specs = [SCALARS] * 2 + [
-        pl.BlockSpec((VIEWS, nz), lambda i, v: (0, 0)),
-        pl.BlockSpec((cy, 8, nz), lambda i, v: (0, i, 0)),
-    ]
-    aliases = {}
-    if parts is not None:
-        operands.append(parts)
-        in_specs.append(ANYWHERE)
-        aliases = {4: 0}
     cells = VIEWS * cx * cy * nz
     return pl.pallas_call(
         render_kernel,
         out_shape=jax.ShapeDtypeStruct((count, 8 * VIEWS, nz), F32),
         grid=(cx // 8, VIEWS),
-        in_specs=in_specs,
+        in_specs=[SCALARS] * 2
+        + [
+            pl.BlockSpec((VIEWS, nz), lambda i, v: (0, 0)),
+            pl.BlockSpec((cy, 8, nz), lambda i, v: (0, i, 0)),
+        ],
         out_specs=pl.BlockSpec((4, 8, nz), lambda i, v: (spread(i), v, 0)),
         scratch_shapes=[pltpu.VMEM((VIEWS, cy, 8, nz), F32)],
-        input_output_aliases=aliases,
         cost_estimate=pl.CostEstimate(
             flops=60 * cells, bytes_accessed=4 * (cx * cy + count * 8 * VIEWS) * nz, transcendentals=9 * cells
         ),
         name="render",
-    )(*operands)
+    )(offs, scene, order, ft)
 
 
 def combine_kernel(parts, order, image, trans):
@@ -535,8 +562,9 @@
 
     field, turned, rim = inner(u, d, r, yn, yp)
     parts = render(offsets, scene, depth_order, turned, lambda i: i + 1, cx // 2)
-    field, turned = outer(u, d, r, yn, yp, xm, xp, cn, cp, rim, field)
-    parts = render(offsets, scene, depth_order, turned, lambda i: 3 * i, cx // 2, parts)
+    field, parts = outer(
+        u, d, r, yn, yp, xm, xp, cn, cp, rim, offsets, scene, depth_order, field, parts
+    )
     parts = lax.all_to_all(parts, "sy", split_axis=0, concat_axis=0, tiled=True)
     image, trans = combine(parts, depth_order)
     return field, image, trans

time: 157 us -> 155 us (0.987)
  Pallas kernels: 79.4 us -> 77.1 us
    pallas_call x2 -> x1, Pallas kernels: 27.8 us -> 13.9 us  [render(): pl.pallas_call(render_kernel, out_shape=jax.ShapeDtypeStruct((count, 8 *...]
    pallas_call x1, Pallas kernels: 15 us -> 26.6 us  [outer(): pl.pallas_call(outer_kernel, out_shape=(jax.ShapeDtypeStruct((cx, cy, nz)...]
where the time goes in v7:
time: 155 us; the launch traced here: 152 us
  Pallas kernels  77.1 us (50%)
  waiting for transfers between devices  30.7 us (20%)
  blocking collectives  23.4 us (15%)
  starting transfers between devices  16.6 us (11%)
  local copies, waits for them, and re-layouts  2.55 us (2%)
    ppermute x6, waiting for transfers between devices, shift(): return lax.ppermute(value, axis, pairs)  30.7 us
    pallas_call x1, Pallas kernels, inner(): pl.pallas_call(inner_kernel, out_shape=(jax.ShapeDtypeStruct((cx, cy, nz)...  28.7 us
    pallas_call x1, Pallas kernels, outer(): pl.pallas_call(outer_kernel, out_shape=(jax.ShapeDtypeStruct((cx, cy, nz)...  26.6 us
    all_to_all x1, blocking collectives, scene_of(): parts = lax.all_to_all(parts, 'sy', split_axis=0, concat_axis=0, tiled=True)  23.4 us
    ppermute x6, starting transfers between devices, shift(): return lax.ppermute(value, axis, pairs)  16.6 us
    pallas_call x1, Pallas kernels, render(): pl.pallas_call(render_kernel, out_shape=jax.ShapeDtypeStruct((count, 8 *...  13.9 us
    pallas_call x1, Pallas kernels, rows_of(): pl.pallas_call(rows_kernel, out_shape=(message, message), in_specs=[ANYWH...  3.11 us
  transfers between devices with their start and end apart: 6, of which 1 were waited for; matrix products, arithmetic and copies ran while one was open for 1% of the time, Pallas kernels for 30%

profile of v7, /device:TPU:0, one launch (start us, length us, event | category | flops | bytes accessed | tf_op | source)
XLA Modules:
  0.0 152.4 jit_solution(8225768722328143618)
XLA Ops:
  0.6 2.5 %planes.1 = (f32[11,32,512]{2,1,0:T(8,128)}, f32[11,32,512]{2,1,0:T(8,128)}) custom-call(f32[32,32,512]{2,1,0:T(8,128)} %u_hbm.7, f32[32,32,512]{2,1,0:T(8,128)} %d_hbm.7, f32[32,32,512]{2,1,0:T(8,128)} %r_hbm.7), custom_call_target="tpu_custom_call" | custom-call | tf_op jit(solution)/shard_map/planes/pallas_call | solution.py:94
  3.1 5.9 %collective-permute-start.2 = (f32[11,32,512]{2,1,0:T(8,128)}, f32[11,32,512]{2,1,0:T(8,128)S(1)}, u32[]{:S(2)}, u32[]{:S(2)}) collective-permute-start(f32[11,32,512]{2,1,0:T(8,128)} %get-tuple-element.16), channel_id=1, source_target_pairs={{0,16},{16,32},{32,48},{48,64},{64,80},{80,96},{96,112},{1,17},{17... | collective-permute-start | bytes 2162696 | tf_op jit(solution)/shard_map/ppermute | solution.py:24
  9.1 0.0 copy-start.6
  9.1 0.0 copy-start.5
  9.1 1.3 collective-permute-start.3
  10.4 3.1 %rows.1 = (f32[3,32,4,512]{3,2,1,0:T(4,128)}, f32[3,32,4,512]{3,2,1,0:T(4,128)}) custom-call(f32[32,32,512]{2,1,0:T(8,128)} %u_hbm.7, f32[32,32,512]{2,1,0:T(8,128)} %d_hbm.7, f32[32,32,512]{2,1,0:T(8,128)} %r_hbm.7), custom_call_target="tpu_custom_call" | custom-call | tf_op jit(solution)/shard_map/rows/pallas_call | solution.py:59
  13.5 1.3 collective-permute-start
  14.8 3.1 %collective-permute-start.1 = (f32[3,32,4,512]{3,2,1,0:T(4,128)}, f32[3,32,4,512]{3,2,1,0:T(4,128)S(1)}, u32[]{:S(2)}, u32[]{:S(2)}) collective-permute-start(f32[3,32,4,512]{3,2,1,0:T(4,128)} %get-tuple-element.15), channel_id=1, source_target_pairs={{0,1},{1,2},{2,3},{3,4},{4,5},{5,6},{6,7},{7,8},{8,9},{9,10},{10,1... | collective-permute-start | bytes 2359304 | tf_op jit(solution)/shard_map/ppermute | solution.py:24
  18.0 30.6 %collective-permute-done.2.xm_hbm = f32[11,32,512]{2,1,0:T(8,128)S(1)} collective-permute-done((f32[11,32,512]{2,1,0:T(8,128)}, f32[11,32,512]{2,1,0:T(8,128)S(1)}, u32[]{:S(2)}, u32[]{:S(2)}) %collective-permute-start.2) | collective-permute-done | bytes 720928 | tf_op jit(solution)/shard_map/ppermute | solution.py:24
  48.6 0.0 collective-permute-done.3.xp_hbm
  48.8 1.3 collective-permute-start.4
  50.1 3.7 %collective-permute-start.5 = (f32[22,4,512]{2,1,0:T(4,128)S(1)}, f32[22,4,512]{2,1,0:T(4,128)}, u32[]{:S(2)}, u32[]{:S(2)}) collective-permute-start(f32[22,4,512]{2,1,0:T(4,128)S(1)} %pad_maximum_fusion.1), channel_id=1, source_target_pairs={{0,1},{1,2},{2,3},{3,4},{4,5},{5,6},{6,7},{7,8},{8,9},{9,10},{10,1... | collective-permute-start | bytes 540680 | tf_op jit(solution)/shard_map/ppermute | solution.py:24
  53.8 0.7 multiply_bitcast_fusion.1
  54.5 0.6 pad_maximum_fusion.2.scene
  55.1 0.0 collective-permute-done.yn
  55.1 0.0 collective-permute-done.1.yp
  55.1 0.9 copy-done
  56.0 0.9 copy-done.1
  56.9 28.7 %inner.1 = (f32[32,32,512]{2,1,0:T(8,128)}, f32[32,16,512]{2,1,0:T(8,128)}, f32[12,40,512]{2,1,0:T(8,128)}) custom-call(f32[32,32,512]{2,1,0:T(8,128)} %u_hbm.7, f32[32,32,512]{2,1,0:T(8,128)} %d_hbm.7, f32[32,32,512]{2,1,0:T(8,128)} %r_hbm.7, f32[3,32,4,512]{3,2,1,0:T(4,128)} %copy-done, f32[3,32,4,512]{3,2,1,0:T(4,128)} %copy-done.1), custom_call_target="tpu_custom_call" | custom-call | flops 83886080 | bytes 12582912 | tf_op jit(solution)/shard_map/inner/pallas_call | solution.py:255
  85.6 13.9 %render.1.parts_hbm = f32[16,32,512]{2,1,0:T(8,128)} custom-call(s32[4,512]{1,0:T(4,128)} %offs.3, f32[5,8]{1,0:T(8,128)} %pad_maximum_fusion.2.scene, s32[4,512]{1,0:T(4,128)} %order.5, f32[32,16,512]{2,1,0:T(8,128)} %get-tuple-element.20.ft), custom_call_target="tpu_custom_call" | custom-call | flops 62914560 | bytes 2097152 | tf_op jit(solution)/shard_map/render/pallas_call | solution.py:501
  99.5 0.7 copy-done.4
  100.2 26.6 %outer.1 = (f32[32,32,512]{2,1,0:T(8,128)}, f32[16,32,512]{2,1,0:T(8,128)}) custom-call(f32[32,32,512]{2,1,0:T(8,128)} %u_hbm.7, f32[32,32,512]{2,1,0:T(8,128)} %d_hbm.7, f32[32,32,512]{2,1,0:T(8,128)} %r_hbm.7, f32[3,32,4,512]{3,2,1,0:T(4,128)} %copy-done, f32[3,32,4,512]{3,2,1,0:T(4,128)} %copy-done.1, ...), custom_call_target="tpu_custom_call", output_to_operand_aliasing={{0}: (13, {}), {1}: (14, {})} | custom-call | tf_op jit(solution)/shard_map/outer/pallas_call | solution.py:397
  126.8 23.4 %all_to_all.5.parts = f32[16,32,512]{2,1,0:T(8,128)} all-to-all(f32[16,32,512]{2,1,0:T(8,128)} %get-tuple-element.22), channel_id=1, replica_groups=mesh['sx'=8,'sy'=16] {'sy'}, dimensions={0} | all-to-all | bytes 2097152 | tf_op jit(solution)/shard_map/all_to_all | solution.py:568
  150.2 2.2 %combine.1 = (f32[4,3,2,512]{3,2,1,0:T(2,128)}, f32[4,2,512]{2,1,0:T(2,128)}) custom-call(f32[16,32,512]{2,1,0:T(8,128)} %all_to_all.5.parts, s32[4,512]{1,0:T(4,128)} %order.5), custom_call_target="tpu_custom_call" | custom-call | tf_op jit(solution)/shard_map/combine/pallas_call | solution.py:540
  (17 shorter events, 0.2 us)
Async XLA Ops:
  3.1 45.5 %collective-permute-start.2 = (f32[11,32,512]{2,1,0:T(8,128)}, f32[11,32,512]{2,1,0:T(8,128)S(1)}, u32[]{:S(2)}, u32[]{:S(2)}) collective-permute-start(f32[11,32,512]{2,1,0:T(8,128)} %get-tuple-element.16), channel_id=1, source_target_pairs={{0,16},{16,32},{32,48},{48,64},{64,80},{80,96},{96,112},{1,17},{17... | collective-permute-start | bytes 2162696 | tf_op jit(solution)/shard_map/ppermute | solution.py:24
  9.1 8.8 %copy-start.6 = (f32[8]{0:T(128)S(1)}, f32[8]{0:T(128)}, u32[]{:S(2)}) copy-start(f32[8]{0:T(128)} %param.15) | copy-start | bytes 100
  9.1 8.8 %copy-start.5 = (f32[3,8]{1,0:T(4,128)S(1)}, f32[3,8]{1,0:T(4,128)}, u32[]{:S(2)}) copy-start(f32[3,8]{1,0:T(4,128)} %param.14) | copy-start | bytes 292
  9.1 39.5 %collective-permute-start.3 = (f32[11,32,512]{2,1,0:T(8,128)}, f32[11,32,512]{2,1,0:T(8,128)S(1)}, u32[]{:S(2)}, u32[]{:S(2)}) collective-permute-start(f32[11,32,512]{2,1,0:T(8,128)} %get-tuple-element.17), channel_id=1, source_target_pairs={{16,0},{32,16},{48,32},{64,48},{80,64},{96,80},{112,96},{17,1},{33... | collective-permute-start | bytes 2162696 | tf_op jit(solution)/shard_map/ppermute | solution.py:24
  13.5 41.6 %collective-permute-start = (f32[3,32,4,512]{3,2,1,0:T(4,128)}, f32[3,32,4,512]{3,2,1,0:T(4,128)S(1)}, u32[]{:S(2)}, u32[]{:S(2)}) collective-permute-start(f32[3,32,4,512]{3,2,1,0:T(4,128)} %get-tuple-element.14), channel_id=1, source_target_pairs={{1,0},{2,1},{3,2},{4,3},{5,4},{6,5},{7,6},{8,7},{9,8},{10,9},{11,1... | collective-permute-start | bytes 2359304 | tf_op jit(solution)/shard_map/ppermute | solution.py:24
  14.8 40.3 %collective-permute-start.1 = (f32[3,32,4,512]{3,2,1,0:T(4,128)}, f32[3,32,4,512]{3,2,1,0:T(4,128)S(1)}, u32[]{:S(2)}, u32[]{:S(2)}) collective-permute-start(f32[3,32,4,512]{3,2,1,0:T(4,128)} %get-tuple-element.15), channel_id=1, source_target_pairs={{0,1},{1,2},{2,3},{3,4},{4,5},{5,6},{6,7},{7,8},{8,9},{9,10},{10,1... | collective-permute-start | bytes 2359304 | tf_op jit(solution)/shard_map/ppermute | solution.py:24
  48.6 37.0 %copy-start.2 = (f32[11,32,512]{2,1,0:T(8,128)}, f32[11,32,512]{2,1,0:T(8,128)S(1)}, u32[]{:S(2)}) copy-start(f32[11,32,512]{2,1,0:T(8,128)S(1)} %collective-permute-done.2.xm_hbm) | copy-start | bytes 2162692
  48.7 36.9 %copy-start.3 = (f32[11,32,512]{2,1,0:T(8,128)}, f32[11,32,512]{2,1,0:T(8,128)S(1)}, u32[]{:S(2)}) copy-start(f32[11,32,512]{2,1,0:T(8,128)S(1)} %collective-permute-done.3.xp_hbm) | copy-start | bytes 2162692
  48.8 50.8 %collective-permute-start.4 = (f32[22,4,512]{2,1,0:T(4,128)S(1)}, f32[22,4,512]{2,1,0:T(4,128)S(1)}, u32[]{:S(2)}, u32[]{:S(2)}) collective-permute-start(f32[22,4,512]{2,1,0:T(4,128)S(1)} %pad_maximum_fusion), channel_id=1, source_target_pairs={{1,0},{2,1},{3,2},{4,3},{5,4},{6,5},{7,6},{8,7},{9,8},{10,9},{11,1... | collective-permute-start | bytes 540680 | tf_op jit(solution)/shard_map/ppermute | solution.py:24
  50.1 49.4 %collective-permute-start.5 = (f32[22,4,512]{2,1,0:T(4,128)S(1)}, f32[22,4,512]{2,1,0:T(4,128)}, u32[]{:S(2)}, u32[]{:S(2)}) collective-permute-start(f32[22,4,512]{2,1,0:T(4,128)S(1)} %pad_maximum_fusion.1), channel_id=1, source_target_pairs={{0,1},{1,2},{2,3},{3,4},{4,5},{5,6},{6,7},{7,8},{8,9},{9,10},{10,1... | collective-permute-start | bytes 540680 | tf_op jit(solution)/shard_map/ppermute | solution.py:24
  55.1 0.9 copy-start
  56.0 0.9 copy-start.1
  99.5 0.7 copy-start.4
